TPU v7x, 256 devices: a whole 4x4x8 slice. The times are simulated.
256 devices in a mesh: slot: 8 (over y_lo, x), feat: 32 (over y_hi, z, core).
Axes of the slice: x: 4, y: 4 (y_hi: 2, y_lo: 2; y = y_hi * 2 + y_lo), z: 8, core: 2. Of those that a mesh axis runs over, the one named last changes fastest.
Arguments:
- acts_in: bfloat16 [3, 256, 2304], P(None, None, 'slot'), may hold values from -6 to 6
- acts_out: bfloat16 [3, 256, 2304], P(None, None, 'slot'), may hold values from -6 to 6
- enc_weight: bfloat16 [3, 2304, 16384], P(None, 'slot', 'feat'), may hold values from -0.125 to 0.125
- enc_bias: float32 [3, 16384], P(None, 'feat'), may hold values from -3 to 3
- dec_weight: bfloat16 [6, 16384, 2304], P(None, 'feat', 'slot'), may hold values from -0.046875 to 0.046875
- dec_bias: float32 [3, 2304], P(None, 'slot'), may hold values from -3 to 3
Outputs:
- enc_grad: float32 [3, 2304, 16384], P(None, 'slot', 'feat')
- enc_bias_grad: float32 [3, 16384], P(None, 'feat')
- dec_grad: float32 [6, 16384, 2304], P(None, 'feat', 'slot')
- mse: float32 [], replicated
All inputs are finite; a program needn't handle non-finite values.
Results may differ from a plain program's by a relative error of at most 0.0095.
Values may be sent and summed in bfloat16 or wider, within the bound.
No kernel may reach another device: no remote copies, remote signals or barrier semaphores. Data moves between devices by JAX's collectives and lax.ppermute only.
A program may use at most 64 MiB of HBM per device.

v0:
```python
import functools

import jax
import jax.numpy as jnp
from jax import lax
from jax.sharding import Mesh
from jax.sharding import PartitionSpec as P

D = 2304
SLOT = ("slot_0", "slot_1")
FEAT = ("feat_0", "feat_1", "feat_2")
SLOT_FEAT = ("slot_0", "slot_1", "feat_0", "feat_1", "feat_2")


def cut_along(x, dim, devices):
    before, after = (x.shape[:dim], x.shape[dim + 1 :])
    return jnp.moveaxis(x.reshape(*before, devices, -1, *after), dim, 0)


def sum_at_owner(x, axis, dim):
    tiles = cut_along(x, dim, lax.axis_size(axis))
    arrived = lax.all_to_all(tiles, axis, split_axis=0, concat_axis=0, tiled=True)
    return arrived.sum(axis=0)


def over_axes(x, axes):
    return functools.reduce(lax.psum, axes, x)


def sent_to_all(x, axis):
    devices = lax.axis_size(axis)
    return lax.all_to_all(jnp.broadcast_to(x[None], (devices, *x.shape)), axis, 0, 0, tiled=True)


def joined_along(tiles, dim):
    dims = list(tiles.shape[1:])
    dims[dim] *= tiles.shape[0]
    return jnp.moveaxis(tiles, 0, dim).reshape(dims)


def collect(x, axis, dim):
    tiles = sent_to_all(x, axis)
    return joined_along(tiles, dim)


def activate(preact):
    return (
        jnp.maximum(preact, 0.0).astype(jnp.bfloat16),
        jnp.where(preact > 0, 1.0, 0.0).astype(jnp.bfloat16),
    )


def local(acts_in, acts_out, enc_weight, enc_bias, dec_weight, dec_bias):
    layers = acts_in.shape[0]
    tokens = acts_in.shape[1]
    width_dev = acts_in.shape[2]
    feature_dev = enc_weight.shape[2]
    pair_list = [(a, b) for a in range(layers) for b in range(a, layers)]

    def encode_rows():
        pieces = [
            jnp.dot(acts_in[a], enc_weight[a], preferred_element_type=jnp.float32)
            for a in range(layers)
        ]
        return jnp.concatenate(pieces, axis=1)

    bias_row = enc_bias.reshape(1, layers * feature_dev)
    preact = lax.psum(encode_rows(), SLOT) + bias_row
    features, slopes = activate(preact)
    target = (
        jnp.transpose(acts_out, (1, 0, 2)).reshape(tokens, layers * width_dev).astype(jnp.float32)
    )
    dec_row = dec_bias.reshape(1, layers * width_dev)
    portion = tokens // lax.axis_size(FEAT)
    row_block = features
    pieces = []
    for decode_b in range(layers):
        summed = jnp.zeros((portion * lax.axis_size(FEAT), width_dev), jnp.float32)
        for decode_a in range(decode_b + 1):
            pair_num = pair_list.index((decode_a, decode_b))
            summed = summed + jnp.dot(
                row_block[:, decode_a * feature_dev : (decode_a + 1) * feature_dev],
                dec_weight[pair_num],
                preferred_element_type=jnp.float32,
            )
        pieces.append(summed)
    rebuilt = sum_at_owner(jnp.concatenate(pieces, axis=1), FEAT, 0)
    offset = lax.axis_index(FEAT) * portion
    error_full = rebuilt + dec_row - lax.dynamic_slice_in_dim(target, offset, portion, 0)
    squared = over_axes(jnp.sum(error_full * error_full), SLOT_FEAT)
    error_half = collect(error_full.astype(jnp.bfloat16), FEAT, 0)
    mse = squared / (layers * tokens * D)
    dec_grads = []
    for a, b in pair_list:
        dec_grads.append(
            lax.dot_general(
                features[:, a * feature_dev : (a + 1) * feature_dev],
                error_half[:, b * width_dev : (b + 1) * width_dev],
                (((0,), (0,)), ((), ())),
                preferred_element_type=jnp.float32,
            )
        )
    row_block = error_half
    partials = []
    for upstream_a in range(layers):
        summed = jnp.zeros((tokens, feature_dev), jnp.float32)
        for b in range(upstream_a, layers):
            pair_num = pair_list.index((upstream_a, b))
            summed = summed + lax.dot_general(
                row_block[:, b * width_dev : (b + 1) * width_dev],
                dec_weight[pair_num],
                (((1,), (1,)), ((), ())),
                preferred_element_type=jnp.float32,
            )
        partials.append(summed)
    upstream = lax.psum(jnp.concatenate(partials, axis=1), SLOT)
    delta = upstream * slopes.astype(jnp.float32)
    bias_grad = jnp.sum(delta, axis=0).reshape(layers, feature_dev)
    delta_half = delta.astype(jnp.bfloat16)
    enc_grads = []
    for a in range(layers):
        enc_grads.append(
            lax.dot_general(
                acts_in[a],
                delta_half[:, a * feature_dev : (a + 1) * feature_dev],
                (((0,), (0,)), ((), ())),
                preferred_element_type=jnp.float32,
            )
        )
    return (jnp.stack(enc_grads), bias_grad, jnp.stack(dec_grads), mse)


def solution(mesh):
    split = Mesh(
        mesh.devices.reshape(2, 4, 2, 8, 2), ("slot_0", "slot_1", "feat_0", "feat_1", "feat_2")
    )
    in_specs = (
        P(None, None, SLOT),
        P(None, None, SLOT),
        P(None, SLOT, FEAT),
        P(None, FEAT),
        P(None, FEAT, SLOT),
        P(None, SLOT),
    )
    out_specs = (P(None, SLOT, FEAT), P(None, FEAT), P(None, FEAT, SLOT), P())
    return jax.shard_map(local, mesh=split, in_specs=in_specs, out_specs=out_specs, check_vma=False)
```

profile of v0, /device:TPU:32, one launch (start us, length us, event | category | flops | bytes accessed | tf_op | source)
XLA Modules:
  0.0 258.0 jit_solution(12020248933589295281)
XLA Ops:
  7.2 0.0 all-reduce.3.cloned.1.call-start
  7.2 1.4 fusion.26
  8.6 1.4 fusion.28
  9.9 1.4 fusion.30
  11.3 0.0 copy-start.3
  11.3 1.3 pad_maximum_fusion.1
  12.6 0.0 copy-start
  12.6 0.0 all-reduce.3.cloned.1.call-update
  12.6 0.0 copy-done.3
  12.6 87.5 %all-reduce.3.cloned.1.call-done = f32[256,1536]{1,0:T(8,128)} async-done(((f32[256,1536]{1,0:T(8,128)}), f32[256,1536]{1,0:T(8,128)}) %all-reduce.3.cloned.1.call-update) | async-done | bytes 1572880 | tf_op jit(solution)/shard_map/psum | solution.py:68
  100.1 1.6 maximum_convert_fusion
  101.7 0.0 copy-done
  101.7 0.3 fusion.14
  101.9 0.3 fusion.20
  102.2 0.3 fusion.24
  102.5 0.3 convolution_add_fusion.4
  102.8 0.3 convolution_add_fusion.3
  103.0 0.3 convolution_add_fusion.5
  103.3 0.1 pad_maximum_fusion.3
  103.4 1.2 copy.15
  104.6 9.8 %all-to-all-start = ((f32[32,8,864]{2,1,0:T(8,128)}), f32[32,8,864]{2,1,0:T(8,128)S(1)}, u32[]{:S(2)}, u32[]{:S(2)}) async-start(f32[32,8,864]{2,1,0:T(8,128)} %bitcast.107), calls=%async_computation | async-start | bytes 1835008 | tf_op jit(solution)/shard_map/all_to_all | solution.py:22
  114.4 0.0 copy-start.4
  114.4 0.0 all-reduce.5.cloned.1.call-start
  114.5 2.0 convert_element_type.33
  116.5 2.0 constant_dynamic-slice_fusion
  118.5 1.2 copy.17
  119.6 0.0 copy-done.4
  119.6 0.1 add.67
  119.7 22.4 %all-to-all-done = f32[32,8,864]{2,1,0:T(8,128)S(1)} async-done(((f32[32,8,864]{2,1,0:T(8,128)}), f32[32,8,864]{2,1,0:T(8,128)S(1)}, u32[]{:S(2)}, u32[]{:S(2)}) %all-to-all-start) | async-done | bytes 884768 | tf_op jit(solution)/shard_map/all_to_all | solution.py:22
  142.1 0.1 reduce_sum.27
  142.2 0.6 multiply_reduce_fusion
  142.8 21.1 %all_to_all.10 = bf16[32,8,864]{2,1,0:T(8,128)(2,1)S(1)} all-to-all(bf16[32,8,864]{2,1,0:T(8,128)(2,1)S(1)} %broadcast_in_dim.12), channel_id=1, replica_groups=mesh['slot_0'=2,'slot_1'=4,'feat_0'=2,'feat_1'=8,'feat_2'=2] {'feat_0','..., dimensions={0} | all-to-all | bytes 884736 | tf_op jit(solution)/shard_map/all_to_all | solution.py:32
  163.9 0.3 fusion.22
  164.2 0.3 fusion.16
  164.6 0.3 fusion.8
  164.9 0.3 convolution_add_fusion.2
  165.3 0.3 convolution_add_fusion.1
  165.6 0.3 convolution_add_fusion
  166.0 1.3 pad_maximum_fusion.2
  167.2 0.0 all-reduce.5.cloned.1.call-update
  167.3 5.6 %psum.51 = f32[]{:T(128)} all-reduce(f32[]{:T(128)} %get-tuple-element.6), channel_id=1, replica_groups=mesh['slot_0'=2,'slot_1'=4,'feat_0'=2,'feat_1'=8,'feat_2'=2] {'slot_0'}, use_global_device_ids=true, to_apply=%region_5.6 | all-reduce | flops 1 | bytes 8 | tf_op jit(solution)/shard_map/psum | solution.py:27
  172.8 9.6 %psum.52 = f32[]{:T(128)} all-reduce(f32[]{:T(128)} %psum.51), channel_id=1, replica_groups=mesh['slot_0'=2,'slot_1'=4,'feat_0'=2,'feat_1'=8,'feat_2'=2] {'slot_1'}, use_global_device_ids=true, to_apply=%region_6.7 | all-reduce | flops 1 | bytes 8 | tf_op jit(solution)/shard_map/psum | solution.py:27
  182.5 7.1 %psum.53 = f32[]{:T(128)} all-reduce(f32[]{:T(128)} %psum.52), channel_id=1, replica_groups=mesh['slot_0'=2,'slot_1'=4,'feat_0'=2,'feat_1'=8,'feat_2'=2] {'feat_0'}, use_global_device_ids=true, to_apply=%region_7.8 | all-reduce | flops 1 | bytes 8 | tf_op jit(solution)/shard_map/psum | solution.py:27
  189.5 15.8 %psum.54 = f32[]{:T(128)} all-reduce(f32[]{:T(128)} %psum.53), channel_id=1, replica_groups=mesh['slot_0'=2,'slot_1'=4,'feat_0'=2,'feat_1'=8,'feat_2'=2] {'feat_1'}, use_global_device_ids=true, to_apply=%region_8.9 | all-reduce | flops 1 | bytes 8 | tf_op jit(solution)/shard_map/psum | solution.py:27
  205.3 3.1 %psum.55 = f32[]{:T(128)} all-reduce(f32[]{:T(128)} %psum.54), channel_id=1, replica_groups=mesh['slot_0'=2,'slot_1'=4,'feat_0'=2,'feat_1'=8,'feat_2'=2] {'feat_2'}, use_global_device_ids=true, to_apply=%region_9.10 | all-reduce | flops 1 | bytes 8 | tf_op jit(solution)/shard_map/psum | solution.py:27
  209.0 1.1 fusion.5
  210.1 1.2 fusion.4
  211.3 1.2 fusion.3
  212.6 0.0 copy-start.1
  212.6 1.2 fusion.2
  213.8 1.2 fusion.1
  215.0 1.2 fusion
  216.2 0.0 copy-start.2
  216.2 29.3 %all-reduce.5.cloned.1.call-done = f32[256,1536]{1,0:T(8,128)} async-done(((f32[256,1536]{1,0:T(8,128)}), f32[256,1536]{1,0:T(8,128)}) %all-reduce.5.cloned.1.call-update) | async-done | bytes 1572880 | tf_op jit(solution)/shard_map/psum | solution.py:116
  245.5 0.0 copy-done.1
  245.5 1.8 fusion.6
  247.3 0.0 copy-done.2
  247.3 0.2 convolution_bitcast_fusion
  247.5 0.2 convolution_bitcast_fusion.1
  247.8 0.2 convolution_bitcast_fusion.2
  248.0 0.6 reshape.27
  248.6 1.3 pad_maximum_fusion
  (2 shorter events, 0.0 us)
Async XLA Ops:
  7.2 92.9 %all-reduce.3.cloned.1.call-start = ((), (), s32[]{:S(2)}) async-start(), calls=%async_computation.2 | async-start | bytes 3145728 | tf_op jit(solution)/shard_map/psum | solution.py:68
  11.3 1.3 copy-start.3
  12.6 89.1 %copy-start = (bf16[6,512,288]{1,2,0:T(8,128)(2,1)S(1)}, bf16[6,512,288]{1,2,0:T(8,128)(2,1)}, u32[]{:S(2)}) copy-start(bf16[6,512,288]{1,2,0:T(8,128)(2,1)} %param.10) | copy-start | bytes 5308420
  104.6 37.5 %all-to-all-start = ((f32[32,8,864]{2,1,0:T(8,128)}), f32[32,8,864]{2,1,0:T(8,128)S(1)}, u32[]{:S(2)}, u32[]{:S(2)}) async-start(f32[32,8,864]{2,1,0:T(8,128)} %bitcast.107), calls=%async_computation | async-start | bytes 1835008 | tf_op jit(solution)/shard_map/all_to_all | solution.py:22
  114.4 5.2 %copy-start.4 = (f32[3,288]{1,0:T(4,128)S(1)}, f32[3,288]{1,0:T(4,128)}, u32[]{:S(2)}) copy-start(f32[3,288]{1,0:T(4,128)} %param.11) | copy-start | bytes 10372
  114.4 131.1 %all-reduce.5.cloned.1.call-start = ((), (), s32[]{:S(2)}) async-start(), calls=%async_computation.3 | async-start | bytes 3145728 | tf_op jit(solution)/shard_map/psum | solution.py:116
  212.6 33.0 %copy-start.1 = (f32[256,1536]{1,0:T(8,128)S(1)}, f32[256,1536]{1,0:T(8,128)}, u32[]{:S(2)}) copy-start(f32[256,1536]{1,0:T(8,128)} %all-reduce.3.cloned.1.call-done) | copy-start | bytes 4718596
  216.2 31.1 %copy-start.2 = (bf16[3,256,288]{1,2,0:T(8,128)(2,1)S(1)}, bf16[3,256,288]{1,2,0:T(8,128)(2,1)}, u32[]{:S(2)}) copy-start(bf16[3,256,288]{1,2,0:T(8,128)(2,1)} %param.6) | copy-start | bytes 1327108
Sparse Core Ops, SparseCore 0:
  12.7 87.3 all-reduce.2
  167.4 78.1 all-reduce.4
where the time goes:
time: 259 us; the launch traced here: 258 us
  waiting for transfers between devices  139 us (54%)
  blocking collectives  62.2 us (24%)
  between operations  16 us (6%)
  matrix products  15.5 us (6%)
  other arithmetic  9.89 us (4%)
  starting transfers between devices  9.88 us (4%)
  local copies, waits for them, and re-layouts  5.13 us (2%)
    psum x1, waiting for transfers between devices, local(): preact = lax.psum(encode_rows(), SLOT) + bias_row  87.5 us
    psum x5, blocking collectives, over_axes(): return functools.reduce(lax.psum, axes, x)  41.1 us
    psum x1, waiting for transfers between devices, local(): upstream = lax.psum(jnp.concatenate(partials, axis=1), SLOT)  29.3 us
    all_to_all x1, waiting for transfers between devices, sum_at_owner(): lax.all_to_all(tiles, axis, split_axis=0, concat_axis=0, tiled=True)  22.4 us
    all_to_all x1, blocking collectives, sent_to_all(): lax.all_to_all(jnp.broadcast_to(x[None], (devices, *x.shape)), axis, 0, 0...  21.1 us
    all_to_all x1, starting transfers between devices, sum_at_owner(): lax.all_to_all(tiles, axis, split_axis=0, concat_axis=0, tiled=True)  9.8 us
    dot_general x6, matrix products, local(): lax.dot_general(features[:, a * feature_dev:(a + 1) * feature_dev], error...  7.18 us
  transfers between devices with their start and end apart: 3, of which 3 were waited for; matrix products, arithmetic and copies ran while one was open for 5% of the time, Pallas kernels for 0%

commit v1 on v0

v1 whole, which is shorter than its diff:
```python
import jax
import jax.numpy as jnp
from jax import lax
from jax.sharding import Mesh
from jax.sharding import PartitionSpec as P

D = 2304
SLOT = ("slot_0", "slot_1")
FEAT = ("feat_0", "feat_1", "feat_2")
CHIPS = ("feat_0", "feat_1")
CORE = "feat_2"


def exchange(tiles, axis):
    return lax.all_to_all(tiles, axis, split_axis=0, concat_axis=0, tiled=True)


def sent_to_all(x, axis):
    return exchange(jnp.broadcast_to(x[None], (lax.axis_size(axis), *x.shape)), axis)


def local(acts_in, acts_out, enc_weight, enc_bias, dec_weight, dec_bias):
    layers, tokens, width_dev = acts_in.shape
    feature_dev = enc_weight.shape[2]
    pair_list = [(a, b) for a in range(layers) for b in range(a, layers)]
    slots = lax.axis_size(SLOT)
    chips = lax.axis_size(CHIPS)
    core = lax.axis_index(CORE)
    f32, bf16 = jnp.float32, jnp.bfloat16

    def feats(x, a):
        return x[:, a * feature_dev : (a + 1) * feature_dev]

    def width(x, b):
        return x[:, b * width_dev : (b + 1) * width_dev]

    preact = jnp.concatenate(
        [jnp.dot(acts_in[a], enc_weight[a], preferred_element_type=f32) for a in range(layers)], axis=1
    )
    arrived = exchange(preact.reshape(slots, tokens // slots, -1), SLOT)
    own_preact = arrived.sum(axis=0) + enc_bias.reshape(1, -1)
    own_features = jnp.maximum(own_preact, 0.0).astype(bf16)
    features = sent_to_all(own_features, SLOT).reshape(tokens, -1)

    pieces = []
    for b in range(layers):
        summed = jnp.zeros((tokens, width_dev), f32)
        for a in range(b + 1):
            summed = summed + jnp.dot(
                feats(features, a), dec_weight[pair_list.index((a, b))], preferred_element_type=f32
            )
        pieces.append(summed)
    partial = jnp.concatenate(pieces, axis=1)
    half = tokens // 2
    theirs = lax.dynamic_slice_in_dim(partial, (1 - core) * half, half, 0).astype(bf16)
    mine = lax.dynamic_slice_in_dim(partial, core * half, half, 0)
    chip_sum = (mine + lax.ppermute(theirs, CORE, [(0, 1), (1, 0)]).astype(f32)).astype(bf16)
    portion = half // chips
    rebuilt = exchange(chip_sum.reshape(chips, portion, -1), CHIPS).astype(f32).sum(axis=0)
    offset = core * half + lax.axis_index(CHIPS) * portion
    target = lax.dynamic_slice_in_dim(acts_out, offset, portion, 1)
    target = jnp.transpose(target, (1, 0, 2)).reshape(portion, -1).astype(f32)
    own_error = (rebuilt + dec_bias.reshape(1, -1) - target).astype(bf16)
    half_error = sent_to_all(own_error, CHIPS).reshape(half, -1)
    error = lax.all_gather(half_error, CORE, axis=0, tiled=True)

    wide = error.astype(f32)
    squared = jnp.sum(wide * wide)
    coarse = lax.reduce_precision(squared, 8, 7)
    fine = lax.reduce_precision(squared - coarse, 8, 7)
    lane = lax.broadcasted_iota(jnp.int32, (tokens, 128), 1)
    extra = jnp.where(lane == 0, coarse, jnp.where(lane == 1, fine, 0.0))

    partials = []
    for a in range(layers):
        summed = jnp.zeros((tokens, feature_dev), f32)
        for b in range(a, layers):
            summed = summed + lax.dot_general(
                width(error, b),
                dec_weight[pair_list.index((a, b))],
                (((1,), (1,)), ((), ())),
                preferred_element_type=f32,
            )
        partials.append(summed)
    sent = jnp.concatenate([*partials, extra], axis=1).astype(bf16)
    total = exchange(sent.reshape(slots, tokens // slots, -1), SLOT).astype(f32).sum(axis=0)
    mse = (total[0, layers * feature_dev] + total[0, layers * feature_dev + 1]) / (layers * tokens * D)
    own_delta = jnp.where(own_features > 0, total[:, : layers * feature_dev], 0.0).astype(bf16)
    delta = sent_to_all(own_delta, SLOT).reshape(tokens, -1)

    dec_grads = [
        lax.dot_general(
            feats(features, a), width(error, b), (((0,), (0,)), ((), ())), preferred_element_type=f32
        )
        for a, b in pair_list
    ]
    bias_grad = jnp.sum(delta.astype(f32), axis=0).reshape(layers, feature_dev)
    enc_grads = [
        lax.dot_general(
            acts_in[a], feats(delta, a), (((0,), (0,)), ((), ())), preferred_element_type=f32
        )
        for a in range(layers)
    ]
    return (jnp.stack(enc_grads), bias_grad, jnp.stack(dec_grads), mse)


def solution(mesh):
    split = Mesh(mesh.devices.reshape(2, 4, 2, 8, 2), (*SLOT, *FEAT))
    in_specs = (
        P(None, None, SLOT),
        P(None, None, SLOT),
        P(None, SLOT, FEAT),
        P(None, FEAT),
        P(None, FEAT, SLOT),
        P(None, SLOT),
    )
    out_specs = (P(None, SLOT, FEAT), P(None, FEAT), P(None, FEAT, SLOT), P())
    return jax.shard_map(local, mesh=split, in_specs=in_specs, out_specs=out_specs, check_vma=False)
```

time: 259 us -> 150 us (0.58)
  waiting for transfers between devices: 139 us -> 75.1 us
  blocking collectives: 62.2 us -> 2.12 us
  starting transfers between devices: 9.88 us -> 31.5 us
  between operations: 16 us -> 6.32 us
    psum x2 -> x0, waiting for transfers between devices: 117 us -> none  [the longest x1 87.5 us: local(): preact = lax.psum(encode_rows(), SLOT) + bias_row]
    all_to_all x1 -> x6, waiting for transfers between devices: 22.4 us -> 73.3 us  [exchange(): return lax.all_to_all(tiles, axis, split_axis=0, concat_axis=0, tiled=True)]
    psum x5 -> x0, blocking collectives: 41.1 us -> none  [over_axes(): return functools.reduce(lax.psum, axes, x)]
    all_to_all x1 -> x6, starting transfers between devices: 9.8 us -> 31.5 us  [exchange(): return lax.all_to_all(tiles, axis, split_axis=0, concat_axis=0, tiled=True)]
    all_to_all x1 -> x0, blocking collectives: 21.1 us -> none  [sent_to_all(): lax.all_to_all(jnp.broadcast_to(x[None], (devices, *x.shape)), axis, 0, 0...]
    convert_element_type x0 -> x3, local copies, waits for them, and re-layouts: none -> 2.63 us  [the longest x1 1.76 us: local(): (mine + lax.ppermute(theirs, CORE, [(0, 1), (1, 0)]).astype(f32)).astype(...]
  transfers between devices with their start and end apart: 3 -> 7, of which waited for: 3 -> 7; matrix products, arithmetic and copies ran while one was open for 5% -> 6% of each run, Pallas kernels for 0% -> 0%
where the time goes in v1:
time: 150 us; the launch traced here: 149 us
  waiting for transfers between devices  75.1 us (50%)
  starting transfers between devices  31.5 us (21%)
  matrix products  17.1 us (11%)
  other arithmetic  9.93 us (7%)
  local copies, waits for them, and re-layouts  6.66 us (4%)
  between operations  6.32 us (4%)
  blocking collectives  2.12 us (1%)
    all_to_all x6, waiting for transfers between devices, exchange(): return lax.all_to_all(tiles, axis, split_axis=0, concat_axis=0, tiled=True)  73.3 us
    all_to_all x6, starting transfers between devices, exchange(): return lax.all_to_all(tiles, axis, split_axis=0, concat_axis=0, tiled=True)  31.5 us
    dot_general x6, matrix products, local(): lax.dot_general(feats(features, a), width(error, b), (((0,), (0,)), ((),...  7.18 us
    dot_general x3, matrix products, local(): jnp.dot(acts_in[a], enc_weight[a], preferred_element_type=f32)  4.07 us
  transfers between devices with their start and end apart: 7, of which 7 were waited for; matrix products, arithmetic and copies ran while one was open for 6% of the time, Pallas kernels for 0%

profile of v1, /device:TPU:32, one launch (start us, length us, event | category | flops | bytes accessed | tf_op | source)
XLA Modules:
  0.0 148.7 jit_solution(9378091980327522966)
XLA Ops:
  0.6 1.4 fusion.25
  2.0 1.4 fusion.27
  3.4 1.4 fusion.29
  4.7 1.3 pad_maximum_fusion.1
  6.0 5.4 %all-to-all-start = ((f32[8,32,1536]{2,1,0:T(8,128)}), f32[8,32,1536]{2,1,0:T(8,128)S(1)}, u32[]{:S(2)}, u32[]{:S(2)}) async-start(f32[8,32,1536]{2,1,0:T(8,128)} %bitcast.6), calls=%async_computation | async-start | bytes 3145728 | tf_op jit(solution)/shard_map/all_to_all | solution.py:15
  11.4 21.3 %all-to-all-done = f32[8,32,1536]{2,1,0:T(8,128)S(1)} async-done(((f32[8,32,1536]{2,1,0:T(8,128)}), f32[8,32,1536]{2,1,0:T(8,128)S(1)}, u32[]{:S(2)}, u32[]{:S(2)}) %all-to-all-start) | async-done | bytes 1572896 | tf_op jit(solution)/shard_map/all_to_all | solution.py:15
  32.7 0.1 reduce_sum.45
  32.8 0.0 copy-start
  32.9 0.9 broadcast_in_dim.32
  33.8 3.5 %all-to-all-start.1 = ((bf16[8,32,1536]{2,1,0:T(8,128)(2,1)}), bf16[8,32,1536]{2,1,0:T(8,128)(2,1)S(1)}, u32[]{:S(2)}, u32[]{:S(2)}) async-start(bf16[8,32,1536]{2,1,0:T(8,128)(2,1)} %broadcast_in_dim.32), calls=%async_computation.1 | async-start | bytes 1572864 | tf_op jit(solution)/shard_map/all_to_all | solution.py:15
  37.4 12.9 %all-to-all-done.1 = bf16[8,32,1536]{2,1,0:T(8,128)(2,1)S(1)} async-done(((bf16[8,32,1536]{2,1,0:T(8,128)(2,1)}), bf16[8,32,1536]{2,1,0:T(8,128)(2,1)S(1)}, u32[]{:S(2)}, u32[]{:S(2)}) %all-to-all-start.1) | async-done | bytes 786464 | tf_op jit(solution)/shard_map/all_to_all | solution.py:15
  50.3 0.3 fusion.13
  50.6 0.3 fusion.19
  50.9 0.3 fusion.23
  51.2 0.3 convolution_add_fusion.4
  51.4 0.3 convolution_add_fusion.3
  51.7 0.3 convolution_add_fusion.5
  52.0 0.1 pad_maximum_fusion.2
  52.1 0.0 copy-start.5
  52.1 0.7 dynamic-slice_convert_fusion
  52.8 0.0 collective-permute-start
  52.8 1.8 %collective-permute-done = bf16[128,864]{0,1:T(8,128)(2,1)} collective-permute-done((bf16[128,864]{0,1:T(8,128)(2,1)}, bf16[128,864]{0,1:T(8,128)(2,1)}, u32[]{:S(2)}, u32[]{:S(2)}) %collective-permute-start) | collective-permute-done | bytes 221216 | tf_op jit(solution)/shard_map/ppermute | solution.py:57
  54.6 1.7 %add_convert_fusion = bf16[128,864]{0,1:T(8,128)(2,1)} fusion(bf16[128,864]{0,1:T(8,128)(2,1)} %collective-permute-done, f32[256,864]{0,1:T(8,128)S(1)} %pad_maximum_fusion.2, s32[]{:T(128)S(6)} %select_n.23), kind=kLoop, calls=%fused_computation.32 | loop fusion | flops 331776 | bytes 884740 | tf_op jit(solution)/shard_map/convert_element_type | solution.py:57
  56.3 1.8 %copy.17 = bf16[128,864]{1,0:T(8,128)(2,1)} copy(bf16[128,864]{0,1:T(8,128)(2,1)} %add_convert_fusion) | data formatting | bytes 442368 | tf_op jit(solution)/shard_map/convert_element_type | solution.py:57
  58.0 10.9 %all-to-all-start.2 = ((bf16[16,8,864]{2,1,0:T(8,128)(2,1)}), bf16[16,8,864]{2,1,0:T(8,128)(2,1)S(1)}, u32[]{:S(2)}, u32[]{:S(2)}) async-start(bf16[16,8,864]{2,1,0:T(8,128)(2,1)} %bitcast.14), calls=%async_computation.2 | async-start | bytes 458752 | tf_op jit(solution)/shard_map/all_to_all | solution.py:15
  69.0 1.1 dynamic-slice_convert_fusion.1
  70.0 0.1 copy.19
  70.2 0.1 add.77
  70.2 10.0 %all-to-all-done.2 = bf16[16,8,864]{2,1,0:T(8,128)(2,1)S(1)} async-done(((bf16[16,8,864]{2,1,0:T(8,128)(2,1)}), bf16[16,8,864]{2,1,0:T(8,128)(2,1)S(1)}, u32[]{:S(2)}, u32[]{:S(2)}) %all-to-all-start.2) | async-done | bytes 221216 | tf_op jit(solution)/shard_map/all_to_all | solution.py:15
  80.3 0.7 broadcast_in_dim.33
  81.0 4.5 %all-to-all-start.3 = ((bf16[16,8,864]{2,1,0:T(8,128)(2,1)}), bf16[16,8,864]{2,1,0:T(8,128)(2,1)S(1)}, u32[]{:S(2)}, u32[]{:S(2)}) async-start(bf16[16,8,864]{2,1,0:T(8,128)(2,1)} %broadcast_in_dim.33), calls=%async_computation.3 | async-start | bytes 458752 | tf_op jit(solution)/shard_map/all_to_all | solution.py:15
  85.5 11.0 %all-to-all-done.3 = bf16[16,8,864]{2,1,0:T(8,128)(2,1)S(1)} async-done(((bf16[16,8,864]{2,1,0:T(8,128)(2,1)}), bf16[16,8,864]{2,1,0:T(8,128)(2,1)S(1)}, u32[]{:S(2)}, u32[]{:S(2)}) %all-to-all-start.3) | async-done | bytes 221216 | tf_op jit(solution)/shard_map/all_to_all | solution.py:15
  96.5 2.1 %all_gather.3 = bf16[256,864]{1,0:T(8,128)(2,1)S(1)} all-gather(bf16[128,864]{1,0:T(8,128)(2,1)S(1)} %bitcast.122), channel_id=1, replica_groups=mesh['slot_0'=2,'slot_1'=4,'feat_0'=2,'feat_1'=8,'feat_2'=2] {'feat_2'}, dimensions={0}, use_global_device_ids=true | all-gather | bytes 663552 | tf_op jit(solution)/shard_map/all_gather | solution.py:65
  98.6 0.3 fusion.21
  98.9 0.3 fusion.15
  99.3 0.1 slice.128
  99.4 0.8 multiply_reduce_fusion
  100.2 0.3 convolution_add_fusion.2
  100.6 0.3 fusion.6
  100.9 0.3 fusion.7
  101.3 1.0 convolution_convert_fusion
  105.2 0.6 compare_select_fusion
  105.9 0.7 select_convert_fusion
  106.5 1.9 %pad_maximum_fusion.3 = bf16[8,32,1664]{2,1,0:T(8,128)(2,1)} fusion(bf16[8,32,128]{2,1,0:T(8,128)(2,1)S(1)} %select_convert_fusion, bf16[8,32,512]{2,1,0:T(8,128)(2,1)} %convolution_convert_fusion, bf16[8,32,512]{2,1,0:T(8,128)(2,1)S(1)} %bitcast.121, bf16[8,32,512]{2,1,0:T(8,128)(2,1)S(1)} %bitcast.120), kind=kLoop, calls=%fused_computation.30 | loop fusion | flops 3407872 | bytes 1703936 | tf_op jit(solution)/shard_map/concatenate | solution.py:85
  108.5 3.6 %all-to-all-start.4 = ((bf16[8,32,1664]{2,1,0:T(8,128)(2,1)}), bf16[8,32,1664]{2,1,0:T(8,128)(2,1)S(1)}, u32[]{:S(2)}, u32[]{:S(2)}) async-start(bf16[8,32,1664]{2,1,0:T(8,128)(2,1)} %pad_maximum_fusion.3), calls=%async_computation.4 | async-start | bytes 1703936 | tf_op jit(solution)/shard_map/all_to_all | solution.py:15
  112.0 1.1 fusion.5
  113.1 1.2 fusion.4
  114.3 1.2 fusion.3
  115.6 10.6 %all-to-all-done.4 = bf16[8,32,1664]{2,1,0:T(8,128)(2,1)S(1)} async-done(((bf16[8,32,1664]{2,1,0:T(8,128)(2,1)}), bf16[8,32,1664]{2,1,0:T(8,128)(2,1)S(1)}, u32[]{:S(2)}, u32[]{:S(2)}) %all-to-all-start.4) | async-done | bytes 852000 | tf_op jit(solution)/shard_map/all_to_all | solution.py:15
  126.1 0.1 convert_reduce_fusion
  126.3 0.9 broadcast_in_dim.37
  127.3 3.5 %all-to-all-start.5 = ((bf16[8,32,1536]{2,1,0:T(8,128)(2,1)}), bf16[8,32,1536]{2,1,0:T(8,128)(2,1)S(1)}, u32[]{:S(2)}, u32[]{:S(2)}) async-start(bf16[8,32,1536]{2,1,0:T(8,128)(2,1)} %broadcast_in_dim.37), calls=%async_computation.5 | async-start | bytes 1572864 | tf_op jit(solution)/shard_map/all_to_all | solution.py:15
  130.8 0.0 copy-start.3
  130.8 1.2 fusion.2
  132.1 1.2 fusion.1
  133.3 1.2 fusion
  134.5 0.6 fusion.85
  136.4 7.5 %all-to-all-done.5 = bf16[8,32,1536]{2,1,0:T(8,128)(2,1)S(1)} async-done(((bf16[8,32,1536]{2,1,0:T(8,128)(2,1)}), bf16[8,32,1536]{2,1,0:T(8,128)(2,1)S(1)}, u32[]{:S(2)}, u32[]{:S(2)}) %all-to-all-start.5) | async-done | bytes 786464 | tf_op jit(solution)/shard_map/all_to_all | solution.py:15
  143.8 0.2 convolution_bitcast_fusion
  144.1 0.2 convolution_bitcast_fusion.1
  144.3 1.1 convolution_bitcast_fusion.2
  145.5 0.1 convert_reduce_fusion.1
  145.6 0.6 reshape.107
  146.2 1.4 pad_maximum_fusion
  (15 shorter events, 0.1 us)
Async XLA Ops:
  6.0 5.5 %copy-start.4 = (f32[3,512]{1,0:T(4,128)S(1)}, f32[3,512]{1,0:T(4,128)}, u32[]{:S(2)}) copy-start(f32[3,512]{1,0:T(4,128)} %param.9) | copy-start | bytes 18436
  6.0 26.8 %all-to-all-start = ((f32[8,32,1536]{2,1,0:T(8,128)}), f32[8,32,1536]{2,1,0:T(8,128)S(1)}, u32[]{:S(2)}, u32[]{:S(2)}) async-start(f32[8,32,1536]{2,1,0:T(8,128)} %bitcast.6), calls=%async_computation | async-start | bytes 3145728 | tf_op jit(solution)/shard_map/all_to_all | solution.py:15
  32.8 17.8 %copy-start.1 = (f32[32,1536]{1,0:T(8,128)}, f32[32,1536]{1,0:T(8,128)S(1)}, u32[]{:S(2)}) copy-start(f32[32,1536]{1,0:T(8,128)S(1)} %reduce_sum.45) | copy-start | bytes 589828
  32.8 17.5 %copy-start = (bf16[6,512,288]{1,2,0:T(8,128)(2,1)S(1)}, bf16[6,512,288]{1,2,0:T(8,128)(2,1)}, u32[]{:S(2)}) copy-start(bf16[6,512,288]{1,2,0:T(8,128)(2,1)} %param.10) | copy-start | bytes 5308420
  33.8 16.5 %all-to-all-start.1 = ((bf16[8,32,1536]{2,1,0:T(8,128)(2,1)}), bf16[8,32,1536]{2,1,0:T(8,128)(2,1)S(1)}, u32[]{:S(2)}, u32[]{:S(2)}) async-start(bf16[8,32,1536]{2,1,0:T(8,128)(2,1)} %broadcast_in_dim.32), calls=%async_computation.1 | async-start | bytes 1572864 | tf_op jit(solution)/shard_map/all_to_all | solution.py:15
  52.1 18.1 %copy-start.5 = (f32[3,288]{1,0:T(4,128)S(1)}, f32[3,288]{1,0:T(4,128)}, u32[]{:S(2)}) copy-start(f32[3,288]{1,0:T(4,128)} %param.11) | copy-start | bytes 10372
  52.8 1.8 %collective-permute-start = (bf16[128,864]{0,1:T(8,128)(2,1)}, bf16[128,864]{0,1:T(8,128)(2,1)}, u32[]{:S(2)}, u32[]{:S(2)}) collective-permute-start(bf16[128,864]{0,1:T(8,128)(2,1)} %dynamic-slice_convert_fusion), channel_id=1, source_target_pairs={{0,1},{1,0},{2,3},{3,2},{4,5},{5,4},{6,7},{7,6},{8,9},{9,8},{10,11... | collective-permute-start | bytes 663560 | tf_op jit(solution)/shard_map/ppermute | solution.py:57
  58.0 22.2 %all-to-all-start.2 = ((bf16[16,8,864]{2,1,0:T(8,128)(2,1)}), bf16[16,8,864]{2,1,0:T(8,128)(2,1)S(1)}, u32[]{:S(2)}, u32[]{:S(2)}) async-start(bf16[16,8,864]{2,1,0:T(8,128)(2,1)} %bitcast.14), calls=%async_computation.2 | async-start | bytes 458752 | tf_op jit(solution)/shard_map/all_to_all | solution.py:15
  81.0 15.5 %all-to-all-start.3 = ((bf16[16,8,864]{2,1,0:T(8,128)(2,1)}), bf16[16,8,864]{2,1,0:T(8,128)(2,1)S(1)}, u32[]{:S(2)}, u32[]{:S(2)}) async-start(bf16[16,8,864]{2,1,0:T(8,128)(2,1)} %broadcast_in_dim.33), calls=%async_computation.3 | async-start | bytes 458752 | tf_op jit(solution)/shard_map/all_to_all | solution.py:15
  108.5 17.7 %all-to-all-start.4 = ((bf16[8,32,1664]{2,1,0:T(8,128)(2,1)}), bf16[8,32,1664]{2,1,0:T(8,128)(2,1)S(1)}, u32[]{:S(2)}, u32[]{:S(2)}) async-start(bf16[8,32,1664]{2,1,0:T(8,128)(2,1)} %pad_maximum_fusion.3), calls=%async_computation.4 | async-start | bytes 1703936 | tf_op jit(solution)/shard_map/all_to_all | solution.py:15
  113.1 13.1 %copy-start.2 = (f32[32,1536]{1,0:T(8,128)S(1)}, f32[32,1536]{1,0:T(8,128)}, u32[]{:S(2)}) copy-start(f32[32,1536]{1,0:T(8,128)} %copy-done.1) | copy-start | bytes 589828
  127.3 16.6 %all-to-all-start.5 = ((bf16[8,32,1536]{2,1,0:T(8,128)(2,1)}), bf16[8,32,1536]{2,1,0:T(8,128)(2,1)S(1)}, u32[]{:S(2)}, u32[]{:S(2)}) async-start(bf16[8,32,1536]{2,1,0:T(8,128)(2,1)} %broadcast_in_dim.37), calls=%async_computation.5 | async-start | bytes 1572864 | tf_op jit(solution)/shard_map/all_to_all | solution.py:15
  130.8 13.0 %copy-start.3 = (bf16[3,256,288]{1,2,0:T(8,128)(2,1)S(1)}, bf16[3,256,288]{1,2,0:T(8,128)(2,1)}, u32[]{:S(2)}) copy-start(bf16[3,256,288]{1,2,0:T(8,128)(2,1)} %param.6) | copy-start | bytes 1327108

commit v2 on v1

v2 whole, which is shorter than its diff:
```python
import functools

import jax
import jax.numpy as jnp
from jax import lax
from jax.experimental import pallas as pl
from jax.experimental.pallas import tpu as pltpu
from jax.sharding import Mesh
from jax.sharding import PartitionSpec as P

D = 2304
SLOT = ("slot_0", "slot_1")
FEAT = ("feat_0", "feat_1", "feat_2")
CHIPS = ("feat_0", "feat_1")
CORE = "feat_2"
LANES = 128
VMEM = 16 * 2**20
F32 = jnp.float32
BF16 = jnp.bfloat16


def exchange(tiles, axis):
    return lax.all_to_all(tiles, axis, split_axis=0, concat_axis=0, tiled=True)


def sent_to_all(x, axis):
    return exchange(jnp.broadcast_to(x[None], (lax.axis_size(axis), *x.shape)), axis)


def pair_number(a, b, layers):
    return a * layers - a * (a - 1) // 2 + (b - a)


def contract(x, y, x_dim, y_dim):
    return lax.dot_general(x, y, (((x_dim,), (y_dim,)), ((), ())), preferred_element_type=F32)


def encode_kernel(acts_ref, weight_ref, out_ref):
    out_ref[...] = contract(acts_ref[0], weight_ref[0], 0, 0)


def encode(acts_t, enc_weight):
    layers, width, tokens = acts_t.shape
    feature_dev = enc_weight.shape[2]
    return pl.pallas_call(
        encode_kernel,
        grid=(layers,),
        in_specs=[
            pl.BlockSpec((1, width, tokens), lambda a: (a, 0, 0)),
            pl.BlockSpec((1, width, feature_dev), lambda a: (a, 0, 0)),
        ],
        out_specs=pl.BlockSpec((tokens, feature_dev), lambda a: (0, a)),
        out_shape=jax.ShapeDtypeStruct((tokens, layers * feature_dev), F32),
        name="encode",
    )(acts_t, enc_weight)


def decode_kernel(layers, core_ref, features_ref, weight_ref, theirs_ref, mine_ref):
    feature_dev = weight_ref.shape[2]
    width = weight_ref.shape[1]
    half = theirs_ref.shape[0]
    core = core_ref[0]
    for ref, side in ((theirs_ref, 1 - core), (mine_ref, core)):
        rows = pl.ds(pl.multiple_of(side * half, half), half)
        for b in range(layers):
            total = None
            for a in range(b + 1):
                term = contract(
                    features_ref[rows, a * feature_dev : (a + 1) * feature_dev],
                    weight_ref[pair_number(a, b, layers)],
                    1,
                    1,
                )
                total = term if total is None else total + term
            ref[:, b * width : (b + 1) * width] = total.astype(ref.dtype)


def decode(core, features, dec_t, layers):
    tokens = features.shape[0]
    shape = (tokens // 2, layers * dec_t.shape[1])
    vmem = pl.BlockSpec(memory_space=pltpu.VMEM)
    return pl.pallas_call(
        functools.partial(decode_kernel, layers),
        in_specs=[pl.BlockSpec(memory_space=pltpu.SMEM), vmem, vmem],
        out_specs=[vmem, vmem],
        out_shape=[jax.ShapeDtypeStruct(shape, BF16), jax.ShapeDtypeStruct(shape, F32)],
        compiler_params=pltpu.CompilerParams(vmem_limit_bytes=VMEM),
        name="decode",
    )(core, features, dec_t)


def upstream_kernel(layers, error_ref, weight_ref, out_ref):
    tokens = error_ref.shape[0]
    width, feature_dev = weight_ref.shape[1:]
    for a in range(layers):
        total = None
        for b in range(a, layers):
            term = contract(
                error_ref[:, b * width : (b + 1) * width], weight_ref[pair_number(a, b, layers)], 1, 0
            )
            total = term if total is None else total + term
        out_ref[:, a * feature_dev : (a + 1) * feature_dev] = total.astype(BF16)
    wide = error_ref[...].astype(F32)
    squared = jnp.sum(wide * wide)
    coarse = squared.astype(BF16).astype(F32)
    fine = squared - coarse
    lane = lax.broadcasted_iota(jnp.int32, (tokens, LANES), 1)
    extra = jnp.where(lane == 0, coarse, jnp.where(lane == 1, fine, 0.0))
    out_ref[:, layers * feature_dev :] = extra.astype(BF16)


def upstream(error, dec_t, layers):
    tokens = error.shape[0]
    vmem = pl.BlockSpec(memory_space=pltpu.VMEM)
    return pl.pallas_call(
        functools.partial(upstream_kernel, layers),
        in_specs=[vmem, vmem],
        out_specs=vmem,
        out_shape=jax.ShapeDtypeStruct((tokens, layers * dec_t.shape[2] + LANES), BF16),
        compiler_params=pltpu.CompilerParams(vmem_limit_bytes=VMEM),
        name="upstream",
    )(error, dec_t)


def encoder_grad_kernel(acts_ref, delta_ref, grad_ref, bias_ref):
    delta = delta_ref[...]
    grad_ref[0] = contract(acts_ref[0], delta, 1, 0)
    bias_ref[0] = jnp.sum(delta.astype(F32), axis=0, keepdims=True)


def encoder_grad(acts_t, delta):
    layers, width, tokens = acts_t.shape
    feature_dev = delta.shape[1] // layers
    grad, bias = pl.pallas_call(
        encoder_grad_kernel,
        grid=(layers,),
        in_specs=[
            pl.BlockSpec((1, width, tokens), lambda a: (a, 0, 0)),
            pl.BlockSpec((tokens, feature_dev), lambda a: (0, a)),
        ],
        out_specs=[
            pl.BlockSpec((1, width, feature_dev), lambda a: (a, 0, 0)),
            pl.BlockSpec((1, 1, feature_dev), lambda a: (a, 0, 0)),
        ],
        out_shape=[
            jax.ShapeDtypeStruct((layers, width, feature_dev), F32),
            jax.ShapeDtypeStruct((layers, 1, feature_dev), F32),
        ],
        compiler_params=pltpu.CompilerParams(vmem_limit_bytes=VMEM),
        name="encoder_grad",
    )(acts_t, delta)
    return grad, bias.reshape(layers, feature_dev)


def local(acts_in, acts_out, enc_weight, enc_bias, dec_weight, dec_bias):
    layers, tokens, width_dev = acts_in.shape
    feature_dev = enc_weight.shape[2]
    pair_list = [(a, b) for a in range(layers) for b in range(a, layers)]
    slots = lax.axis_size(SLOT)
    chips = lax.axis_size(CHIPS)
    core = lax.axis_index(CORE)
    acts_t = jnp.transpose(acts_in, (0, 2, 1))
    dec_t = jnp.transpose(dec_weight, (0, 2, 1))

    def feats(x, a):
        return x[:, a * feature_dev : (a + 1) * feature_dev]

    def width(x, b):
        return x[:, b * width_dev : (b + 1) * width_dev]

    preact = encode(acts_t, enc_weight)
    arrived = exchange(preact.reshape(slots, tokens // slots, -1), SLOT)
    own_preact = arrived.sum(axis=0) + enc_bias.reshape(1, -1)
    own_features = jnp.maximum(own_preact, 0.0).astype(BF16)
    features = sent_to_all(own_features, SLOT).reshape(tokens, -1)

    theirs, mine = decode(core.reshape(1), features, dec_t, layers)
    chip_sum = (mine + lax.ppermute(theirs, CORE, [(0, 1), (1, 0)]).astype(F32)).astype(BF16)
    half = tokens // 2
    portion = half // chips
    rebuilt = exchange(chip_sum.reshape(chips, portion, -1), CHIPS).astype(F32).sum(axis=0)
    offset = core * half + lax.axis_index(CHIPS) * portion
    target = lax.dynamic_slice_in_dim(acts_out, offset, portion, 1)
    target = jnp.transpose(target, (1, 0, 2)).reshape(portion, -1).astype(F32)
    own_error = (rebuilt + dec_bias.reshape(1, -1) - target).astype(BF16)
    half_error = sent_to_all(own_error, CHIPS).reshape(half, -1)
    error = lax.all_gather(half_error, CORE, axis=0, tiled=True)

    sent = upstream(error, dec_t, layers)
    total = exchange(sent.reshape(slots, tokens // slots, -1), SLOT).astype(F32).sum(axis=0)
    mse = (total[0, layers * feature_dev] + total[0, layers * feature_dev + 1]) / (layers * tokens * D)
    own_delta = jnp.where(own_features > 0, total[:, : layers * feature_dev], 0.0).astype(BF16)
    delta = sent_to_all(own_delta, SLOT).reshape(tokens, -1)

    dec_grads = [contract(feats(features, a), width(error, b), 0, 0) for a, b in pair_list]
    enc_grad, bias_grad = encoder_grad(acts_t, delta)
    return (enc_grad, bias_grad, jnp.stack(dec_grads), mse)


def solution(mesh):
    split = Mesh(mesh.devices.reshape(2, 4, 2, 8, 2), (*SLOT, *FEAT))
    in_specs = (
        P(None, None, SLOT),
        P(None, None, SLOT),
        P(None, SLOT, FEAT),
        P(None, FEAT),
        P(None, FEAT, SLOT),
        P(None, SLOT),
    )
    out_specs = (P(None, SLOT, FEAT), P(None, FEAT), P(None, FEAT, SLOT), P())
    return jax.shard_map(local, mesh=split, in_specs=in_specs, out_specs=out_specs, check_vma=False)
```

time: 150 us -> 136 us (0.907)
  blocking collectives: 2.12 us -> 17.4 us
  waiting for transfers between devices: 75.1 us -> 63.8 us
  matrix products: 17.1 us -> 7.18 us
  Pallas kernels: 0 us -> 8.44 us
  other arithmetic: 9.93 us -> 3.53 us
  starting transfers between devices: 31.5 us -> 27.2 us
  between operations: 6.32 us -> 3.18 us
  local copies, waits for them, and re-layouts: 6.66 us -> 4.23 us
    all_to_all x0 -> x1, blocking collectives: none -> 15.3 us  [exchange(): return lax.all_to_all(tiles, axis, split_axis=0, concat_axis=0, tiled=True)]
    all_to_all x6 -> x5, waiting for transfers between devices: 73.3 us -> 62.4 us  [exchange(): return lax.all_to_all(tiles, axis, split_axis=0, concat_axis=0, tiled=True)]
    dot_general x24 -> x6, matrix products: 17.1 us -> 7.18 us  [contract(): lax.dot_general(x, y, (((x_dim,), (y_dim,)), ((), ())), preferred_element...]
    pallas_call x0 -> x4, Pallas kernels: none -> 8.44 us  [the longest x1 3.72 us: encode(): pl.pallas_call(encode_kernel, grid=(layers,), in_specs=[pl.BlockSpec((1,...]
    all_to_all x6 -> x5, starting transfers between devices: 31.5 us -> 27.1 us  [exchange(): return lax.all_to_all(tiles, axis, split_axis=0, concat_axis=0, tiled=True)]
    concatenate x3 -> x0, other arithmetic: 3.24 us -> none  [the longest x1 1.93 us: local(): sent = jnp.concatenate([*partials, extra], axis=1).astype(bf16)]
    convert_element_type x3 -> x1, local copies, waits for them, and re-layouts: 2.63 us -> 0.14 us  [local(): target = jnp.transpose(target, (1, 0, 2)).reshape(portion, -1).astype(F32)]
    another operation x2 -> x0, other arithmetic: 2.04 us -> none  [the longest x1 1.38 us: local(): return (jnp.stack(enc_grads), bias_grad, jnp.stack(dec_grads), mse)]
  transfers between devices with their start and end apart: 7 -> 6, of which waited for: 7 -> 6; matrix products, arithmetic and copies ran while one was open for 6% -> 7% of each run, Pallas kernels for 0% -> 0%
where the time goes in v2:
time: 136 us; the launch traced here: 135 us
  waiting for transfers between devices  63.8 us (47%)
  starting transfers between devices  27.2 us (20%)
  blocking collectives  17.4 us (13%)
  Pallas kernels  8.44 us (6%)
  matrix products  7.18 us (5%)
  local copies, waits for them, and re-layouts  4.23 us (3%)
  other arithmetic  3.53 us (3%)
  between operations  3.18 us (2%)
    all_to_all x5, waiting for transfers between devices, exchange(): return lax.all_to_all(tiles, axis, split_axis=0, concat_axis=0, tiled=True)  62.4 us
    all_to_all x5, starting transfers between devices, exchange(): return lax.all_to_all(tiles, axis, split_axis=0, concat_axis=0, tiled=True)  27.1 us
    all_to_all x1, blocking collectives, exchange(): return lax.all_to_all(tiles, axis, split_axis=0, concat_axis=0, tiled=True)  15.3 us
    dot_general x6, matrix products, contract(): lax.dot_general(x, y, (((x_dim,), (y_dim,)), ((), ())), preferred_element...  7.18 us
    pallas_call x1, Pallas kernels, encode(): pl.pallas_call(encode_kernel, grid=(layers,), in_specs=[pl.BlockSpec((1,...  3.72 us
  transfers between devices with their start and end apart: 6, of which 6 were waited for; matrix products, arithmetic and copies ran while one was open for 7% of the time, Pallas kernels for 0%

profile of v2, /device:TPU:32, one launch (start us, length us, event | category | flops | bytes accessed | tf_op | source)
XLA Modules:
  0.0 135.1 jit_solution(5545887314911407378)
XLA Ops:
  0.6 0.0 copy-start.3
  0.6 3.7 %encode.1 = f32[256,1536]{1,0:T(8,128)} custom-call(bf16[3,288,256]{2,1,0:T(8,128)(2,1)} %bitcast.52, bf16[3,288,512]{2,1,0:T(8,128)(2,1)} %weight_ref.1), custom_call_target="tpu_custom_call" | custom-call | tf_op jit(solution)/shard_map/encode/pallas_call | solution.py:45
  4.4 0.0 copy-start
  4.4 5.4 %all-to-all-start = ((f32[8,32,1536]{2,1,0:T(8,128)}), f32[8,32,1536]{2,1,0:T(8,128)}, u32[]{:S(2)}, u32[]{:S(2)}) async-start(f32[8,32,1536]{2,1,0:T(8,128)} %bitcast.54), calls=%async_computation | async-start | bytes 3145728 | tf_op jit(solution)/shard_map/all_to_all | solution.py:23
  9.8 0.0 copy-done.3
  9.8 21.4 %all-to-all-done = f32[8,32,1536]{2,1,0:T(8,128)} async-done(((f32[8,32,1536]{2,1,0:T(8,128)}), f32[8,32,1536]{2,1,0:T(8,128)}, u32[]{:S(2)}, u32[]{:S(2)}) %all-to-all-start) | async-done | bytes 1572896 | tf_op jit(solution)/shard_map/all_to_all | solution.py:23
  31.2 1.5 %reduce_sum.27 = f32[32,1536]{1,0:T(8,128)S(1)} reduce(f32[8,32,1536]{2,1,0:T(8,128)} %all-to-all-done, f32[]{:T(128)} %constant.10.clone.1), dimensions={0}, to_apply=%region_0.0 | reduce | flops 344064 | bytes 1769476 | tf_op jit(solution)/shard_map/reduce_sum | solution.py:173
  32.8 0.9 broadcast_in_dim.7
  33.7 0.0 copy-start.4
  33.7 3.7 %all-to-all-start.1 = ((bf16[8,32,1536]{2,1,0:T(8,128)(2,1)}), bf16[8,32,1536]{2,1,0:T(8,128)(2,1)S(1)}, u32[]{:S(2)}, u32[]{:S(2)}) async-start(bf16[8,32,1536]{2,1,0:T(8,128)(2,1)} %broadcast_in_dim.7), calls=%async_computation.1 | async-start | bytes 1572864 | tf_op jit(solution)/shard_map/all_to_all | solution.py:23
  37.4 12.9 %all-to-all-done.1 = bf16[8,32,1536]{2,1,0:T(8,128)(2,1)S(1)} async-done(((bf16[8,32,1536]{2,1,0:T(8,128)(2,1)}), bf16[8,32,1536]{2,1,0:T(8,128)(2,1)S(1)}, u32[]{:S(2)}, u32[]{:S(2)}) %all-to-all-start.1) | async-done | bytes 786464 | tf_op jit(solution)/shard_map/all_to_all | solution.py:23
  50.3 0.0 copy-done
  50.3 1.5 %decode.1 = (bf16[128,864]{1,0:T(8,128)(2,1)S(1)}, f32[128,864]{1,0:T(8,128)S(1)}) custom-call(s32[1]{0:T(128)} %bitcast.2.core_ref, bf16[256,1536]{1,0:T(8,128)(2,1)S(1)} %bitcast.41, bf16[6,288,512]{2,1,0:T(8,128)(2,1)S(1)} %bitcast.48), custom_call_target="tpu_custom_call" | custom-call | tf_op jit(solution)/shard_map/decode/pallas_call | solution.py:82
  51.9 0.1 collective-permute-start
  52.0 1.5 %collective-permute-done = bf16[128,864]{1,0:T(8,128)(2,1)S(1)} collective-permute-done((bf16[128,864]{1,0:T(8,128)(2,1)S(1)}, bf16[128,864]{1,0:T(8,128)(2,1)S(1)}, u32[]{:S(2)}, u32[]{:S(2)}) %collective-permute-start) | collective-permute-done | bytes 221216 | tf_op jit(solution)/shard_map/ppermute | solution.py:178
  53.5 0.7 fusion.9
  54.2 10.9 %all-to-all-start.2 = ((bf16[16,8,864]{2,1,0:T(8,128)(2,1)}), bf16[16,8,864]{2,1,0:T(8,128)(2,1)S(1)}, u32[]{:S(2)}, u32[]{:S(2)}) async-start(bf16[16,8,864]{2,1,0:T(8,128)(2,1)} %fusion.9), calls=%async_computation.2 | async-start | bytes 458752 | tf_op jit(solution)/shard_map/all_to_all | solution.py:23
  65.1 1.1 dynamic-slice_convert_fusion
  66.2 0.1 copy.13
  66.3 0.0 copy-done.4
  66.3 0.1 add.48
  66.4 10.0 %all-to-all-done.2 = bf16[16,8,864]{2,1,0:T(8,128)(2,1)S(1)} async-done(((bf16[16,8,864]{2,1,0:T(8,128)(2,1)}), bf16[16,8,864]{2,1,0:T(8,128)(2,1)S(1)}, u32[]{:S(2)}, u32[]{:S(2)}) %all-to-all-start.2) | async-done | bytes 221216 | tf_op jit(solution)/shard_map/all_to_all | solution.py:23
  76.5 15.3 %all_to_all.30 = bf16[16,8,864]{2,1,0:T(8,128)(2,1)S(1)} all-to-all(bf16[16,8,864]{2,1,0:T(8,128)(2,1)S(1)} %broadcast_in_dim.8), channel_id=1, replica_groups=mesh['slot_0'=2,'slot_1'=4,'feat_0'=2,'feat_1'=8,'feat_2'=2] {'feat_0','..., dimensions={0} | all-to-all | bytes 442368 | tf_op jit(solution)/shard_map/all_to_all | solution.py:23
  91.8 2.1 %all_gather.3.error_ref = bf16[256,864]{1,0:T(8,128)(2,1)S(1)} all-gather(bf16[128,864]{1,0:T(8,128)(2,1)S(1)} %bitcast.56), channel_id=1, replica_groups=mesh['slot_0'=2,'slot_1'=4,'feat_0'=2,'feat_1'=8,'feat_2'=2] {'feat_2'}, dimensions={0}, use_global_device_ids=true | all-gather | bytes 663552 | tf_op jit(solution)/shard_map/all_gather | solution.py:187
  93.9 1.0 upstream.1
  94.9 0.0 copy-start.1
  94.9 0.9 copy-done.1
  95.8 3.6 %all-to-all-start.4 = ((bf16[8,32,1664]{2,1,0:T(8,128)(2,1)}), bf16[8,32,1664]{2,1,0:T(8,128)(2,1)S(1)}, u32[]{:S(2)}, u32[]{:S(2)}) async-start(bf16[8,32,1664]{2,1,0:T(8,128)(2,1)} %bitcast.50), calls=%async_computation.4 | async-start | bytes 1703936 | tf_op jit(solution)/shard_map/all_to_all | solution.py:23
  99.4 1.1 fusion.5
  100.5 1.2 fusion.4
  101.7 1.2 fusion.3
  102.9 0.0 copy-start.2
  102.9 10.6 %all-to-all-done.4 = bf16[8,32,1664]{2,1,0:T(8,128)(2,1)S(1)} async-done(((bf16[8,32,1664]{2,1,0:T(8,128)(2,1)}), bf16[8,32,1664]{2,1,0:T(8,128)(2,1)S(1)}, u32[]{:S(2)}, u32[]{:S(2)}) %all-to-all-start.4) | async-done | bytes 852000 | tf_op jit(solution)/shard_map/all_to_all | solution.py:23
  113.5 0.1 convert_reduce_fusion
  113.6 0.9 broadcast_in_dim.10
  114.6 3.5 %all-to-all-start.5 = ((bf16[8,32,1536]{2,1,0:T(8,128)(2,1)}), bf16[8,32,1536]{2,1,0:T(8,128)(2,1)S(1)}, u32[]{:S(2)}, u32[]{:S(2)}) async-start(bf16[8,32,1536]{2,1,0:T(8,128)(2,1)} %broadcast_in_dim.10), calls=%async_computation.5 | async-start | bytes 1572864 | tf_op jit(solution)/shard_map/all_to_all | solution.py:23
  118.1 1.2 fusion.2
  119.4 1.2 fusion.1
  120.6 1.2 fusion
  121.8 0.6 fusion.20
  123.7 7.5 %all-to-all-done.5 = bf16[8,32,1536]{2,1,0:T(8,128)(2,1)S(1)} async-done(((bf16[8,32,1536]{2,1,0:T(8,128)(2,1)}), bf16[8,32,1536]{2,1,0:T(8,128)(2,1)S(1)}, u32[]{:S(2)}, u32[]{:S(2)}) %all-to-all-start.5) | async-done | bytes 786464 | tf_op jit(solution)/shard_map/all_to_all | solution.py:23
  131.2 0.0 copy-done.2
  131.2 2.2 %encoder_grad.1 = (f32[3,288,512]{2,1,0:T(8,128)}, f32[3,1,512]{2,1,0:T(1,128)S(1)}) custom-call(bf16[3,288,256]{2,1,0:T(8,128)(2,1)S(1)} %bitcast.53, bf16[256,1536]{1,0:T(8,128)(2,1)S(1)} %bitcast.51), custom_call_target="tpu_custom_call" | custom-call | tf_op jit(solution)/shard_map/encoder_grad/pallas_call | solution.py:134
  133.3 0.6 copy.16
  (6 shorter events, 0.1 us)
Async XLA Ops:
  0.6 9.2 %copy-start.3 = (f32[3,512]{1,0:T(4,128)S(1)}, f32[3,512]{1,0:T(4,128)}, u32[]{:S(2)}) copy-start(f32[3,512]{1,0:T(4,128)} %param.9) | copy-start | bytes 18436
  4.4 46.0 %copy-start = (bf16[6,512,288]{1,2,0:T(8,128)(2,1)S(1)}, bf16[6,512,288]{1,2,0:T(8,128)(2,1)}, u32[]{:S(2)}) copy-start(bf16[6,512,288]{1,2,0:T(8,128)(2,1)} %param.10) | copy-start | bytes 5308420
  4.4 26.9 %all-to-all-start = ((f32[8,32,1536]{2,1,0:T(8,128)}), f32[8,32,1536]{2,1,0:T(8,128)}, u32[]{:S(2)}, u32[]{:S(2)}) async-start(f32[8,32,1536]{2,1,0:T(8,128)} %bitcast.54), calls=%async_computation | async-start | bytes 3145728 | tf_op jit(solution)/shard_map/all_to_all | solution.py:23
  33.7 32.6 %copy-start.4 = (f32[3,288]{1,0:T(4,128)S(1)}, f32[3,288]{1,0:T(4,128)}, u32[]{:S(2)}) copy-start(f32[3,288]{1,0:T(4,128)} %param.11) | copy-start | bytes 10372
  33.7 16.6 %all-to-all-start.1 = ((bf16[8,32,1536]{2,1,0:T(8,128)(2,1)}), bf16[8,32,1536]{2,1,0:T(8,128)(2,1)S(1)}, u32[]{:S(2)}, u32[]{:S(2)}) async-start(bf16[8,32,1536]{2,1,0:T(8,128)(2,1)} %broadcast_in_dim.7), calls=%async_computation.1 | async-start | bytes 1572864 | tf_op jit(solution)/shard_map/all_to_all | solution.py:23
  51.9 1.6 %collective-permute-start = (bf16[128,864]{1,0:T(8,128)(2,1)S(1)}, bf16[128,864]{1,0:T(8,128)(2,1)S(1)}, u32[]{:S(2)}, u32[]{:S(2)}) collective-permute-start(bf16[128,864]{1,0:T(8,128)(2,1)S(1)} %get-tuple-element.9), channel_id=1, source_target_pairs={{0,1},{1,0},{2,3},{3,2},{4,5},{5,4},{6,7},{7,6},{8,9},{9,8},{10,11... | collective-permute-start | bytes 663560 | tf_op jit(solution)/shard_map/ppermute | solution.py:178
  54.2 22.2 %all-to-all-start.2 = ((bf16[16,8,864]{2,1,0:T(8,128)(2,1)}), bf16[16,8,864]{2,1,0:T(8,128)(2,1)S(1)}, u32[]{:S(2)}, u32[]{:S(2)}) async-start(bf16[16,8,864]{2,1,0:T(8,128)(2,1)} %fusion.9), calls=%async_computation.2 | async-start | bytes 458752 | tf_op jit(solution)/shard_map/all_to_all | solution.py:23
  94.9 0.9 copy-start.1
  95.8 17.7 %all-to-all-start.4 = ((bf16[8,32,1664]{2,1,0:T(8,128)(2,1)}), bf16[8,32,1664]{2,1,0:T(8,128)(2,1)S(1)}, u32[]{:S(2)}, u32[]{:S(2)}) async-start(bf16[8,32,1664]{2,1,0:T(8,128)(2,1)} %bitcast.50), calls=%async_computation.4 | async-start | bytes 1703936 | tf_op jit(solution)/shard_map/all_to_all | solution.py:23
  102.9 28.3 %copy-start.2 = (bf16[3,256,288]{1,2,0:T(8,128)(2,1)S(1)}, bf16[3,256,288]{1,2,0:T(8,128)(2,1)}, u32[]{:S(2)}) copy-start(bf16[3,256,288]{1,2,0:T(8,128)(2,1)} %param.6) | copy-start | bytes 1327108
  114.6 16.6 %all-to-all-start.5 = ((bf16[8,32,1536]{2,1,0:T(8,128)(2,1)}), bf16[8,32,1536]{2,1,0:T(8,128)(2,1)S(1)}, u32[]{:S(2)}, u32[]{:S(2)}) async-start(bf16[8,32,1536]{2,1,0:T(8,128)(2,1)} %broadcast_in_dim.10), calls=%async_computation.5 | async-start | bytes 1572864 | tf_op jit(solution)/shard_map/all_to_all | solution.py:23

commit v3 on v2

--- a/solution.py
+++ b/solution.py
@@ -35,8 +35,10 @@
     return lax.dot_general(x, y, (((x_dim,), (y_dim,)), ((), ())), preferred_element_type=F32)
 
 
-def encode_kernel(acts_ref, weight_ref, out_ref):
-    out_ref[...] = contract(acts_ref[0], weight_ref[0], 0, 0)
+def encode_kernel(acts_ref, weight_ref, out_ref, rounded_ref):
+    preact = contract(acts_ref[0], weight_ref[0], 0, 0)
+    out_ref[...] = preact
+    rounded_ref[...] = preact.astype(BF16)
 
 
 def encode(acts_t, enc_weight):
@@ -49,8 +51,8 @@
             pl.BlockSpec((1, width, tokens), lambda a: (a, 0, 0)),
             pl.BlockSpec((1, width, feature_dev), lambda a: (a, 0, 0)),
         ],
-        out_specs=pl.BlockSpec((tokens, feature_dev), lambda a: (0, a)),
-        out_shape=jax.ShapeDtypeStruct((tokens, layers * feature_dev), F32),
+        out_specs=[pl.BlockSpec((tokens, feature_dev), lambda a: (0, a))] * 2,
+        out_shape=[jax.ShapeDtypeStruct((tokens, layers * feature_dev), kind) for kind in (F32, BF16)],
         name="encode",
     )(acts_t, enc_weight)
 
@@ -168,11 +170,14 @@
     def width(x, b):
         return x[:, b * width_dev : (b + 1) * width_dev]
 
-    preact = encode(acts_t, enc_weight)
-    arrived = exchange(preact.reshape(slots, tokens // slots, -1), SLOT)
-    own_preact = arrived.sum(axis=0) + enc_bias.reshape(1, -1)
+    bias_row = enc_bias.reshape(1, -1)
+    preact, rounded = encode(acts_t, enc_weight)
+    arrived = exchange(rounded.reshape(slots, tokens // slots, -1), SLOT)
+    own_preact = arrived.astype(F32).sum(axis=0) + bias_row
     own_features = jnp.maximum(own_preact, 0.0).astype(BF16)
     features = sent_to_all(own_features, SLOT).reshape(tokens, -1)
+    features, preact = lax.optimization_barrier((features, preact))
+    slope = lax.psum_scatter(preact, SLOT, scatter_dimension=0, tiled=True) + bias_row > 0
 
     theirs, mine = decode(core.reshape(1), features, dec_t, layers)
     chip_sum = (mine + lax.ppermute(theirs, CORE, [(0, 1), (1, 0)]).astype(F32)).astype(BF16)
@@ -189,7 +194,7 @@
     sent = upstream(error, dec_t, layers)
     total = exchange(sent.reshape(slots, tokens // slots, -1), SLOT).astype(F32).sum(axis=0)
     mse = (total[0, layers * feature_dev] + total[0, layers * feature_dev + 1]) / (layers * tokens * D)
-    own_delta = jnp.where(own_features > 0, total[:, : layers * feature_dev], 0.0).astype(BF16)
+    own_delta = jnp.where(slope, total[:, : layers * feature_dev], 0.0).astype(BF16)
     delta = sent_to_all(own_delta, SLOT).reshape(tokens, -1)
 
     dec_grads = [contract(feats(features, a), width(error, b), 0, 0) for a, b in pair_list]

time: 136 us -> 140 us (1.029)
  waiting for transfers between devices: 63.8 us -> 41.7 us
  blocking collectives: 17.4 us -> 33.8 us
  between operations: 3.18 us -> 16.6 us
  starting transfers between devices: 27.2 us -> 23.6 us
    all_to_all x5 -> x4, waiting for transfers between devices: 62.4 us -> 40.2 us  [exchange(): return lax.all_to_all(tiles, axis, split_axis=0, concat_axis=0, tiled=True)]
    all_to_all x1 -> x2, blocking collectives: 15.3 us -> 31.7 us  [exchange(): return lax.all_to_all(tiles, axis, split_axis=0, concat_axis=0, tiled=True)]
    all_to_all x5 -> x4, starting transfers between devices: 27.1 us -> 23.5 us  [exchange(): return lax.all_to_all(tiles, axis, split_axis=0, concat_axis=0, tiled=True)]
  transfers between devices with their start and end apart: 6 -> 6, of which waited for: 6 -> 5; matrix products, arithmetic and copies ran while one was open for 7% -> 8% of each run, Pallas kernels for 0% -> 2%
where the time goes in v3:
time: 140 us; the launch traced here: 139 us
  waiting for transfers between devices  41.7 us (30%)
  blocking collectives  33.8 us (24%)
  starting transfers between devices  23.6 us (17%)
  between operations  16.6 us (12%)
  Pallas kernels  8.73 us (6%)
  matrix products  7.18 us (5%)
  local copies, waits for them, and re-layouts  4.04 us (3%)
  other arithmetic  3.05 us (2%)
    all_to_all x4, waiting for transfers between devices, exchange(): return lax.all_to_all(tiles, axis, split_axis=0, concat_axis=0, tiled=True)  40.2 us
    all_to_all x2, blocking collectives, exchange(): return lax.all_to_all(tiles, axis, split_axis=0, concat_axis=0, tiled=True)  31.7 us
    all_to_all x4, starting transfers between devices, exchange(): return lax.all_to_all(tiles, axis, split_axis=0, concat_axis=0, tiled=True)  23.5 us
    dot_general x6, matrix products, contract(): lax.dot_general(x, y, (((x_dim,), (y_dim,)), ((), ())), preferred_element...  7.18 us
    pallas_call x1, Pallas kernels, encode(): pl.pallas_call(encode_kernel, grid=(layers,), in_specs=[pl.BlockSpec((1,...  4 us
  transfers between devices with their start and end apart: 6, of which 5 were waited for; matrix products, arithmetic and copies ran while one was open for 8% of the time, Pallas kernels for 2%

profile of v3, /device:TPU:32, one launch (start us, length us, event | category | flops | bytes accessed | tf_op | source)
XLA Modules:
  0.0 138.7 jit_solution(18306089241933847605)
XLA Ops:
  7.2 4.0 %encode.1 = (f32[256,1536]{1,0:T(8,128)}, bf16[256,1536]{1,0:T(8,128)(2,1)}) custom-call(bf16[3,288,256]{2,1,0:T(8,128)(2,1)} %bitcast.52, bf16[3,288,512]{2,1,0:T(8,128)(2,1)} %weight_ref.1), custom_call_target="tpu_custom_call" | custom-call | tf_op jit(solution)/shard_map/encode/pallas_call | solution.py:47
  11.2 0.0 copy-start
  11.2 5.4 %all-to-all-start = ((bf16[8,32,1536]{2,1,0:T(8,128)(2,1)}), bf16[8,32,1536]{2,1,0:T(8,128)(2,1)S(1)}, u32[]{:S(2)}, u32[]{:S(2)}) async-start(bf16[8,32,1536]{2,1,0:T(8,128)(2,1)} %bitcast.56), calls=%async_computation | async-start | bytes 1572864 | tf_op jit(solution)/shard_map/all_to_all | solution.py:23
  16.6 0.0 reduce-scatter.2.cloned.1.call-start
  16.7 0.7 add.52
  17.4 12.1 %all-to-all-done = bf16[8,32,1536]{2,1,0:T(8,128)(2,1)S(1)} async-done(((bf16[8,32,1536]{2,1,0:T(8,128)(2,1)}), bf16[8,32,1536]{2,1,0:T(8,128)(2,1)S(1)}, u32[]{:S(2)}, u32[]{:S(2)}) %all-to-all-start) | async-done | bytes 786464 | tf_op jit(solution)/shard_map/all_to_all | solution.py:23
  29.5 0.1 convert_reduce_fusion.1
  29.6 0.1 broadcast_in_dim.7
  29.7 15.4 %all_to_all.30 = bf16[8,32,1536]{2,1,0:T(8,128)(2,1)S(1)} all-to-all(bf16[8,32,1536]{2,1,0:T(8,128)(2,1)S(1)} %broadcast_in_dim.7), channel_id=1, replica_groups=mesh['slot_0'=2,'slot_1'=4,'feat_0'=2,'feat_1'=8,'feat_2'=2] {'slot_0','..., dimensions={0} | all-to-all | bytes 1572864 | tf_op jit(solution)/shard_map/all_to_all | solution.py:23
  45.1 0.0 copy-start.3
  45.1 0.0 reduce-scatter.2.cloned.1.call-update
  45.2 0.0 copy-done
  45.2 1.5 %decode.1 = (bf16[128,864]{1,0:T(8,128)(2,1)S(1)}, f32[128,864]{1,0:T(8,128)S(1)}) custom-call(s32[1]{0:T(128)} %bitcast.3.core_ref, bf16[256,1536]{1,0:T(8,128)(2,1)S(1)} %bitcast.41, bf16[6,288,512]{2,1,0:T(8,128)(2,1)S(1)} %bitcast.48), custom_call_target="tpu_custom_call" | custom-call | tf_op jit(solution)/shard_map/decode/pallas_call | solution.py:84
  46.7 0.1 collective-permute-start
  46.8 1.5 %collective-permute-done = bf16[128,864]{1,0:T(8,128)(2,1)S(1)} collective-permute-done((bf16[128,864]{1,0:T(8,128)(2,1)S(1)}, bf16[128,864]{1,0:T(8,128)(2,1)S(1)}, u32[]{:S(2)}, u32[]{:S(2)}) %collective-permute-start) | collective-permute-done | bytes 221216 | tf_op jit(solution)/shard_map/ppermute | solution.py:183
  48.3 0.7 fusion.9
  49.0 10.9 %all-to-all-start.2 = ((bf16[16,8,864]{2,1,0:T(8,128)(2,1)}), bf16[16,8,864]{2,1,0:T(8,128)(2,1)S(1)}, u32[]{:S(2)}, u32[]{:S(2)}) async-start(bf16[16,8,864]{2,1,0:T(8,128)(2,1)} %fusion.9), calls=%async_computation.3 | async-start | bytes 458752 | tf_op jit(solution)/shard_map/all_to_all | solution.py:23
  60.0 1.1 dynamic-slice_convert_fusion
  61.0 0.1 copy.13
  61.2 0.0 copy-done.3
  61.2 0.1 add.57
  61.3 10.0 %all-to-all-done.2 = bf16[16,8,864]{2,1,0:T(8,128)(2,1)S(1)} async-done(((bf16[16,8,864]{2,1,0:T(8,128)(2,1)}), bf16[16,8,864]{2,1,0:T(8,128)(2,1)S(1)}, u32[]{:S(2)}, u32[]{:S(2)}) %all-to-all-start.2) | async-done | bytes 221216 | tf_op jit(solution)/shard_map/all_to_all | solution.py:23
  71.3 16.3 %all_to_all.31 = bf16[16,8,864]{2,1,0:T(8,128)(2,1)S(1)} all-to-all(bf16[16,8,864]{2,1,0:T(8,128)(2,1)S(1)} %broadcast_in_dim.8), channel_id=1, replica_groups=mesh['slot_0'=2,'slot_1'=4,'feat_0'=2,'feat_1'=8,'feat_2'=2] {'feat_0','..., dimensions={0} | all-to-all | bytes 442368 | tf_op jit(solution)/shard_map/all_to_all | solution.py:23
  87.6 2.1 %all_gather.3.error_ref = bf16[256,864]{1,0:T(8,128)(2,1)S(1)} all-gather(bf16[128,864]{1,0:T(8,128)(2,1)S(1)} %bitcast.55), channel_id=1, replica_groups=mesh['slot_0'=2,'slot_1'=4,'feat_0'=2,'feat_1'=8,'feat_2'=2] {'feat_2'}, dimensions={0}, use_global_device_ids=true | all-gather | bytes 663552 | tf_op jit(solution)/shard_map/all_gather | solution.py:192
  89.7 1.0 upstream.1
  90.7 0.0 copy-start.1
  90.7 0.9 copy-done.1
  91.6 3.5 %all-to-all-start.4 = ((bf16[8,32,1664]{2,1,0:T(8,128)(2,1)}), bf16[8,32,1664]{2,1,0:T(8,128)(2,1)S(1)}, u32[]{:S(2)}, u32[]{:S(2)}) async-start(bf16[8,32,1664]{2,1,0:T(8,128)(2,1)} %bitcast.50), calls=%async_computation.5 | async-start | bytes 1703936 | tf_op jit(solution)/shard_map/all_to_all | solution.py:23
  95.2 1.1 fusion.5
  96.3 1.2 fusion.4
  97.5 1.2 fusion.3
  98.7 0.0 copy-start.2
  98.7 10.6 %all-to-all-done.4 = bf16[8,32,1664]{2,1,0:T(8,128)(2,1)S(1)} async-done(((bf16[8,32,1664]{2,1,0:T(8,128)(2,1)}), bf16[8,32,1664]{2,1,0:T(8,128)(2,1)S(1)}, u32[]{:S(2)}, u32[]{:S(2)}) %all-to-all-start.4) | async-done | bytes 852000 | tf_op jit(solution)/shard_map/all_to_all | solution.py:23
  109.3 0.1 convert_reduce_fusion
  109.4 0.0 reduce-scatter.2.cloned.1.call-done
  109.4 1.0 fusion.14
  110.4 0.9 broadcast_in_dim.10
  111.3 3.5 %all-to-all-start.5 = ((bf16[8,32,1536]{2,1,0:T(8,128)(2,1)}), bf16[8,32,1536]{2,1,0:T(8,128)(2,1)S(1)}, u32[]{:S(2)}, u32[]{:S(2)}) async-start(bf16[8,32,1536]{2,1,0:T(8,128)(2,1)} %broadcast_in_dim.10), calls=%async_computation.6 | async-start | bytes 1572864 | tf_op jit(solution)/shard_map/all_to_all | solution.py:23
  114.9 1.2 fusion.2
  116.1 1.2 fusion.1
  117.3 1.2 fusion
  118.6 0.6 fusion.20
  120.4 7.5 %all-to-all-done.5 = bf16[8,32,1536]{2,1,0:T(8,128)(2,1)S(1)} async-done(((bf16[8,32,1536]{2,1,0:T(8,128)(2,1)}), bf16[8,32,1536]{2,1,0:T(8,128)(2,1)S(1)}, u32[]{:S(2)}, u32[]{:S(2)}) %all-to-all-start.5) | async-done | bytes 786464 | tf_op jit(solution)/shard_map/all_to_all | solution.py:23
  127.9 0.0 copy-done.2
  127.9 2.2 %encoder_grad.1 = (f32[3,288,512]{2,1,0:T(8,128)}, f32[3,1,512]{2,1,0:T(1,128)S(1)}) custom-call(bf16[3,288,256]{2,1,0:T(8,128)(2,1)S(1)} %bitcast.53, bf16[256,1536]{1,0:T(8,128)(2,1)S(1)} %bitcast.51), custom_call_target="tpu_custom_call" | custom-call | tf_op jit(solution)/shard_map/encoder_grad/pallas_call | solution.py:136
  130.1 0.6 copy.16
  (4 shorter events, 0.1 us)
Async XLA Ops:
  11.2 34.0 %copy-start = (bf16[6,512,288]{1,2,0:T(8,128)(2,1)S(1)}, bf16[6,512,288]{1,2,0:T(8,128)(2,1)}, u32[]{:S(2)}) copy-start(bf16[6,512,288]{1,2,0:T(8,128)(2,1)} %param.10) | copy-start | bytes 5308420
  11.2 18.3 %all-to-all-start = ((bf16[8,32,1536]{2,1,0:T(8,128)(2,1)}), bf16[8,32,1536]{2,1,0:T(8,128)(2,1)S(1)}, u32[]{:S(2)}, u32[]{:S(2)}) async-start(bf16[8,32,1536]{2,1,0:T(8,128)(2,1)} %bitcast.56), calls=%async_computation | async-start | bytes 1572864 | tf_op jit(solution)/shard_map/all_to_all | solution.py:23
  16.6 92.8 %reduce-scatter.2.cloned.1.call-start = ((), (), s32[]{:S(2)}) async-start(), calls=%async_computation.7 | async-start | bytes 1769472 | tf_op jit(solution)/shard_map/reduce_scatter | solution.py:180
  45.1 16.0 %copy-start.3 = (f32[3,288]{1,0:T(4,128)S(1)}, f32[3,288]{1,0:T(4,128)}, u32[]{:S(2)}) copy-start(f32[3,288]{1,0:T(4,128)} %param.11) | copy-start | bytes 10372
  46.7 1.6 %collective-permute-start = (bf16[128,864]{1,0:T(8,128)(2,1)S(1)}, bf16[128,864]{1,0:T(8,128)(2,1)S(1)}, u32[]{:S(2)}, u32[]{:S(2)}) collective-permute-start(bf16[128,864]{1,0:T(8,128)(2,1)S(1)} %get-tuple-element.17), channel_id=1, source_target_pairs={{0,1},{1,0},{2,3},{3,2},{4,5},{5,4},{6,7},{7,6},{8,9},{9,8},{10,11... | collective-permute-start | bytes 663560 | tf_op jit(solution)/shard_map/ppermute | solution.py:183
  49.0 22.2 %all-to-all-start.2 = ((bf16[16,8,864]{2,1,0:T(8,128)(2,1)}), bf16[16,8,864]{2,1,0:T(8,128)(2,1)S(1)}, u32[]{:S(2)}, u32[]{:S(2)}) async-start(bf16[16,8,864]{2,1,0:T(8,128)(2,1)} %fusion.9), calls=%async_computation.3 | async-start | bytes 458752 | tf_op jit(solution)/shard_map/all_to_all | solution.py:23
  90.7 0.9 copy-start.1
  91.6 17.7 %all-to-all-start.4 = ((bf16[8,32,1664]{2,1,0:T(8,128)(2,1)}), bf16[8,32,1664]{2,1,0:T(8,128)(2,1)S(1)}, u32[]{:S(2)}, u32[]{:S(2)}) async-start(bf16[8,32,1664]{2,1,0:T(8,128)(2,1)} %bitcast.50), calls=%async_computation.5 | async-start | bytes 1703936 | tf_op jit(solution)/shard_map/all_to_all | solution.py:23
  98.7 29.2 %copy-start.2 = (bf16[3,256,288]{1,2,0:T(8,128)(2,1)S(1)}, bf16[3,256,288]{1,2,0:T(8,128)(2,1)}, u32[]{:S(2)}) copy-start(bf16[3,256,288]{1,2,0:T(8,128)(2,1)} %param.6) | copy-start | bytes 1327108
  111.3 16.6 %all-to-all-start.5 = ((bf16[8,32,1536]{2,1,0:T(8,128)(2,1)}), bf16[8,32,1536]{2,1,0:T(8,128)(2,1)S(1)}, u32[]{:S(2)}, u32[]{:S(2)}) async-start(bf16[8,32,1536]{2,1,0:T(8,128)(2,1)} %broadcast_in_dim.10), calls=%async_computation.6 | async-start | bytes 1572864 | tf_op jit(solution)/shard_map/all_to_all | solution.py:23
Sparse Core Ops, SparseCore 0:
  45.3 45.2 reduce-scatter.1

commit v4 on v2

--- a/solution.py
+++ b/solution.py
@@ -15,6 +15,9 @@
 CORE = "feat_2"
 LANES = 128
 VMEM = 16 * 2**20
+SPAN = 173.2868
+ABOVE = 1.0078125
+TINY = 1e-30
 F32 = jnp.float32
 BF16 = jnp.bfloat16
 
@@ -35,24 +38,150 @@
     return lax.dot_general(x, y, (((x_dim,), (y_dim,)), ((), ())), preferred_element_type=F32)
 
 
-def encode_kernel(acts_ref, weight_ref, out_ref):
-    out_ref[...] = contract(acts_ref[0], weight_ref[0], 0, 0)
+def start(copies):
+    for copy in copies:
+        copy.start()
+    return copies
+
+
+def finish(copies):
+    for copy in copies:
+        copy.wait()
+
+
+def encode_kernel(acts_hbm, weight_hbm, out_hbm, acts_ref, weight_ref, held_ref, acts_sems, weight_sems, out_sems):
+    layers = acts_ref.shape[0]
+    feature_dev = weight_ref.shape[2]
+    tokens = held_ref.shape[0]
+    arriving = [
+        start(
+            [
+                pltpu.make_async_copy(acts_hbm.at[a], acts_ref.at[a], acts_sems.at[a]),
+                pltpu.make_async_copy(weight_hbm.at[a], weight_ref.at[a], weight_sems.at[a]),
+            ]
+        )
+        for a in range(layers)
+    ]
+    leaving = []
+
+    def send(step, columns):
+        copy = pltpu.make_async_copy(held_ref.at[:, columns], out_hbm.at[:, columns], out_sems.at[step])
+        leaving.extend(start([copy]))
+
+    lane = lax.broadcasted_iota(jnp.int32, (tokens, LANES), 1)
+    scales = jnp.zeros((tokens, LANES), F32)
+    for a in range(layers):
+        finish(arriving[a])
+        preact = contract(acts_ref[a], weight_ref[a], 0, 0)
+        size = jnp.abs(preact)
+        largest = jnp.maximum(jnp.max(size, axis=1, keepdims=True), TINY)
+        scale = (largest * ABOVE).astype(BF16).astype(F32)
+        code = jnp.exp(jnp.sqrt(size * (1.0 / scale)) * SPAN - SPAN / 2)
+        columns = pl.ds(a * feature_dev, feature_dev)
+        held_ref[:, columns] = jnp.where(preact < 0, -code, code).astype(BF16)
+        send(a, columns)
+        scales = jnp.where(lane == a, scale, scales)
+    columns = pl.ds(layers * feature_dev, LANES)
+    held_ref[:, columns] = scales.astype(BF16)
+    send(layers, columns)
+    finish(leaving)
 
 
 def encode(acts_t, enc_weight):
     layers, width, tokens = acts_t.shape
     feature_dev = enc_weight.shape[2]
+    shape = (tokens, layers * feature_dev + LANES)
+    anywhere = pl.BlockSpec(memory_space=pl.ANY)
     return pl.pallas_call(
         encode_kernel,
-        grid=(layers,),
-        in_specs=[
-            pl.BlockSpec((1, width, tokens), lambda a: (a, 0, 0)),
-            pl.BlockSpec((1, width, feature_dev), lambda a: (a, 0, 0)),
-        ],
-        out_specs=pl.BlockSpec((tokens, feature_dev), lambda a: (0, a)),
-        out_shape=jax.ShapeDtypeStruct((tokens, layers * feature_dev), F32),
+        in_specs=[anywhere, anywhere],
+        out_specs=anywhere,
+        out_shape=jax.ShapeDtypeStruct(shape, BF16),
+        scratch_shapes=[
+            pltpu.VMEM(acts_t.shape, BF16),
+            pltpu.VMEM(enc_weight.shape, BF16),
+            pltpu.VMEM(shape, BF16),
+            pltpu.SemaphoreType.DMA((layers,)),
+            pltpu.SemaphoreType.DMA((layers,)),
+            pltpu.SemaphoreType.DMA((layers + 1,)),
+        ],
         name="encode",
     )(acts_t, enc_weight)
+
+
+def features_kernel(arrived_hbm, bias_ref, own_ref, out_hbm, arrived_ref, in_sems, out_sems):
+    slots, rows, _ = arrived_ref.shape
+    layers, feature_dev = bias_ref.shape
+    arriving = start(
+        [pltpu.make_async_copy(arrived_hbm.at[k], arrived_ref.at[k], in_sems.at[k]) for k in range(slots)]
+    )
+    totals = [jnp.broadcast_to(bias_ref[a : a + 1, :], (rows, feature_dev)) for a in range(layers)]
+    for k in range(slots):
+        arriving[k].wait()
+        scales = arrived_ref[k, :, layers * feature_dev :].astype(F32)
+        for a in range(layers):
+            code = arrived_ref[k, :, a * feature_dev : (a + 1) * feature_dev].astype(F32)
+            root = jnp.log(jnp.abs(code)) * (1.0 / SPAN) + 0.5
+            size = root * root * scales[:, a : a + 1]
+            totals[a] = totals[a] + jnp.where(code < 0, -size, size)
+    for a in range(layers):
+        own_ref[:, a * feature_dev : (a + 1) * feature_dev] = jnp.maximum(totals[a], 0.0).astype(BF16)
+    finish(start([pltpu.make_async_copy(own_ref, out_hbm.at[k], out_sems.at[k]) for k in range(slots)]))
+
+
+def own_features_of(arrived, enc_bias):
+    slots, rows, _ = arrived.shape
+    own = (rows, enc_bias.size)
+    anywhere = pl.BlockSpec(memory_space=pl.ANY)
+    vmem = pl.BlockSpec(memory_space=pltpu.VMEM)
+    return pl.pallas_call(
+        features_kernel,
+        in_specs=[anywhere, vmem],
+        out_specs=[vmem, anywhere],
+        out_shape=[jax.ShapeDtypeStruct(own, BF16), jax.ShapeDtypeStruct((slots, *own), BF16)],
+        scratch_shapes=[
+            pltpu.VMEM(arrived.shape, BF16),
+            pltpu.SemaphoreType.DMA((slots,)),
+            pltpu.SemaphoreType.DMA((slots,)),
+        ],
+        name="own_features",
+    )(arrived, enc_bias)
+
+
+def delta_kernel(share, arrived_hbm, features_ref, mse_ref, out_hbm, arrived_ref, own_ref, in_sems, out_sems):
+    slots = arrived_ref.shape[0]
+    columns = features_ref.shape[1]
+    arriving = start(
+        [pltpu.make_async_copy(arrived_hbm.at[k], arrived_ref.at[k], in_sems.at[k]) for k in range(slots)]
+    )
+    arriving[0].wait()
+    total = arrived_ref[0].astype(F32)
+    for k in range(1, slots):
+        arriving[k].wait()
+        total = total + arrived_ref[k].astype(F32)
+    own_ref[...] = jnp.where(features_ref[...] > 0, total[:, :columns], 0.0).astype(BF16)
+    leaving = start([pltpu.make_async_copy(own_ref, out_hbm.at[k], out_sems.at[k]) for k in range(slots)])
+    mse_ref[0, 0] = jnp.sum(total[:1, columns:]) * share
+    finish(leaving)
+
+
+def own_delta_of(arrived, own_features, share):
+    slots = arrived.shape[0]
+    own = own_features.shape
+    anywhere = pl.BlockSpec(memory_space=pl.ANY)
+    return pl.pallas_call(
+        functools.partial(delta_kernel, share),
+        in_specs=[anywhere, pl.BlockSpec(memory_space=pltpu.VMEM)],
+        out_specs=[pl.BlockSpec(memory_space=pltpu.SMEM), anywhere],
+        out_shape=[jax.ShapeDtypeStruct((1, 1), F32), jax.ShapeDtypeStruct((slots, *own), BF16)],
+        scratch_shapes=[
+            pltpu.VMEM(arrived.shape, BF16),
+            pltpu.VMEM(own, BF16),
+            pltpu.SemaphoreType.DMA((slots,)),
+            pltpu.SemaphoreType.DMA((slots,)),
+        ],
+        name="own_delta",
+    )(arrived, own_features)
 
 
 def decode_kernel(layers, core_ref, features_ref, weight_ref, theirs_ref, mine_ref):
@@ -125,13 +254,13 @@
 def encoder_grad_kernel(acts_ref, delta_ref, grad_ref, bias_ref):
     delta = delta_ref[...]
     grad_ref[0] = contract(acts_ref[0], delta, 1, 0)
-    bias_ref[0] = jnp.sum(delta.astype(F32), axis=0, keepdims=True)
+    bias_ref[pl.ds(pl.program_id(0), 1), :] = jnp.sum(delta.astype(F32), axis=0, keepdims=True)
 
 
 def encoder_grad(acts_t, delta):
     layers, width, tokens = acts_t.shape
     feature_dev = delta.shape[1] // layers
-    grad, bias = pl.pallas_call(
+    return pl.pallas_call(
         encoder_grad_kernel,
         grid=(layers,),
         in_specs=[
@@ -140,16 +269,15 @@
         ],
         out_specs=[
             pl.BlockSpec((1, width, feature_dev), lambda a: (a, 0, 0)),
-            pl.BlockSpec((1, 1, feature_dev), lambda a: (a, 0, 0)),
+            pl.BlockSpec((layers, feature_dev), lambda a: (0, 0)),
         ],
         out_shape=[
             jax.ShapeDtypeStruct((layers, width, feature_dev), F32),
-            jax.ShapeDtypeStruct((layers, 1, feature_dev), F32),
+            jax.ShapeDtypeStruct((layers, feature_dev), F32),
         ],
         compiler_params=pltpu.CompilerParams(vmem_limit_bytes=VMEM),
         name="encoder_grad",
     )(acts_t, delta)
-    return grad, bias.reshape(layers, feature_dev)
 
 
 def local(acts_in, acts_out, enc_weight, enc_bias, dec_weight, dec_bias):
@@ -168,11 +296,10 @@
     def width(x, b):
         return x[:, b * width_dev : (b + 1) * width_dev]
 
-    preact = encode(acts_t, enc_weight)
-    arrived = exchange(preact.reshape(slots, tokens // slots, -1), SLOT)
-    own_preact = arrived.sum(axis=0) + enc_bias.reshape(1, -1)
-    own_features = jnp.maximum(own_preact, 0.0).astype(BF16)
-    features = sent_to_all(own_features, SLOT).reshape(tokens, -1)
+    sent = encode(acts_t, enc_weight)
+    arrived = exchange(sent.reshape(slots, tokens // slots, -1), SLOT)
+    own_features, copies = own_features_of(arrived, enc_bias)
+    features = exchange(copies, SLOT).reshape(tokens, -1)
 
     theirs, mine = decode(core.reshape(1), features, dec_t, layers)
     chip_sum = (mine + lax.ppermute(theirs, CORE, [(0, 1), (1, 0)]).astype(F32)).astype(BF16)
@@ -187,14 +314,13 @@
     error = lax.all_gather(half_error, CORE, axis=0, tiled=True)
 
     sent = upstream(error, dec_t, layers)
-    total = exchange(sent.reshape(slots, tokens // slots, -1), SLOT).astype(F32).sum(axis=0)
-    mse = (total[0, layers * feature_dev] + total[0, layers * feature_dev + 1]) / (layers * tokens * D)
-    own_delta = jnp.where(own_features > 0, total[:, : layers * feature_dev], 0.0).astype(BF16)
-    delta = sent_to_all(own_delta, SLOT).reshape(tokens, -1)
+    arrived = exchange(sent.reshape(slots, tokens // slots, -1), SLOT)
+    mse, copies = own_delta_of(arrived, own_features, 1.0 / (layers * tokens * D))
+    delta = exchange(copies, SLOT).reshape(tokens, -1)
 
     dec_grads = [contract(feats(features, a), width(error, b), 0, 0) for a, b in pair_list]
     enc_grad, bias_grad = encoder_grad(acts_t, delta)
-    return (enc_grad, bias_grad, jnp.stack(dec_grads), mse)
+    return (enc_grad, bias_grad, jnp.stack(dec_grads), mse.reshape(()))
 
 
 def solution(mesh):

time: 136 us -> 131 us (0.963)
  waiting for transfers between devices: 63.8 us -> 42.9 us
  blocking collectives: 17.4 us -> 36.6 us
  Pallas kernels: 8.44 us -> 16.5 us
  starting transfers between devices: 27.2 us -> 21.7 us
  between operations: 3.18 us -> 0.76 us
  local copies, waits for them, and re-layouts: 4.23 us -> 2.05 us
  other arithmetic: 3.53 us -> 1.85 us
    all_to_all x5 -> x4, waiting for transfers between devices: 62.4 us -> 41.4 us  [exchange(): return lax.all_to_all(tiles, axis, split_axis=0, concat_axis=0, tiled=True)]
    all_to_all x1 -> x2, blocking collectives: 15.3 us -> 34.5 us  [exchange(): return lax.all_to_all(tiles, axis, split_axis=0, concat_axis=0, tiled=True)]
    pallas_call x1 -> x3, Pallas kernels: 3.72 us -> 11.7 us  [the longest x1 4.08 us: own_features_of(): pl.pallas_call(features_kernel, in_specs=[anywhere, vmem], out_specs=[vme...]
    all_to_all x5 -> x4, starting transfers between devices: 27.1 us -> 21.6 us  [exchange(): return lax.all_to_all(tiles, axis, split_axis=0, concat_axis=0, tiled=True)]
    broadcast_in_dim x3 -> x1, local copies, waits for them, and re-layouts: 1.91 us -> 0.02 us  [sent_to_all(): jnp.broadcast_to(x[None], (lax.axis_size(axis), *x.shape))]
    reduce_sum x2 -> x0, other arithmetic: 1.62 us -> none  [the longest x1 1.51 us: local(): own_preact = arrived.sum(axis=0) + enc_bias.reshape(1, -1)]
  transfers between devices with their start and end apart: 6 -> 5, of which waited for: 6 -> 5; matrix products, arithmetic and copies ran while one was open for 7% -> 7% of each run, Pallas kernels for 0% -> 0%
where the time goes in v4:
time: 131 us; the launch traced here: 130 us
  waiting for transfers between devices  42.9 us (33%)
  blocking collectives  36.6 us (28%)
  starting transfers between devices  21.7 us (17%)
  Pallas kernels  16.5 us (13%)
  matrix products  7.18 us (5%)
  local copies, waits for them, and re-layouts  2.05 us (2%)
  other arithmetic  1.85 us (1%)
    all_to_all x4, waiting for transfers between devices, exchange(): return lax.all_to_all(tiles, axis, split_axis=0, concat_axis=0, tiled=True)  41.4 us
    all_to_all x2, blocking collectives, exchange(): return lax.all_to_all(tiles, axis, split_axis=0, concat_axis=0, tiled=True)  34.5 us
    all_to_all x4, starting transfers between devices, exchange(): return lax.all_to_all(tiles, axis, split_axis=0, concat_axis=0, tiled=True)  21.6 us
    dot_general x6, matrix products, contract(): lax.dot_general(x, y, (((x_dim,), (y_dim,)), ((), ())), preferred_element...  7.18 us
    pallas_call x1, Pallas kernels, own_features_of(): pl.pallas_call(features_kernel, in_specs=[anywhere, vmem], out_specs=[vme...  4.08 us
    pallas_call x1, Pallas kernels, encode(): pl.pallas_call(encode_kernel, in_specs=[anywhere, anywhere], out_specs=an...  3.93 us
    pallas_call x1, Pallas kernels, own_delta_of(): pl.pallas_call(functools.partial(delta_kernel, share), in_specs=[anywhere...  3.74 us
  transfers between devices with their start and end apart: 5, of which 5 were waited for; matrix products, arithmetic and copies ran while one was open for 7% of the time, Pallas kernels for 0%

profile of v4, /device:TPU:32, one launch (start us, length us, event | category | flops | bytes accessed | tf_op | source)
XLA Modules:
  0.0 129.5 jit_solution(17332801314598316141)
XLA Ops:
  0.6 0.0 copy-start
  0.6 3.9 %encode.1 = bf16[256,1664]{1,0:T(8,128)(2,1)} custom-call(bf16[3,288,256]{2,1,0:T(8,128)(2,1)} %bitcast.49, bf16[3,288,512]{2,1,0:T(8,128)(2,1)} %weight_hbm.1), custom_call_target="tpu_custom_call" | custom-call | tf_op jit(solution)/shard_map/encode/pallas_call | solution.py:95
  4.6 19.2 %all_to_all.30.arrived_hbm = bf16[8,32,1664]{2,1,0:T(8,128)(2,1)} all-to-all(bf16[8,32,1664]{2,1,0:T(8,128)(2,1)} %bitcast.51), channel_id=1, replica_groups=mesh['slot_0'=2,'slot_1'=4,'feat_0'=2,'feat_1'=8,'feat_2'=2] {'slot_0','..., dimensions={0} | all-to-all | bytes 1703936 | tf_op jit(solution)/shard_map/all_to_all | solution.py:26
  23.8 4.1 %own_features.1 = (bf16[32,1536]{1,0:T(8,128)(2,1)}, bf16[8,32,1536]{2,1,0:T(8,128)(2,1)}) custom-call(bf16[8,32,1664]{2,1,0:T(8,128)(2,1)} %all_to_all.30.arrived_hbm, f32[3,512]{1,0:T(4,128)} %bias_ref.1), custom_call_target="tpu_custom_call" | custom-call | tf_op jit(solution)/shard_map/own_features/pallas_call | solution.py:137
  27.8 0.0 copy-start.4
  27.9 3.6 %all-to-all-start.1 = ((bf16[8,32,1536]{2,1,0:T(8,128)(2,1)}), bf16[8,32,1536]{2,1,0:T(8,128)(2,1)S(1)}, u32[]{:S(2)}, u32[]{:S(2)}) async-start(bf16[8,32,1536]{2,1,0:T(8,128)(2,1)} %get-tuple-element.12), calls=%async_computation.1 | async-start | bytes 1572864 | tf_op jit(solution)/shard_map/all_to_all | solution.py:26
  31.4 11.5 %all-to-all-done.1 = bf16[8,32,1536]{2,1,0:T(8,128)(2,1)S(1)} async-done(((bf16[8,32,1536]{2,1,0:T(8,128)(2,1)}), bf16[8,32,1536]{2,1,0:T(8,128)(2,1)S(1)}, u32[]{:S(2)}, u32[]{:S(2)}) %all-to-all-start.1) | async-done | bytes 786464 | tf_op jit(solution)/shard_map/all_to_all | solution.py:26
  43.0 0.0 copy-done
  43.0 1.5 %decode.1 = (bf16[128,864]{1,0:T(8,128)(2,1)S(1)}, f32[128,864]{1,0:T(8,128)S(1)}) custom-call(s32[1]{0:T(128)} %bitcast.1.core_ref, bf16[256,1536]{1,0:T(8,128)(2,1)S(1)} %bitcast.38, bf16[6,288,512]{2,1,0:T(8,128)(2,1)S(1)} %bitcast.45), custom_call_target="tpu_custom_call" | custom-call | tf_op jit(solution)/shard_map/decode/pallas_call | solution.py:211
  44.5 0.1 collective-permute-start
  44.6 1.5 %collective-permute-done = bf16[128,864]{1,0:T(8,128)(2,1)S(1)} collective-permute-done((bf16[128,864]{1,0:T(8,128)(2,1)S(1)}, bf16[128,864]{1,0:T(8,128)(2,1)S(1)}, u32[]{:S(2)}, u32[]{:S(2)}) %collective-permute-start) | collective-permute-done | bytes 221216 | tf_op jit(solution)/shard_map/ppermute | solution.py:305
  46.1 0.7 fusion.9
  46.9 10.9 %all-to-all-start.2 = ((bf16[16,8,864]{2,1,0:T(8,128)(2,1)}), bf16[16,8,864]{2,1,0:T(8,128)(2,1)S(1)}, u32[]{:S(2)}, u32[]{:S(2)}) async-start(bf16[16,8,864]{2,1,0:T(8,128)(2,1)} %fusion.9), calls=%async_computation.2 | async-start | bytes 458752 | tf_op jit(solution)/shard_map/all_to_all | solution.py:26
  57.8 1.1 dynamic-slice_convert_fusion
  58.8 0.1 copy.13
  59.0 0.0 copy-done.4
  59.0 0.1 add.27
  59.1 10.0 %all-to-all-done.2 = bf16[16,8,864]{2,1,0:T(8,128)(2,1)S(1)} async-done(((bf16[16,8,864]{2,1,0:T(8,128)(2,1)}), bf16[16,8,864]{2,1,0:T(8,128)(2,1)S(1)}, u32[]{:S(2)}, u32[]{:S(2)}) %all-to-all-start.2) | async-done | bytes 221216 | tf_op jit(solution)/shard_map/all_to_all | solution.py:26
  69.1 15.3 %all_to_all.31 = bf16[16,8,864]{2,1,0:T(8,128)(2,1)S(1)} all-to-all(bf16[16,8,864]{2,1,0:T(8,128)(2,1)S(1)} %broadcast_in_dim.2), channel_id=1, replica_groups=mesh['slot_0'=2,'slot_1'=4,'feat_0'=2,'feat_1'=8,'feat_2'=2] {'feat_0','..., dimensions={0} | all-to-all | bytes 442368 | tf_op jit(solution)/shard_map/all_to_all | solution.py:26
  84.4 2.1 %all_gather.3.error_ref = bf16[256,864]{1,0:T(8,128)(2,1)S(1)} all-gather(bf16[128,864]{1,0:T(8,128)(2,1)S(1)} %bitcast.53), channel_id=1, replica_groups=mesh['slot_0'=2,'slot_1'=4,'feat_0'=2,'feat_1'=8,'feat_2'=2] {'feat_2'}, dimensions={0}, use_global_device_ids=true | all-gather | bytes 663552 | tf_op jit(solution)/shard_map/all_gather | solution.py:314
  86.5 1.0 upstream.1
  87.5 0.0 copy-start.1
  87.6 0.9 copy-done.1
  88.4 3.6 %all-to-all-start.4 = ((bf16[8,32,1664]{2,1,0:T(8,128)(2,1)}), bf16[8,32,1664]{2,1,0:T(8,128)(2,1)S(1)}, u32[]{:S(2)}, u32[]{:S(2)}) async-start(bf16[8,32,1664]{2,1,0:T(8,128)(2,1)} %bitcast.47), calls=%async_computation.4 | async-start | bytes 1703936 | tf_op jit(solution)/shard_map/all_to_all | solution.py:26
  92.0 1.1 fusion.5
  93.1 1.2 fusion.4
  94.3 0.0 copy-start.2
  94.3 1.2 fusion.3
  95.5 10.6 %all-to-all-done.4.arrived_hbm = bf16[8,32,1664]{2,1,0:T(8,128)(2,1)S(1)} async-done(((bf16[8,32,1664]{2,1,0:T(8,128)(2,1)}), bf16[8,32,1664]{2,1,0:T(8,128)(2,1)S(1)}, u32[]{:S(2)}, u32[]{:S(2)}) %all-to-all-start.4) | async-done | bytes 852000 | tf_op jit(solution)/shard_map/all_to_all | solution.py:26
  106.1 0.0 copy-start.3
  106.1 0.9 copy-done.3
  107.0 3.7 %own_delta.1 = (f32[1,1]{1,0:T(1,128)}, bf16[8,32,1536]{2,1,0:T(8,128)(2,1)}) custom-call(bf16[8,32,1664]{2,1,0:T(8,128)(2,1)} %copy-done.3, bf16[32,1536]{1,0:T(8,128)(2,1)} %get-tuple-element.15.features_ref), custom_call_target="tpu_custom_call" | custom-call | tf_op jit(solution)/shard_map/own_delta/pallas_call | solution.py:172
  110.8 3.6 %all-to-all-start.5 = ((bf16[8,32,1536]{2,1,0:T(8,128)(2,1)}), bf16[8,32,1536]{2,1,0:T(8,128)(2,1)S(1)}, u32[]{:S(2)}, u32[]{:S(2)}) async-start(bf16[8,32,1536]{2,1,0:T(8,128)(2,1)} %get-tuple-element.16), calls=%async_computation.5 | async-start | bytes 1572864 | tf_op jit(solution)/shard_map/all_to_all | solution.py:26
  114.3 1.2 fusion.2
  115.5 1.2 fusion.1
  116.8 1.2 fusion
  118.0 9.4 %all-to-all-done.5 = bf16[8,32,1536]{2,1,0:T(8,128)(2,1)S(1)} async-done(((bf16[8,32,1536]{2,1,0:T(8,128)(2,1)}), bf16[8,32,1536]{2,1,0:T(8,128)(2,1)S(1)}, u32[]{:S(2)}, u32[]{:S(2)}) %all-to-all-start.5) | async-done | bytes 786464 | tf_op jit(solution)/shard_map/all_to_all | solution.py:26
  127.4 0.0 copy-done.2
  127.4 2.2 %encoder_grad.1 = (f32[3,288,512]{2,1,0:T(8,128)}, f32[3,512]{1,0:T(4,128)}) custom-call(bf16[3,288,256]{2,1,0:T(8,128)(2,1)S(1)} %bitcast.50, bf16[256,1536]{1,0:T(8,128)(2,1)S(1)} %bitcast.48), custom_call_target="tpu_custom_call" | custom-call | tf_op jit(solution)/shard_map/encoder_grad/pallas_call | solution.py:263
  (3 shorter events, 0.1 us)
Async XLA Ops:
  0.6 42.4 %copy-start = (bf16[6,512,288]{1,2,0:T(8,128)(2,1)S(1)}, bf16[6,512,288]{1,2,0:T(8,128)(2,1)}, u32[]{:S(2)}) copy-start(bf16[6,512,288]{1,2,0:T(8,128)(2,1)} %param.10) | copy-start | bytes 5308420
  27.8 31.1 %copy-start.4 = (f32[3,288]{1,0:T(4,128)S(1)}, f32[3,288]{1,0:T(4,128)}, u32[]{:S(2)}) copy-start(f32[3,288]{1,0:T(4,128)} %param.11) | copy-start | bytes 10372
  27.9 15.1 %all-to-all-start.1 = ((bf16[8,32,1536]{2,1,0:T(8,128)(2,1)}), bf16[8,32,1536]{2,1,0:T(8,128)(2,1)S(1)}, u32[]{:S(2)}, u32[]{:S(2)}) async-start(bf16[8,32,1536]{2,1,0:T(8,128)(2,1)} %get-tuple-element.12), calls=%async_computation.1 | async-start | bytes 1572864 | tf_op jit(solution)/shard_map/all_to_all | solution.py:26
  44.5 1.6 %collective-permute-start = (bf16[128,864]{1,0:T(8,128)(2,1)S(1)}, bf16[128,864]{1,0:T(8,128)(2,1)S(1)}, u32[]{:S(2)}, u32[]{:S(2)}) collective-permute-start(bf16[128,864]{1,0:T(8,128)(2,1)S(1)} %get-tuple-element.14), channel_id=1, source_target_pairs={{0,1},{1,0},{2,3},{3,2},{4,5},{5,4},{6,7},{7,6},{8,9},{9,8},{10,11... | collective-permute-start | bytes 663560 | tf_op jit(solution)/shard_map/ppermute | solution.py:305
  46.9 22.2 %all-to-all-start.2 = ((bf16[16,8,864]{2,1,0:T(8,128)(2,1)}), bf16[16,8,864]{2,1,0:T(8,128)(2,1)S(1)}, u32[]{:S(2)}, u32[]{:S(2)}) async-start(bf16[16,8,864]{2,1,0:T(8,128)(2,1)} %fusion.9), calls=%async_computation.2 | async-start | bytes 458752 | tf_op jit(solution)/shard_map/all_to_all | solution.py:26
  87.5 0.9 copy-start.1
  88.4 17.7 %all-to-all-start.4 = ((bf16[8,32,1664]{2,1,0:T(8,128)(2,1)}), bf16[8,32,1664]{2,1,0:T(8,128)(2,1)S(1)}, u32[]{:S(2)}, u32[]{:S(2)}) async-start(bf16[8,32,1664]{2,1,0:T(8,128)(2,1)} %bitcast.47), calls=%async_computation.4 | async-start | bytes 1703936 | tf_op jit(solution)/shard_map/all_to_all | solution.py:26
  94.3 33.0 %copy-start.2 = (bf16[3,256,288]{1,2,0:T(8,128)(2,1)S(1)}, bf16[3,256,288]{1,2,0:T(8,128)(2,1)}, u32[]{:S(2)}) copy-start(bf16[3,256,288]{1,2,0:T(8,128)(2,1)} %param.6) | copy-start | bytes 1327108
  106.1 0.9 copy-start.3
  110.8 16.6 %all-to-all-start.5 = ((bf16[8,32,1536]{2,1,0:T(8,128)(2,1)}), bf16[8,32,1536]{2,1,0:T(8,128)(2,1)S(1)}, u32[]{:S(2)}, u32[]{:S(2)}) async-start(bf16[8,32,1536]{2,1,0:T(8,128)(2,1)} %get-tuple-element.16), calls=%async_computation.5 | async-start | bytes 1572864 | tf_op jit(solution)/shard_map/all_to_all | solution.py:26

commit v5 on v2

v5 whole, which is shorter than its diff:
```python
import functools

import jax
import jax.numpy as jnp
from jax import lax
from jax.experimental import pallas as pl
from jax.experimental.pallas import tpu as pltpu
from jax.sharding import Mesh
from jax.sharding import PartitionSpec as P

D = 2304
SLOT = ("slot_0", "slot_1")
FEAT = ("feat_0", "feat_1", "feat_2")
CHIPS = ("feat_0", "feat_1")
CORE = "feat_2"
LANES = 128
VMEM = 16 * 2**20
OCTAVES = 250.0
ABOVE = 1.0078125
TINY = 1e-30
LEAST = 1e-12
F32 = jnp.float32
BF16 = jnp.bfloat16


def exchange(tiles, axis):
    return lax.all_to_all(tiles, axis, split_axis=0, concat_axis=0, tiled=True)


def sent_to_all(x, axis):
    return exchange(jnp.broadcast_to(x[None], (lax.axis_size(axis), *x.shape)), axis)


def pair_number(a, b, layers):
    return a * layers - a * (a - 1) // 2 + (b - a)


def contract(x, y, x_dim, y_dim):
    return lax.dot_general(x, y, (((x_dim,), (y_dim,)), ((), ())), preferred_element_type=F32)


def encode_kernel(acts_ref, weight_ref, out_ref):
    layers = acts_ref.shape[0]
    tokens = out_ref.shape[0]
    feature_dev = weight_ref.shape[2]
    lane = lax.broadcasted_iota(jnp.int32, (tokens, LANES), 1)
    scales = jnp.zeros((tokens, LANES), F32)
    for a in range(layers):
        preact = contract(acts_ref[a], weight_ref[a], 0, 0)
        size = jnp.abs(preact)
        largest = jnp.maximum(jnp.max(size, axis=1, keepdims=True), TINY)
        scale = (largest * ABOVE).astype(BF16).astype(F32)
        square = jnp.maximum(size * (1.0 / scale), LEAST)
        code = jnp.exp2(square * lax.rsqrt(square) * OCTAVES - OCTAVES / 2)
        out_ref[:, a * feature_dev : (a + 1) * feature_dev] = jnp.where(preact < 0, -code, code).astype(BF16)
        scales = jnp.where(lane == a, scale, scales)
    out_ref[:, layers * feature_dev :] = scales.astype(BF16)


def on_chip(kernel, name, args, out_shape, scratch_shapes=()):
    vmem = pl.BlockSpec(memory_space=pltpu.VMEM)
    smem = pl.BlockSpec(memory_space=pltpu.SMEM)
    return pl.pallas_call(
        kernel,
        in_specs=[smem if arg.dtype == jnp.int32 else vmem for arg in args],
        out_specs=jax.tree.map(lambda _: vmem, out_shape),
        out_shape=out_shape,
        scratch_shapes=scratch_shapes,
        compiler_params=pltpu.CompilerParams(vmem_limit_bytes=VMEM),
        name=name,
    )(*args)


def encode(acts_t, enc_weight):
    layers, _, tokens = acts_t.shape
    shape = (tokens, layers * enc_weight.shape[2] + LANES)
    return on_chip(encode_kernel, "encode", (acts_t, enc_weight), jax.ShapeDtypeStruct(shape, BF16))


def features_kernel(arrived_ref, bias_ref, own_ref):
    slots, rows, _ = arrived_ref.shape
    layers, feature_dev = bias_ref.shape
    totals = [jnp.broadcast_to(bias_ref[a : a + 1, :], (rows, feature_dev)) for a in range(layers)]
    for k in range(slots):
        scales = arrived_ref[k, :, layers * feature_dev :].astype(F32)
        for a in range(layers):
            code = arrived_ref[k, :, a * feature_dev : (a + 1) * feature_dev].astype(F32)
            root = jnp.log2(jnp.abs(code)) * (1.0 / OCTAVES) + 0.5
            size = root * root * scales[:, a : a + 1]
            totals[a] = totals[a] + jnp.where(code < 0, -size, size)
    for a in range(layers):
        own_ref[:, a * feature_dev : (a + 1) * feature_dev] = jnp.maximum(totals[a], 0.0).astype(BF16)


def own_features_of(arrived, enc_bias):
    shape = (arrived.shape[1], enc_bias.size)
    return on_chip(
        features_kernel, "own_features", (arrived, enc_bias), jax.ShapeDtypeStruct(shape, BF16)
    )


def decode_kernel(layers, core_ref, features_ref, weight_ref, theirs_ref, mine_ref, held_ref):
    width, feature_dev = weight_ref.shape[1:]
    half = theirs_ref.shape[0]
    core = core_ref[0]
    for b in range(layers):
        total = None
        for a in range(b + 1):
            term = contract(
                features_ref[:, a * feature_dev : (a + 1) * feature_dev],
                weight_ref[pair_number(a, b, layers)],
                1,
                1,
            )
            total = term if total is None else total + term
        held_ref[:, b * width : (b + 1) * width] = total
    for ref, side in ((theirs_ref, 1 - core), (mine_ref, core)):
        ref[...] = held_ref[pl.ds(pl.multiple_of(side * half, half), half), :].astype(ref.dtype)


def decode(core, features, dec_t, layers):
    tokens = features.shape[0]
    columns = layers * dec_t.shape[1]
    return on_chip(
        functools.partial(decode_kernel, layers),
        "decode",
        (core, features, dec_t),
        [jax.ShapeDtypeStruct((tokens // 2, columns), kind) for kind in (BF16, F32)],
        [pltpu.VMEM((tokens, columns), F32)],
    )


def error_kernel(offset_ref, arrived_ref, acts_ref, bias_ref, out_ref):
    chips, rows, _ = arrived_ref.shape
    layers, width, tokens = acts_ref.shape
    row = lax.broadcasted_iota(jnp.int32, (rows, tokens), 0)
    token = lax.broadcasted_iota(jnp.int32, (rows, tokens), 1)
    mine = jnp.where(token == row + offset_ref[0], 1.0, 0.0).astype(BF16)
    total = arrived_ref[0].astype(F32)
    for k in range(1, chips):
        total = total + arrived_ref[k].astype(F32)
    for b in range(layers):
        columns = slice(b * width, (b + 1) * width)
        target = contract(mine, acts_ref[b], 1, 1)
        out_ref[:, columns] = (total[:, columns] + bias_ref[b : b + 1, :] - target).astype(BF16)


def own_error_of(offset, arrived, acts_out_t, dec_bias):
    return on_chip(
        error_kernel,
        "own_error",
        (offset, arrived, acts_out_t, dec_bias),
        jax.ShapeDtypeStruct(arrived.shape[1:], BF16),
    )


def upstream_kernel(layers, error_ref, weight_ref, out_ref):
    tokens = error_ref.shape[0]
    width, feature_dev = weight_ref.shape[1:]
    for a in range(layers):
        total = None
        for b in range(a, layers):
            term = contract(
                error_ref[:, b * width : (b + 1) * width], weight_ref[pair_number(a, b, layers)], 1, 0
            )
            total = term if total is None else total + term
        out_ref[:, a * feature_dev : (a + 1) * feature_dev] = total.astype(BF16)
    wide = error_ref[...].astype(F32)
    squared = jnp.sum(wide * wide)
    coarse = squared.astype(BF16).astype(F32)
    fine = squared - coarse
    lane = lax.broadcasted_iota(jnp.int32, (tokens, LANES), 1)
    extra = jnp.where(lane == 0, coarse, jnp.where(lane == 1, fine, 0.0))
    out_ref[:, layers * feature_dev :] = extra.astype(BF16)


def upstream(error, dec_t, layers):
    shape = (error.shape[0], layers * dec_t.shape[2] + LANES)
    return on_chip(
        functools.partial(upstream_kernel, layers), "upstream", (error, dec_t), jax.ShapeDtypeStruct(shape, BF16)
    )


def encoder_grad_kernel(acts_ref, delta_ref, grad_ref, bias_ref):
    delta = delta_ref[...]
    grad_ref[0] = contract(acts_ref[0], delta, 1, 0)
    bias_ref[pl.ds(pl.program_id(0), 1), :] = jnp.sum(delta.astype(F32), axis=0, keepdims=True)


def encoder_grad(acts_t, delta):
    layers, width, tokens = acts_t.shape
    feature_dev = delta.shape[1] // layers
    return pl.pallas_call(
        encoder_grad_kernel,
        grid=(layers,),
        in_specs=[
            pl.BlockSpec((1, width, tokens), lambda a: (a, 0, 0)),
            pl.BlockSpec((tokens, feature_dev), lambda a: (0, a)),
        ],
        out_specs=[
            pl.BlockSpec((1, width, feature_dev), lambda a: (a, 0, 0)),
            pl.BlockSpec((layers, feature_dev), lambda a: (0, 0)),
        ],
        out_shape=[
            jax.ShapeDtypeStruct((layers, width, feature_dev), F32),
            jax.ShapeDtypeStruct((layers, feature_dev), F32),
        ],
        compiler_params=pltpu.CompilerParams(vmem_limit_bytes=VMEM),
        name="encoder_grad",
    )(acts_t, delta)


def local(acts_in, acts_out, enc_weight, enc_bias, dec_weight, dec_bias):
    layers, tokens, width_dev = acts_in.shape
    feature_dev = enc_weight.shape[2]
    pair_list = [(a, b) for a in range(layers) for b in range(a, layers)]
    slots = lax.axis_size(SLOT)
    chips = lax.axis_size(CHIPS)
    core = lax.axis_index(CORE)
    acts_t = jnp.transpose(acts_in, (0, 2, 1))
    dec_t = jnp.transpose(dec_weight, (0, 2, 1))

    def feats(x, a):
        return x[:, a * feature_dev : (a + 1) * feature_dev]

    def width(x, b):
        return x[:, b * width_dev : (b + 1) * width_dev]

    half = tokens // 2
    portion = half // chips
    core = core.reshape(1)
    offset = core * half + lax.axis_index(CHIPS) * portion
    acts_t, core, offset = lax.optimization_barrier((acts_t, core, offset))

    sent = encode(acts_t, enc_weight)
    arrived = exchange(sent.reshape(slots, tokens // slots, -1), SLOT)
    own_features = own_features_of(arrived, enc_bias)
    features = sent_to_all(own_features, SLOT).reshape(tokens, -1)

    theirs, mine = decode(core, features, dec_t, layers)
    chip_sum = (mine + lax.ppermute(theirs, CORE, [(0, 1), (1, 0)]).astype(F32)).astype(BF16)
    arrived = exchange(chip_sum.reshape(chips, portion, -1), CHIPS)
    own_error = own_error_of(offset, arrived, jnp.transpose(acts_out, (0, 2, 1)), dec_bias)
    half_error = sent_to_all(own_error, CHIPS).reshape(half, -1)
    error = lax.all_gather(half_error, CORE, axis=0, tiled=True)

    sent = upstream(error, dec_t, layers)
    total = exchange(sent.reshape(slots, tokens // slots, -1), SLOT).astype(F32).sum(axis=0)
    mse = (total[0, layers * feature_dev] + total[0, layers * feature_dev + 1]) / (layers * tokens * D)
    own_delta = jnp.where(own_features > 0, total[:, : layers * feature_dev], 0.0).astype(BF16)
    delta = sent_to_all(own_delta, SLOT).reshape(tokens, -1)

    dec_grads = [contract(feats(features, a), width(error, b), 0, 0) for a, b in pair_list]
    enc_grad, bias_grad = encoder_grad(acts_t, delta)
    return (enc_grad, bias_grad, jnp.stack(dec_grads), mse)


def solution(mesh):
    split = Mesh(mesh.devices.reshape(2, 4, 2, 8, 2), (*SLOT, *FEAT))
    in_specs = (
        P(None, None, SLOT),
        P(None, None, SLOT),
        P(None, SLOT, FEAT),
        P(None, FEAT),
        P(None, FEAT, SLOT),
        P(None, SLOT),
    )
    out_specs = (P(None, SLOT, FEAT), P(None, FEAT), P(None, FEAT, SLOT), P())
    return jax.shard_map(local, mesh=split, in_specs=in_specs, out_specs=out_specs, check_vma=False)
```

time: 136 us -> 122 us (0.90)
  blocking collectives: 17.4 us -> 72.3 us
  waiting for transfers between devices: 63.8 us -> 19.5 us
  starting transfers between devices: 27.2 us -> 7.19 us
  other arithmetic: 3.53 us -> 0.18 us
    all_to_all x1 -> x4, blocking collectives: 15.3 us -> 70.2 us  [exchange(): return lax.all_to_all(tiles, axis, split_axis=0, concat_axis=0, tiled=True)]
    all_to_all x5 -> x2, waiting for transfers between devices: 62.4 us -> 18.1 us  [exchange(): return lax.all_to_all(tiles, axis, split_axis=0, concat_axis=0, tiled=True)]
    all_to_all x5 -> x2, starting transfers between devices: 27.1 us -> 7.1 us  [exchange(): return lax.all_to_all(tiles, axis, split_axis=0, concat_axis=0, tiled=True)]
    reduce_sum x2 -> x0, other arithmetic: 1.55 us -> none  [the longest x1 1.51 us: local(): own_preact = arrived.sum(axis=0) + enc_bias.reshape(1, -1)]
    pallas_call x3 -> x5, Pallas kernels: 6.28 us -> 5.16 us  [on_chip(): pl.pallas_call(kernel, in_specs=[smem if arg.dtype == jnp.int32 else vmem...]
  transfers between devices with their start and end apart: 6 -> 3, of which waited for: 6 -> 3; matrix products, arithmetic and copies ran while one was open for 7% -> 6% of each run, Pallas kernels for 0% -> 0%
where the time goes in v5:
time: 122 us; the launch traced here: 121 us
  blocking collectives  72.3 us (59%)
  waiting for transfers between devices  19.5 us (16%)
  Pallas kernels  7.33 us (6%)
  starting transfers between devices  7.19 us (6%)
  matrix products  7.18 us (6%)
  local copies, waits for them, and re-layouts  3.8 us (3%)
  between operations  3.18 us (3%)
    all_to_all x4, blocking collectives, exchange(): return lax.all_to_all(tiles, axis, split_axis=0, concat_axis=0, tiled=True)  70.2 us
    all_to_all x2, waiting for transfers between devices, exchange(): return lax.all_to_all(tiles, axis, split_axis=0, concat_axis=0, tiled=True)  18.1 us
    dot_general x6, matrix products, contract(): lax.dot_general(x, y, (((x_dim,), (y_dim,)), ((), ())), preferred_element...  7.18 us
    all_to_all x2, starting transfers between devices, exchange(): return lax.all_to_all(tiles, axis, split_axis=0, concat_axis=0, tiled=True)  7.1 us
    pallas_call x5, Pallas kernels, on_chip(): pl.pallas_call(kernel, in_specs=[smem if arg.dtype == jnp.int32 else vmem...  5.16 us
  transfers between devices with their start and end apart: 3, of which 3 were waited for; matrix products, arithmetic and copies ran while one was open for 6% of the time, Pallas kernels for 0%

profile of v5, /device:TPU:32, one launch (start us, length us, event | category | flops | bytes accessed | tf_op | source)
XLA Modules:
  0.0 120.7 jit_solution(15873751091200398208)
XLA Ops:
  0.6 0.0 copy-start.5
  0.7 0.0 copy-start.1
  0.7 1.0 copy-done.1
  1.7 0.0 copy-start.3
  1.7 1.2 copy-done.3
  2.8 0.0 copy-start
  2.8 1.2 encode.1
  4.0 18.9 %all_to_all.30.arrived_ref = bf16[8,32,1664]{2,1,0:T(8,128)(2,1)S(1)} all-to-all(bf16[8,32,1664]{2,1,0:T(8,128)(2,1)S(1)} %bitcast.46), channel_id=1, replica_groups=mesh['slot_0'=2,'slot_1'=4,'feat_0'=2,'feat_1'=8,'feat_2'=2] {'slot_0','..., dimensions={0} | all-to-all | bytes 1703936 | tf_op jit(solution)/shard_map/all_to_all | solution.py:27
  22.9 0.0 copy-done.5
  22.9 0.0 copy-start.4
  22.9 0.0 copy-start.6
  22.9 0.7 own_features.1
  23.5 0.1 broadcast_in_dim.10
  23.6 14.0 %all_to_all.31 = bf16[8,32,1536]{2,1,0:T(8,128)(2,1)S(1)} all-to-all(bf16[8,32,1536]{2,1,0:T(8,128)(2,1)S(1)} %broadcast_in_dim.10), channel_id=1, replica_groups=mesh['slot_0'=2,'slot_1'=4,'feat_0'=2,'feat_1'=8,'feat_2'=2] {'slot_0','..., dimensions={0} | all-to-all | bytes 1572864 | tf_op jit(solution)/shard_map/all_to_all | solution.py:27
  37.6 0.0 copy-done
  37.6 1.1 decode.1
  38.8 0.1 collective-permute-start
  38.9 1.5 %collective-permute-done = bf16[128,864]{1,0:T(8,128)(2,1)S(1)} collective-permute-done((bf16[128,864]{1,0:T(8,128)(2,1)S(1)}, bf16[128,864]{1,0:T(8,128)(2,1)S(1)}, u32[]{:S(2)}, u32[]{:S(2)}) %collective-permute-start) | collective-permute-done | bytes 221216 | tf_op jit(solution)/shard_map/ppermute | solution.py:241
  40.4 22.0 %all_to_all.32.arrived_ref = bf16[16,8,864]{2,1,0:T(8,128)(2,1)S(1)} all-to-all(bf16[16,8,864]{2,1,0:T(8,128)(2,1)S(1)} %fusion.9), channel_id=1, replica_groups=mesh['slot_0'=2,'slot_1'=4,'feat_0'=2,'feat_1'=8,'feat_2'=2] {'feat_0','..., dimensions={0} | all-to-all | bytes 442368 | tf_op jit(solution)/shard_map/all_to_all | solution.py:27
  62.3 0.0 copy-done.4
  62.3 0.0 copy-done.6
  62.3 0.3 own_error.1
  62.7 15.3 %all_to_all.33 = bf16[16,8,864]{2,1,0:T(8,128)(2,1)S(1)} all-to-all(bf16[16,8,864]{2,1,0:T(8,128)(2,1)S(1)} %broadcast_in_dim.11), channel_id=1, replica_groups=mesh['slot_0'=2,'slot_1'=4,'feat_0'=2,'feat_1'=8,'feat_2'=2] {'feat_0','..., dimensions={0} | all-to-all | bytes 442368 | tf_op jit(solution)/shard_map/all_to_all | solution.py:27
  78.0 2.1 %all_gather.3.error_ref = bf16[256,864]{1,0:T(8,128)(2,1)S(1)} all-gather(bf16[128,864]{1,0:T(8,128)(2,1)S(1)} %bitcast.51), channel_id=1, replica_groups=mesh['slot_0'=2,'slot_1'=4,'feat_0'=2,'feat_1'=8,'feat_2'=2] {'feat_2'}, dimensions={0}, use_global_device_ids=true | all-gather | bytes 663552 | tf_op jit(solution)/shard_map/all_gather | solution.py:245
  80.1 1.9 %upstream.1 = bf16[256,1664]{1,0:T(8,128)(2,1)} custom-call(bf16[256,864]{1,0:T(8,128)(2,1)S(1)} %all_gather.3.error_ref, bf16[6,288,512]{2,1,0:T(8,128)(2,1)S(1)} %bitcast.45), custom_call_target="tpu_custom_call" | custom-call | tf_op jit(solution)/shard_map/upstream/pallas_call | solution.py:63
  82.0 3.6 %all-to-all-start.4 = ((bf16[8,32,1664]{2,1,0:T(8,128)(2,1)}), bf16[8,32,1664]{2,1,0:T(8,128)(2,1)S(1)}, u32[]{:S(2)}, u32[]{:S(2)}) async-start(bf16[8,32,1664]{2,1,0:T(8,128)(2,1)} %bitcast.9), calls=%async_computation.4 | async-start | bytes 1703936 | tf_op jit(solution)/shard_map/all_to_all | solution.py:27
  85.6 1.1 fusion.5
  86.7 1.2 %fusion.4 = f32[6,512,288]{1,2,0:T(8,128)} fusion(f32[6,512,288]{1,2,0:T(8,128)} %fusion.5, bf16[256,1536]{1,0:T(8,128)(2,1)S(1)} %bitcast.39, bf16[256,864]{1,0:T(8,128)(2,1)S(1)} %all_gather.3.error_ref), kind=kOutput, calls=%fused_computation.10 | convolution fusion | flops 75497472 | bytes 1048576 | tf_op jit(solution)/shard_map/dot_general | solution.py:39
  87.9 1.2 %fusion.3 = f32[6,512,288]{1,2,0:T(8,128)} fusion(f32[6,512,288]{1,2,0:T(8,128)} %fusion.4, bf16[256,1536]{1,0:T(8,128)(2,1)S(1)} %bitcast.40, bf16[256,864]{1,0:T(8,128)(2,1)S(1)} %all_gather.3.error_ref), kind=kOutput, calls=%fused_computation.8 | convolution fusion | flops 75497472 | bytes 1048576 | tf_op jit(solution)/shard_map/dot_general | solution.py:39
  89.1 0.0 copy-start.2
  89.1 10.6 %all-to-all-done.4 = bf16[8,32,1664]{2,1,0:T(8,128)(2,1)S(1)} async-done(((bf16[8,32,1664]{2,1,0:T(8,128)(2,1)}), bf16[8,32,1664]{2,1,0:T(8,128)(2,1)S(1)}, u32[]{:S(2)}, u32[]{:S(2)}) %all-to-all-start.4) | async-done | bytes 852000 | tf_op jit(solution)/shard_map/all_to_all | solution.py:27
  99.7 0.1 convert_reduce_fusion
  99.9 0.9 broadcast_in_dim.13
  100.8 3.5 %all-to-all-start.5 = ((bf16[8,32,1536]{2,1,0:T(8,128)(2,1)}), bf16[8,32,1536]{2,1,0:T(8,128)(2,1)S(1)}, u32[]{:S(2)}, u32[]{:S(2)}) async-start(bf16[8,32,1536]{2,1,0:T(8,128)(2,1)} %broadcast_in_dim.13), calls=%async_computation.5 | async-start | bytes 1572864 | tf_op jit(solution)/shard_map/all_to_all | solution.py:27
  104.4 1.2 %fusion.2 = f32[6,512,288]{1,2,0:T(8,128)} fusion(f32[6,512,288]{1,2,0:T(8,128)} %fusion.3, bf16[256,1536]{1,0:T(8,128)(2,1)S(1)} %bitcast.41, bf16[256,864]{1,0:T(8,128)(2,1)S(1)} %all_gather.3.error_ref), kind=kOutput, calls=%fused_computation.6 | convolution fusion | flops 75497472 | bytes 1048576 | tf_op jit(solution)/shard_map/dot_general | solution.py:39
  105.6 1.2 %fusion.1 = f32[6,512,288]{1,2,0:T(8,128)} fusion(f32[6,512,288]{1,2,0:T(8,128)} %fusion.2, bf16[256,1536]{1,0:T(8,128)(2,1)S(1)} %bitcast.42, bf16[256,864]{1,0:T(8,128)(2,1)S(1)} %all_gather.3.error_ref), kind=kOutput, calls=%fused_computation.4 | convolution fusion | flops 75497472 | bytes 1048576 | tf_op jit(solution)/shard_map/dot_general | solution.py:39
  106.8 1.2 %fusion = f32[6,512,288]{1,2,0:T(8,128)} fusion(f32[6,512,288]{1,2,0:T(8,128)} %fusion.1, bf16[256,1536]{1,0:T(8,128)(2,1)S(1)} %bitcast.43, bf16[256,864]{1,0:T(8,128)(2,1)S(1)} %all_gather.3.error_ref), kind=kOutput, calls=%fused_computation.2 | convolution fusion | flops 75497472 | bytes 1048576 | tf_op jit(solution)/shard_map/dot_general | solution.py:39
  108.0 0.6 fusion.20
  109.9 7.5 %all-to-all-done.5 = bf16[8,32,1536]{2,1,0:T(8,128)(2,1)S(1)} async-done(((bf16[8,32,1536]{2,1,0:T(8,128)(2,1)}), bf16[8,32,1536]{2,1,0:T(8,128)(2,1)S(1)}, u32[]{:S(2)}, u32[]{:S(2)}) %all-to-all-start.5) | async-done | bytes 786464 | tf_op jit(solution)/shard_map/all_to_all | solution.py:27
  117.4 0.0 copy-done.2
  117.4 2.2 %encoder_grad.1 = (f32[3,288,512]{2,1,0:T(8,128)}, f32[3,512]{1,0:T(4,128)}) custom-call(bf16[3,288,256]{2,1,0:T(8,128)(2,1)S(1)} %bitcast.49, bf16[256,1536]{1,0:T(8,128)(2,1)S(1)} %bitcast.47), custom_call_target="tpu_custom_call" | custom-call | tf_op jit(solution)/shard_map/encoder_grad/pallas_call | solution.py:193
  (3 shorter events, 0.1 us)
Async XLA Ops:
  0.6 22.2 %copy-start.5 = (f32[3,512]{1,0:T(4,128)S(1)}, f32[3,512]{1,0:T(4,128)}, u32[]{:S(2)}) copy-start(f32[3,512]{1,0:T(4,128)} %bias_ref.2) | copy-start | bytes 18436
  0.7 1.0 copy-start.1
  1.7 1.2 copy-start.3
  2.8 34.8 %copy-start = (bf16[6,512,288]{1,2,0:T(8,128)(2,1)S(1)}, bf16[6,512,288]{1,2,0:T(8,128)(2,1)}, u32[]{:S(2)}) copy-start(bf16[6,512,288]{1,2,0:T(8,128)(2,1)} %param.10) | copy-start | bytes 5308420
  22.9 39.5 %copy-start.4 = (bf16[3,256,288]{1,2,0:T(8,128)(2,1)S(1)}, bf16[3,256,288]{1,2,0:T(8,128)(2,1)}, u32[]{:S(2)}) copy-start(bf16[3,256,288]{1,2,0:T(8,128)(2,1)} %param.7) | copy-start | bytes 1327108
  22.9 39.5 %copy-start.6 = (f32[3,288]{1,0:T(4,128)S(1)}, f32[3,288]{1,0:T(4,128)}, u32[]{:S(2)}) copy-start(f32[3,288]{1,0:T(4,128)} %bias_ref.3) | copy-start | bytes 10372
  38.8 1.6 %collective-permute-start = (bf16[128,864]{1,0:T(8,128)(2,1)S(1)}, bf16[128,864]{1,0:T(8,128)(2,1)S(1)}, u32[]{:S(2)}, u32[]{:S(2)}) collective-permute-start(bf16[128,864]{1,0:T(8,128)(2,1)S(1)} %get-tuple-element.15), channel_id=1, source_target_pairs={{0,1},{1,0},{2,3},{3,2},{4,5},{5,4},{6,7},{7,6},{8,9},{9,8},{10,11... | collective-permute-start | bytes 663560 | tf_op jit(solution)/shard_map/ppermute | solution.py:241
  82.0 17.7 %all-to-all-start.4 = ((bf16[8,32,1664]{2,1,0:T(8,128)(2,1)}), bf16[8,32,1664]{2,1,0:T(8,128)(2,1)S(1)}, u32[]{:S(2)}, u32[]{:S(2)}) async-start(bf16[8,32,1664]{2,1,0:T(8,128)(2,1)} %bitcast.9), calls=%async_computation.4 | async-start | bytes 1703936 | tf_op jit(solution)/shard_map/all_to_all | solution.py:27
  89.1 28.3 %copy-start.2 = (bf16[3,256,288]{1,2,0:T(8,128)(2,1)S(1)}, bf16[3,256,288]{1,2,0:T(8,128)(2,1)}, u32[]{:S(2)}) copy-start(bf16[3,256,288]{1,2,0:T(8,128)(2,1)} %param.6) | copy-start | bytes 1327108
  100.8 16.6 %all-to-all-start.5 = ((bf16[8,32,1536]{2,1,0:T(8,128)(2,1)}), bf16[8,32,1536]{2,1,0:T(8,128)(2,1)S(1)}, u32[]{:S(2)}, u32[]{:S(2)}) async-start(bf16[8,32,1536]{2,1,0:T(8,128)(2,1)} %broadcast_in_dim.13), calls=%async_computation.5 | async-start | bytes 1572864 | tf_op jit(solution)/shard_map/all_to_all | solution.py:27

commit v6 on v5

--- a/solution.py
+++ b/solution.py
@@ -181,58 +181,100 @@
     )
 
 
-def encoder_grad_kernel(acts_ref, delta_ref, grad_ref, bias_ref):
-    delta = delta_ref[...]
-    grad_ref[0] = contract(acts_ref[0], delta, 1, 0)
-    bias_ref[pl.ds(pl.program_id(0), 1), :] = jnp.sum(delta.astype(F32), axis=0, keepdims=True)
-
-
-def encoder_grad(acts_t, delta):
+def delta_kernel(share, arrived_ref, features_ref, own_ref, mse_ref):
+    slots = arrived_ref.shape[0]
+    columns = features_ref.shape[1]
+    total = arrived_ref[0].astype(F32)
+    for k in range(1, slots):
+        total = total + arrived_ref[k].astype(F32)
+    own_ref[...] = jnp.where(features_ref[...] > 0, total[:, :columns], 0.0).astype(BF16)
+    mse_ref[0, 0] = jnp.sum(total[:1, columns:]) * share
+
+
+def own_delta_of(arrived, own_features, share):
+    vmem = pl.BlockSpec(memory_space=pltpu.VMEM)
+    return pl.pallas_call(
+        functools.partial(delta_kernel, share),
+        in_specs=[vmem, vmem],
+        out_specs=[vmem, pl.BlockSpec(memory_space=pltpu.SMEM)],
+        out_shape=[
+            jax.ShapeDtypeStruct(own_features.shape, BF16),
+            jax.ShapeDtypeStruct((1, 1), F32),
+        ],
+        compiler_params=pltpu.CompilerParams(vmem_limit_bytes=VMEM),
+        name="own_delta",
+    )(arrived, own_features)
+
+
+def gradients_kernel(
+    acts_ref, delta_ref, features_ref, error_ref,
+    enc_hbm, bias_ref, dec_hbm, enc_held, dec_held, enc_sems, dec_sems,
+):
+    layers, width, tokens = acts_ref.shape
+    feature_dev = enc_held.shape[2]
+    leaving = []
+
+    def send(held, out, sems, k):
+        copy = pltpu.make_async_copy(held.at[k], out.at[k], sems.at[k])
+        copy.start()
+        leaving.append(copy)
+
+    for a in range(layers):
+        columns = slice(a * feature_dev, (a + 1) * feature_dev)
+        for b in range(a, layers):
+            pair = pair_number(a, b, layers)
+            dec_held[pair] = contract(error_ref[:, b * width : (b + 1) * width], features_ref[:, columns], 0, 0)
+            send(dec_held, dec_hbm, dec_sems, pair)
+    ones = jnp.ones((8, tokens), BF16)
+    for a in range(layers):
+        delta = delta_ref[:, a * feature_dev : (a + 1) * feature_dev]
+        enc_held[a] = contract(acts_ref[a], delta, 1, 0)
+        send(enc_held, enc_hbm, enc_sems, a)
+        bias_ref[a : a + 1, :] = contract(ones, delta, 1, 0)[:1]
+    for copy in leaving:
+        copy.wait()
+
+
+def gradients(acts_t, delta, features, error):
     layers, width, tokens = acts_t.shape
     feature_dev = delta.shape[1] // layers
+    pairs = layers * (layers + 1) // 2
+    vmem = pl.BlockSpec(memory_space=pltpu.VMEM)
+    anywhere = pl.BlockSpec(memory_space=pl.ANY)
+    enc_shape = (layers, width, feature_dev)
+    dec_shape = (pairs, width, feature_dev)
     return pl.pallas_call(
-        encoder_grad_kernel,
-        grid=(layers,),
-        in_specs=[
-            pl.BlockSpec((1, width, tokens), lambda a: (a, 0, 0)),
-            pl.BlockSpec((tokens, feature_dev), lambda a: (0, a)),
+        gradients_kernel,
+        in_specs=[vmem] * 4,
+        out_specs=[anywhere, vmem, anywhere],
+        out_shape=[
+            jax.ShapeDtypeStruct(shape, F32) for shape in (enc_shape, (layers, feature_dev), dec_shape)
         ],
-        out_specs=[
-            pl.BlockSpec((1, width, feature_dev), lambda a: (a, 0, 0)),
-            pl.BlockSpec((layers, feature_dev), lambda a: (0, 0)),
-        ],
-        out_shape=[
-            jax.ShapeDtypeStruct((layers, width, feature_dev), F32),
-            jax.ShapeDtypeStruct((layers, feature_dev), F32),
+        scratch_shapes=[
+            pltpu.VMEM(enc_shape, F32),
+            pltpu.VMEM(dec_shape, F32),
+            pltpu.SemaphoreType.DMA((layers,)),
+            pltpu.SemaphoreType.DMA((pairs,)),
         ],
         compiler_params=pltpu.CompilerParams(vmem_limit_bytes=VMEM),
-        name="encoder_grad",
-    )(acts_t, delta)
+        name="gradients",
+    )(acts_t, delta, features, error)
 
 
 def local(acts_in, acts_out, enc_weight, enc_bias, dec_weight, dec_bias):
-    layers, tokens, width_dev = acts_in.shape
-    feature_dev = enc_weight.shape[2]
-    pair_list = [(a, b) for a in range(layers) for b in range(a, layers)]
+    layers, tokens, _ = acts_in.shape
     slots = lax.axis_size(SLOT)
     chips = lax.axis_size(CHIPS)
     core = lax.axis_index(CORE)
     acts_t = jnp.transpose(acts_in, (0, 2, 1))
     dec_t = jnp.transpose(dec_weight, (0, 2, 1))
 
-    def feats(x, a):
-        return x[:, a * feature_dev : (a + 1) * feature_dev]
-
-    def width(x, b):
-        return x[:, b * width_dev : (b + 1) * width_dev]
-
     half = tokens // 2
     portion = half // chips
     core = core.reshape(1)
     offset = core * half + lax.axis_index(CHIPS) * portion
-    acts_t, core, offset = lax.optimization_barrier((acts_t, core, offset))
-
     sent = encode(acts_t, enc_weight)
+    sent, core, offset = lax.optimization_barrier((sent, core, offset))
     arrived = exchange(sent.reshape(slots, tokens // slots, -1), SLOT)
     own_features = own_features_of(arrived, enc_bias)
     features = sent_to_all(own_features, SLOT).reshape(tokens, -1)
@@ -245,14 +287,11 @@
     error = lax.all_gather(half_error, CORE, axis=0, tiled=True)
 
     sent = upstream(error, dec_t, layers)
-    total = exchange(sent.reshape(slots, tokens // slots, -1), SLOT).astype(F32).sum(axis=0)
-    mse = (total[0, layers * feature_dev] + total[0, layers * feature_dev + 1]) / (layers * tokens * D)
-    own_delta = jnp.where(own_features > 0, total[:, : layers * feature_dev], 0.0).astype(BF16)
+    arrived = exchange(sent.reshape(slots, tokens // slots, -1), SLOT)
+    own_delta, mse = own_delta_of(arrived, own_features, 1.0 / (layers * tokens * D))
     delta = sent_to_all(own_delta, SLOT).reshape(tokens, -1)
-
-    dec_grads = [contract(feats(features, a), width(error, b), 0, 0) for a, b in pair_list]
-    enc_grad, bias_grad = encoder_grad(acts_t, delta)
-    return (enc_grad, bias_grad, jnp.stack(dec_grads), mse)
+    enc_grad, bias_grad, dec_grad_t = gradients(acts_t, delta, features, error)
+    return (enc_grad, bias_grad, jnp.transpose(dec_grad_t, (0, 2, 1)), mse.reshape(()))
 
 
 def solution(mesh):

time: 122 us -> 118 us (0.967)
  blocking collectives: 72.3 us -> 104 us
  waiting for transfers between devices: 19.5 us -> 1.48 us
  matrix products: 7.18 us -> 0 us
  starting transfers between devices: 7.19 us -> 0.09 us
  between operations: 3.18 us -> 0.73 us
  local copies, waits for them, and re-layouts: 3.8 us -> 2.33 us
    all_to_all x4 -> x6, blocking collectives: 70.2 us -> 102 us  [exchange(): return lax.all_to_all(tiles, axis, split_axis=0, concat_axis=0, tiled=True)]
    all_to_all x2 -> x0, waiting for transfers between devices: 18.1 us -> none  [exchange(): return lax.all_to_all(tiles, axis, split_axis=0, concat_axis=0, tiled=True)]
    dot_general x6 -> x0, matrix products: 7.18 us -> none  [contract(): lax.dot_general(x, y, (((x_dim,), (y_dim,)), ((), ())), preferred_element...]
    all_to_all x2 -> x0, starting transfers between devices: 7.1 us -> none  [exchange(): return lax.all_to_all(tiles, axis, split_axis=0, concat_axis=0, tiled=True)]
    pallas_call x1 -> x2, Pallas kernels: 2.17 us -> 4.28 us  [the longest x1 3.47 us: gradients(): pl.pallas_call(gradients_kernel, in_specs=[vmem] * 4, out_specs=[anywhere...]
  transfers between devices with their start and end apart: 3 -> 1, of which waited for: 3 -> 1; matrix products, arithmetic and copies ran while one was open for 6% -> 0% of each run, Pallas kernels for 0% -> 0%
where the time goes in v6:
time: 118 us; the launch traced here: 117 us
  blocking collectives  104 us (88%)
  Pallas kernels  8.53 us (7%)
  local copies, waits for them, and re-layouts  2.33 us (2%)
  waiting for transfers between devices  1.48 us (1%)
    all_to_all x6, blocking collectives, exchange(): return lax.all_to_all(tiles, axis, split_axis=0, concat_axis=0, tiled=True)  102 us
    pallas_call x5, Pallas kernels, on_chip(): pl.pallas_call(kernel, in_specs=[smem if arg.dtype == jnp.int32 else vmem...  4.25 us
    pallas_call x1, Pallas kernels, gradients(): pl.pallas_call(gradients_kernel, in_specs=[vmem] * 4, out_specs=[anywhere...  3.47 us
  transfers between devices with their start and end apart: 1, of which 1 were waited for; matrix products, arithmetic and copies ran while one was open for 0% of the time, Pallas kernels for 0%

profile of v6, /device:TPU:32, one launch (start us, length us, event | category | flops | bytes accessed | tf_op | source)
XLA Modules:
  0.0 117.4 jit_solution(8184113748632702829)
XLA Ops:
  0.6 0.0 copy-start.1
  0.7 1.0 copy-done.1
  1.7 0.0 copy-start.3
  1.7 1.2 copy-done.3
  2.8 0.0 copy-start.5
  2.8 1.2 encode.1
  4.0 18.9 %all_to_all.30.arrived_ref = bf16[8,32,1664]{2,1,0:T(8,128)(2,1)S(1)} all-to-all(bf16[8,32,1664]{2,1,0:T(8,128)(2,1)S(1)} %bitcast.18), channel_id=1, replica_groups=mesh['slot_0'=2,'slot_1'=4,'feat_0'=2,'feat_1'=8,'feat_2'=2] {'slot_0','..., dimensions={0} | all-to-all | bytes 1703936 | tf_op jit(solution)/shard_map/all_to_all | solution.py:27
  22.9 0.0 copy-done.5
  22.9 0.0 copy-start
  22.9 0.7 own_features.1.features_ref
  23.5 0.1 broadcast_in_dim.6
  23.6 14.0 %all_to_all.31 = bf16[8,32,1536]{2,1,0:T(8,128)(2,1)S(1)} all-to-all(bf16[8,32,1536]{2,1,0:T(8,128)(2,1)S(1)} %broadcast_in_dim.6), channel_id=1, replica_groups=mesh['slot_0'=2,'slot_1'=4,'feat_0'=2,'feat_1'=8,'feat_2'=2] {'slot_0','..., dimensions={0} | all-to-all | bytes 1572864 | tf_op jit(solution)/shard_map/all_to_all | solution.py:27
  37.6 0.0 copy-done
  37.6 0.0 copy-start.4
  37.6 0.0 copy-start.6
  37.6 1.1 decode.1
  38.7 0.1 collective-permute-start
  38.8 1.5 %collective-permute-done = bf16[128,864]{1,0:T(8,128)(2,1)S(1)} collective-permute-done((bf16[128,864]{1,0:T(8,128)(2,1)S(1)}, bf16[128,864]{1,0:T(8,128)(2,1)S(1)}, u32[]{:S(2)}, u32[]{:S(2)}) %collective-permute-start) | collective-permute-done | bytes 221216 | tf_op jit(solution)/shard_map/ppermute | solution.py:283
  40.4 22.0 %all_to_all.32.arrived_ref = bf16[16,8,864]{2,1,0:T(8,128)(2,1)S(1)} all-to-all(bf16[16,8,864]{2,1,0:T(8,128)(2,1)S(1)} %fusion), channel_id=1, replica_groups=mesh['slot_0'=2,'slot_1'=4,'feat_0'=2,'feat_1'=8,'feat_2'=2] {'feat_0','..., dimensions={0} | all-to-all | bytes 442368 | tf_op jit(solution)/shard_map/all_to_all | solution.py:27
  62.3 0.0 copy-done.4
  62.3 0.0 copy-done.6
  62.3 0.3 own_error.1
  62.7 15.3 %all_to_all.33 = bf16[16,8,864]{2,1,0:T(8,128)(2,1)S(1)} all-to-all(bf16[16,8,864]{2,1,0:T(8,128)(2,1)S(1)} %broadcast_in_dim.7), channel_id=1, replica_groups=mesh['slot_0'=2,'slot_1'=4,'feat_0'=2,'feat_1'=8,'feat_2'=2] {'feat_0','..., dimensions={0} | all-to-all | bytes 442368 | tf_op jit(solution)/shard_map/all_to_all | solution.py:27
  78.0 2.1 %all_gather.3.error_ref = bf16[256,864]{1,0:T(8,128)(2,1)S(1)} all-gather(bf16[128,864]{1,0:T(8,128)(2,1)S(1)} %bitcast.24), channel_id=1, replica_groups=mesh['slot_0'=2,'slot_1'=4,'feat_0'=2,'feat_1'=8,'feat_2'=2] {'feat_2'}, dimensions={0}, use_global_device_ids=true | all-gather | bytes 663552 | tf_op jit(solution)/shard_map/all_gather | solution.py:287
  80.1 1.0 upstream.1
  81.1 16.7 %all_to_all.34.arrived_ref = bf16[8,32,1664]{2,1,0:T(8,128)(2,1)S(1)} all-to-all(bf16[8,32,1664]{2,1,0:T(8,128)(2,1)S(1)} %bitcast.19), channel_id=1, replica_groups=mesh['slot_0'=2,'slot_1'=4,'feat_0'=2,'feat_1'=8,'feat_2'=2] {'slot_0','..., dimensions={0} | all-to-all | bytes 1703936 | tf_op jit(solution)/shard_map/all_to_all | solution.py:27
  97.8 0.0 copy-start.2
  97.8 0.8 own_delta.1
  98.6 0.1 broadcast_in_dim.8
  98.7 15.2 %all_to_all.35 = bf16[8,32,1536]{2,1,0:T(8,128)(2,1)S(1)} all-to-all(bf16[8,32,1536]{2,1,0:T(8,128)(2,1)S(1)} %broadcast_in_dim.8), channel_id=1, replica_groups=mesh['slot_0'=2,'slot_1'=4,'feat_0'=2,'feat_1'=8,'feat_2'=2] {'slot_0','..., dimensions={0} | all-to-all | bytes 1572864 | tf_op jit(solution)/shard_map/all_to_all | solution.py:27
  113.9 0.0 copy-done.2
  113.9 3.5 %gradients.1 = (f32[3,288,512]{2,1,0:T(8,128)}, f32[3,512]{1,0:T(4,128)}, f32[6,288,512]{2,1,0:T(8,128)}) custom-call(bf16[3,288,256]{2,1,0:T(8,128)(2,1)S(1)} %bitcast.22, bf16[256,1536]{1,0:T(8,128)(2,1)S(1)} %bitcast.20, bf16[256,1536]{1,0:T(8,128)(2,1)S(1)} %bitcast.17, bf16[256,864]{1,0:T(8,128)(2,1)S(1)} %all_gather.3.error_ref), custom_call_target="tpu_custom_call" | custom-call | tf_op jit(solution)/shard_map/gradients/pallas_call | solution.py:246
  (2 shorter events, 0.1 us)
Async XLA Ops:
  0.6 1.0 copy-start.1
  1.7 1.2 copy-start.3
  2.8 20.0 %copy-start.5 = (f32[3,512]{1,0:T(4,128)S(1)}, f32[3,512]{1,0:T(4,128)}, u32[]{:S(2)}) copy-start(f32[3,512]{1,0:T(4,128)} %bias_ref.2) | copy-start | bytes 18436
  22.9 14.8 %copy-start = (bf16[6,512,288]{1,2,0:T(8,128)(2,1)S(1)}, bf16[6,512,288]{1,2,0:T(8,128)(2,1)}, u32[]{:S(2)}) copy-start(bf16[6,512,288]{1,2,0:T(8,128)(2,1)} %param.10) | copy-start | bytes 5308420
  37.6 24.7 %copy-start.4 = (bf16[3,256,288]{1,2,0:T(8,128)(2,1)S(1)}, bf16[3,256,288]{1,2,0:T(8,128)(2,1)}, u32[]{:S(2)}) copy-start(bf16[3,256,288]{1,2,0:T(8,128)(2,1)} %param.7) | copy-start | bytes 1327108
  37.6 24.7 %copy-start.6 = (f32[3,288]{1,0:T(4,128)S(1)}, f32[3,288]{1,0:T(4,128)}, u32[]{:S(2)}) copy-start(f32[3,288]{1,0:T(4,128)} %bias_ref.3) | copy-start | bytes 10372
  38.7 1.6 %collective-permute-start = (bf16[128,864]{1,0:T(8,128)(2,1)S(1)}, bf16[128,864]{1,0:T(8,128)(2,1)S(1)}, u32[]{:S(2)}, u32[]{:S(2)}) collective-permute-start(bf16[128,864]{1,0:T(8,128)(2,1)S(1)} %get-tuple-element.18), channel_id=1, source_target_pairs={{0,1},{1,0},{2,3},{3,2},{4,5},{5,4},{6,7},{7,6},{8,9},{9,8},{10,11... | collective-permute-start | bytes 663560 | tf_op jit(solution)/shard_map/ppermute | solution.py:283
  97.8 16.1 %copy-start.2 = (bf16[3,256,288]{1,2,0:T(8,128)(2,1)S(1)}, bf16[3,256,288]{1,2,0:T(8,128)(2,1)}, u32[]{:S(2)}) copy-start(bf16[3,256,288]{1,2,0:T(8,128)(2,1)} %param.6) | copy-start | bytes 1327108

commit v7 on v6

--- a/solution.py
+++ b/solution.py
@@ -14,6 +14,7 @@
 CHIPS = ("feat_0", "feat_1")
 CORE = "feat_2"
 LANES = 128
+EXTRA = 16
 VMEM = 16 * 2**20
 OCTAVES = 250.0
 ABOVE = 1.0078125
@@ -39,12 +40,22 @@
     return lax.dot_general(x, y, (((x_dim,), (y_dim,)), ((), ())), preferred_element_type=F32)
 
 
+def store_tiles(out_ref, value, first, slots):
+    rows = value.shape[0] // slots
+    for k in range(slots):
+        for j in range(value.shape[1] // LANES):
+            out_ref[k, (first + j) * rows : (first + j + 1) * rows, :] = value[
+                k * rows : (k + 1) * rows, j * LANES : (j + 1) * LANES
+            ]
+
+
 def encode_kernel(acts_ref, weight_ref, out_ref):
     layers = acts_ref.shape[0]
-    tokens = out_ref.shape[0]
     feature_dev = weight_ref.shape[2]
-    lane = lax.broadcasted_iota(jnp.int32, (tokens, LANES), 1)
-    scales = jnp.zeros((tokens, LANES), F32)
+    slots = out_ref.shape[0]
+    rows = acts_ref.shape[2] // slots
+    tiles = feature_dev // LANES
+    scales = []
     for a in range(layers):
         preact = contract(acts_ref[a], weight_ref[a], 0, 0)
         size = jnp.abs(preact)
@@ -52,9 +63,16 @@
         scale = (largest * ABOVE).astype(BF16).astype(F32)
         square = jnp.maximum(size * (1.0 / scale), LEAST)
         code = jnp.exp2(square * lax.rsqrt(square) * OCTAVES - OCTAVES / 2)
-        out_ref[:, a * feature_dev : (a + 1) * feature_dev] = jnp.where(preact < 0, -code, code).astype(BF16)
-        scales = jnp.where(lane == a, scale, scales)
-    out_ref[:, layers * feature_dev :] = scales.astype(BF16)
+        store_tiles(out_ref, jnp.where(preact < 0, -code, code).astype(BF16), a * tiles, slots)
+        scales.append(scale)
+    lane = lax.broadcasted_iota(jnp.int32, (EXTRA, LANES), 1)
+    for k in range(slots):
+        extra = jnp.zeros((EXTRA, LANES), F32)
+        for part in range(rows // EXTRA):
+            at = k * rows + part * EXTRA
+            for a in range(layers):
+                extra = jnp.where(lane == part * layers + a, scales[a][at : at + EXTRA], extra)
+        out_ref[k, layers * tiles * rows :, :] = extra.astype(BF16)
 
 
 def on_chip(kernel, name, args, out_shape, scratch_shapes=()):
@@ -71,29 +89,47 @@
     )(*args)
 
 
-def encode(acts_t, enc_weight):
+def sent_shape(slots, tokens, columns):
+    return jax.ShapeDtypeStruct((slots, tokens // slots * columns // LANES + EXTRA, LANES), BF16)
+
+
+def encode(acts_t, enc_weight, slots):
     layers, _, tokens = acts_t.shape
-    shape = (tokens, layers * enc_weight.shape[2] + LANES)
-    return on_chip(encode_kernel, "encode", (acts_t, enc_weight), jax.ShapeDtypeStruct(shape, BF16))
+    shape = sent_shape(slots, tokens, layers * enc_weight.shape[2])
+    return on_chip(encode_kernel, "encode", (acts_t, enc_weight), shape)
 
 
 def features_kernel(arrived_ref, bias_ref, own_ref):
-    slots, rows, _ = arrived_ref.shape
+    slots = arrived_ref.shape[0]
+    rows = own_ref.shape[0]
     layers, feature_dev = bias_ref.shape
-    totals = [jnp.broadcast_to(bias_ref[a : a + 1, :], (rows, feature_dev)) for a in range(layers)]
+    tiles = feature_dev // LANES
+    scales = []
     for k in range(slots):
-        scales = arrived_ref[k, :, layers * feature_dev :].astype(F32)
-        for a in range(layers):
-            code = arrived_ref[k, :, a * feature_dev : (a + 1) * feature_dev].astype(F32)
-            root = jnp.log2(jnp.abs(code)) * (1.0 / OCTAVES) + 0.5
-            size = root * root * scales[:, a : a + 1]
-            totals[a] = totals[a] + jnp.where(code < 0, -size, size)
-    for a in range(layers):
-        own_ref[:, a * feature_dev : (a + 1) * feature_dev] = jnp.maximum(totals[a], 0.0).astype(BF16)
-
-
-def own_features_of(arrived, enc_bias):
-    shape = (arrived.shape[1], enc_bias.size)
+        extra = arrived_ref[k, layers * tiles * rows :, :].astype(F32)
+        parts = rows // EXTRA
+        scales.append(
+            [
+                jnp.concatenate([extra[:, p * layers + a : p * layers + a + 1] for p in range(parts)], axis=0)
+                for a in range(layers)
+            ]
+        )
+    for a in range(layers):
+        for j in range(tiles):
+            at = (a * tiles + j) * rows
+            columns = slice(j * LANES, (j + 1) * LANES)
+            total = jnp.broadcast_to(bias_ref[a : a + 1, columns], (rows, LANES))
+            for k in range(slots):
+                code = arrived_ref[k, at : at + rows, :].astype(F32)
+                root = jnp.log2(jnp.abs(code)) * (1.0 / OCTAVES) + 0.5
+                size = root * root * scales[k][a]
+                total = total + jnp.where(code < 0, -size, size)
+            at = (a * tiles + j) * LANES
+            own_ref[:, at : at + LANES] = jnp.maximum(total, 0.0).astype(BF16)
+
+
+def own_features_of(arrived, enc_bias, rows):
+    shape = (rows, enc_bias.size)
     return on_chip(
         features_kernel, "own_features", (arrived, enc_bias), jax.ShapeDtypeStruct(shape, BF16)
     )
@@ -154,9 +190,13 @@
     )
 
 
-def upstream_kernel(layers, error_ref, weight_ref, out_ref):
-    tokens = error_ref.shape[0]
+def upstream_kernel(layers, core_ref, mine_ref, theirs_ref, weight_ref, out_ref, error_ref):
     width, feature_dev = weight_ref.shape[1:]
+    slots = out_ref.shape[0]
+    half = mine_ref.shape[0]
+    core = core_ref[0]
+    for ref, side in ((mine_ref, core), (theirs_ref, 1 - core)):
+        error_ref[pl.ds(pl.multiple_of(side * half, half), half), :] = ref[...]
     for a in range(layers):
         total = None
         for b in range(a, layers):
@@ -164,31 +204,42 @@
                 error_ref[:, b * width : (b + 1) * width], weight_ref[pair_number(a, b, layers)], 1, 0
             )
             total = term if total is None else total + term
-        out_ref[:, a * feature_dev : (a + 1) * feature_dev] = total.astype(BF16)
+        store_tiles(out_ref, total.astype(BF16), a * feature_dev // LANES, slots)
     wide = error_ref[...].astype(F32)
     squared = jnp.sum(wide * wide)
     coarse = squared.astype(BF16).astype(F32)
     fine = squared - coarse
-    lane = lax.broadcasted_iota(jnp.int32, (tokens, LANES), 1)
-    extra = jnp.where(lane == 0, coarse, jnp.where(lane == 1, fine, 0.0))
-    out_ref[:, layers * feature_dev :] = extra.astype(BF16)
-
-
-def upstream(error, dec_t, layers):
-    shape = (error.shape[0], layers * dec_t.shape[2] + LANES)
+    lane = lax.broadcasted_iota(jnp.int32, (EXTRA, LANES), 1)
+    extra = jnp.where(lane == 0, coarse, jnp.where(lane == 1, fine, 0.0)).astype(BF16)
+    for k in range(slots):
+        out_ref[k, out_ref.shape[1] - EXTRA :, :] = extra
+
+
+def upstream(core, mine, theirs, dec_t, layers, slots):
+    half, columns = mine.shape
     return on_chip(
-        functools.partial(upstream_kernel, layers), "upstream", (error, dec_t), jax.ShapeDtypeStruct(shape, BF16)
+        functools.partial(upstream_kernel, layers),
+        "upstream",
+        (core, mine, theirs, dec_t),
+        [
+            sent_shape(slots, 2 * half, layers * dec_t.shape[2]),
+            jax.ShapeDtypeStruct((2 * half, columns), BF16),
+        ],
     )
 
 
 def delta_kernel(share, arrived_ref, features_ref, own_ref, mse_ref):
     slots = arrived_ref.shape[0]
-    columns = features_ref.shape[1]
+    rows, columns = features_ref.shape
     total = arrived_ref[0].astype(F32)
     for k in range(1, slots):
         total = total + arrived_ref[k].astype(F32)
-    own_ref[...] = jnp.where(features_ref[...] > 0, total[:, :columns], 0.0).astype(BF16)
-    mse_ref[0, 0] = jnp.sum(total[:1, columns:]) * share
+    for j in range(columns // LANES):
+        at = slice(j * LANES, (j + 1) * LANES)
+        delta = jnp.where(features_ref[:, at] > 0, total[j * rows : (j + 1) * rows, :], 0.0)
+        own_ref[:, at] = delta.astype(BF16)
+    last = columns // LANES * rows
+    mse_ref[0, 0] = jnp.sum(total[last : last + 1, :]) * share
 
 
 def own_delta_of(arrived, own_features, share):
@@ -273,10 +324,9 @@
     portion = half // chips
     core = core.reshape(1)
     offset = core * half + lax.axis_index(CHIPS) * portion
-    sent = encode(acts_t, enc_weight)
+    sent = encode(acts_t, enc_weight, slots)
     sent, core, offset = lax.optimization_barrier((sent, core, offset))
-    arrived = exchange(sent.reshape(slots, tokens // slots, -1), SLOT)
-    own_features = own_features_of(arrived, enc_bias)
+    own_features = own_features_of(exchange(sent, SLOT), enc_bias, tokens // slots)
     features = sent_to_all(own_features, SLOT).reshape(tokens, -1)
 
     theirs, mine = decode(core, features, dec_t, layers)
@@ -284,11 +334,10 @@
     arrived = exchange(chip_sum.reshape(chips, portion, -1), CHIPS)
     own_error = own_error_of(offset, arrived, jnp.transpose(acts_out, (0, 2, 1)), dec_bias)
     half_error = sent_to_all(own_error, CHIPS).reshape(half, -1)
-    error = lax.all_gather(half_error, CORE, axis=0, tiled=True)
-
-    sent = upstream(error, dec_t, layers)
-    arrived = exchange(sent.reshape(slots, tokens // slots, -1), SLOT)
-    own_delta, mse = own_delta_of(arrived, own_features, 1.0 / (layers * tokens * D))
+    other_error = lax.ppermute(half_error, CORE, [(0, 1), (1, 0)])
+
+    sent, error = upstream(core, half_error, other_error, dec_t, layers, slots)
+    own_delta, mse = own_delta_of(exchange(sent, SLOT), own_features, 1.0 / (layers * tokens * D))
     delta = sent_to_all(own_delta, SLOT).reshape(tokens, -1)
     enc_grad, bias_grad, dec_grad_t = gradients(acts_t, delta, features, error)
     return (enc_grad, bias_grad, jnp.transpose(dec_grad_t, (0, 2, 1)), mse.reshape(()))

time: 118 us -> 117 us (level)
  blocking collectives: 104 us -> 102 us
  waiting for transfers between devices: 1.48 us -> 2.96 us
    all_gather x1 -> x0, blocking collectives: 2.12 us -> none  [local(): error = lax.all_gather(half_error, CORE, axis=0, tiled=True)]
    ppermute x0 -> x1, waiting for transfers between devices: none -> 1.49 us  [local(): other_error = lax.ppermute(half_error, CORE, [(0, 1), (1, 0)])]
  transfers between devices with their start and end apart: 1 -> 2, of which waited for: 1 -> 2; matrix products, arithmetic and copies ran while one was open for 0% -> 0% of each run, Pallas kernels for 0% -> 0%
where the time goes in v7:
time: 117 us; the launch traced here: 116 us
  blocking collectives  102 us (87%)
  Pallas kernels  8.6 us (7%)
  waiting for transfers between devices  2.96 us (3%)
  local copies, waits for them, and re-layouts  2.33 us (2%)
    all_to_all x6, blocking collectives, exchange(): return lax.all_to_all(tiles, axis, split_axis=0, concat_axis=0, tiled=True)  102 us
    pallas_call x5, Pallas kernels, on_chip(): pl.pallas_call(kernel, in_specs=[smem if arg.dtype == jnp.int32 else vmem...  4.32 us
    pallas_call x1, Pallas kernels, gradients(): pl.pallas_call(gradients_kernel, in_specs=[vmem] * 4, out_specs=[anywhere...  3.48 us
  transfers between devices with their start and end apart: 2, of which 2 were waited for; matrix products, arithmetic and copies ran while one was open for 0% of the time, Pallas kernels for 0%

profile of v7, /device:TPU:32, one launch (start us, length us, event | category | flops | bytes accessed | tf_op | source)
XLA Modules:
  0.0 116.4 jit_solution(12223386106394152276)
XLA Ops:
  0.6 0.0 copy-start.1
  0.7 1.0 copy-done.1
  1.7 0.0 copy-start.3
  1.7 1.2 %copy-done.3 = bf16[3,288,512]{2,1,0:T(8,128)(2,1)S(1)} copy-done((bf16[3,288,512]{2,1,0:T(8,128)(2,1)S(1)}, bf16[3,288,512]{2,1,0:T(8,128)(2,1)}, u32[]{:S(2)}) %copy-start.3) | copy-done | bytes 884760
  2.8 0.0 copy-start.5
  2.8 1.2 %encode.1 = bf16[8,400,128]{2,1,0:T(8,128)(2,1)S(1)} custom-call(bf16[3,288,256]{2,1,0:T(8,128)(2,1)S(1)} %bitcast.17, bf16[3,288,512]{2,1,0:T(8,128)(2,1)S(1)} %copy-done.3), custom_call_target="tpu_custom_call" | custom-call | tf_op jit(solution)/shard_map/encode/pallas_call | solution.py:81
  4.0 18.6 %all_to_all.30.arrived_ref = bf16[8,400,128]{2,1,0:T(8,128)(2,1)S(1)} all-to-all(bf16[8,400,128]{2,1,0:T(8,128)(2,1)S(1)} %encode.1), channel_id=1, replica_groups=mesh['slot_0'=2,'slot_1'=4,'feat_0'=2,'feat_1'=8,'feat_2'=2] {'slot_0','..., dimensions={0} | all-to-all | bytes 1638400 | tf_op jit(solution)/shard_map/all_to_all | solution.py:28
  22.6 0.0 copy-done.5
  22.6 0.0 copy-start
  22.6 0.7 own_features.1.features_ref
  23.3 0.1 broadcast_in_dim.6
  23.4 14.1 %all_to_all.31 = bf16[8,32,1536]{2,1,0:T(8,128)(2,1)S(1)} all-to-all(bf16[8,32,1536]{2,1,0:T(8,128)(2,1)S(1)} %broadcast_in_dim.6), channel_id=1, replica_groups=mesh['slot_0'=2,'slot_1'=4,'feat_0'=2,'feat_1'=8,'feat_2'=2] {'slot_0','..., dimensions={0} | all-to-all | bytes 1572864 | tf_op jit(solution)/shard_map/all_to_all | solution.py:28
  37.5 0.0 copy-done
  37.5 0.0 copy-start.4
  37.5 0.0 copy-start.6
  37.5 1.1 decode.1
  38.6 0.1 collective-permute-start
  38.7 1.5 %collective-permute-done = bf16[128,864]{1,0:T(8,128)(2,1)S(1)} collective-permute-done((bf16[128,864]{1,0:T(8,128)(2,1)S(1)}, bf16[128,864]{1,0:T(8,128)(2,1)S(1)}, u32[]{:S(2)}, u32[]{:S(2)}) %collective-permute-start) | collective-permute-done | bytes 221216 | tf_op jit(solution)/shard_map/ppermute | solution.py:333
  40.2 0.1 fusion
  40.2 22.0 %all_to_all.32.arrived_ref = bf16[16,8,864]{2,1,0:T(8,128)(2,1)S(1)} all-to-all(bf16[16,8,864]{2,1,0:T(8,128)(2,1)S(1)} %fusion), channel_id=1, replica_groups=mesh['slot_0'=2,'slot_1'=4,'feat_0'=2,'feat_1'=8,'feat_2'=2] {'feat_0','..., dimensions={0} | all-to-all | bytes 442368 | tf_op jit(solution)/shard_map/all_to_all | solution.py:28
  62.2 0.0 copy-done.4
  62.2 0.0 copy-done.6
  62.2 0.3 own_error.1
  62.5 15.3 %all_to_all.33 = bf16[16,8,864]{2,1,0:T(8,128)(2,1)S(1)} all-to-all(bf16[16,8,864]{2,1,0:T(8,128)(2,1)S(1)} %broadcast_in_dim.7), channel_id=1, replica_groups=mesh['slot_0'=2,'slot_1'=4,'feat_0'=2,'feat_1'=8,'feat_2'=2] {'feat_0','..., dimensions={0} | all-to-all | bytes 442368 | tf_op jit(solution)/shard_map/all_to_all | solution.py:28
  77.8 0.0 collective-permute-start.1
  77.8 1.5 %collective-permute-done.1.theirs_ref = bf16[128,864]{1,0:T(8,128)(2,1)S(1)} collective-permute-done((bf16[128,864]{1,0:T(8,128)(2,1)S(1)}, bf16[128,864]{1,0:T(8,128)(2,1)S(1)}, u32[]{:S(2)}, u32[]{:S(2)}) %collective-permute-start.1) | collective-permute-done | bytes 221216 | tf_op jit(solution)/shard_map/ppermute | solution.py:337
  79.3 1.1 upstream.1
  80.4 16.4 %all_to_all.34.arrived_ref = bf16[8,400,128]{2,1,0:T(8,128)(2,1)S(1)} all-to-all(bf16[8,400,128]{2,1,0:T(8,128)(2,1)S(1)} %get-tuple-element.21), channel_id=1, replica_groups=mesh['slot_0'=2,'slot_1'=4,'feat_0'=2,'feat_1'=8,'feat_2'=2] {'slot_0','..., dimensions={0} | all-to-all | bytes 1638400 | tf_op jit(solution)/shard_map/all_to_all | solution.py:28
  96.8 0.0 copy-start.2
  96.8 0.8 own_delta.1
  97.6 0.1 broadcast_in_dim.8
  97.7 15.2 %all_to_all.35 = bf16[8,32,1536]{2,1,0:T(8,128)(2,1)S(1)} all-to-all(bf16[8,32,1536]{2,1,0:T(8,128)(2,1)S(1)} %broadcast_in_dim.8), channel_id=1, replica_groups=mesh['slot_0'=2,'slot_1'=4,'feat_0'=2,'feat_1'=8,'feat_2'=2] {'slot_0','..., dimensions={0} | all-to-all | bytes 1572864 | tf_op jit(solution)/shard_map/all_to_all | solution.py:28
  112.9 0.0 copy-done.2
  112.9 3.5 %gradients.1 = (f32[3,288,512]{2,1,0:T(8,128)}, f32[3,512]{1,0:T(4,128)}, f32[6,288,512]{2,1,0:T(8,128)}) custom-call(bf16[3,288,256]{2,1,0:T(8,128)(2,1)S(1)} %bitcast.18, bf16[256,1536]{1,0:T(8,128)(2,1)S(1)} %bitcast.16, bf16[256,1536]{1,0:T(8,128)(2,1)S(1)} %bitcast.15, bf16[256,864]{1,0:T(8,128)(2,1)S(1)} %get-tuple-element.23.error_ref), custom_call_target="tpu_custom_call" | custom-call | tf_op jit(solution)/shard_map/gradients/pallas_call | solution.py:297
  (1 shorter events, 0.0 us)
Async XLA Ops:
  0.6 1.0 copy-start.1
  1.7 1.2 %copy-start.3 = (bf16[3,288,512]{2,1,0:T(8,128)(2,1)S(1)}, bf16[3,288,512]{2,1,0:T(8,128)(2,1)}, u32[]{:S(2)}) copy-start(bf16[3,288,512]{2,1,0:T(8,128)(2,1)} %weight_ref.1) | copy-start | bytes 2654212
  2.8 19.8 %copy-start.5 = (f32[3,512]{1,0:T(4,128)S(1)}, f32[3,512]{1,0:T(4,128)}, u32[]{:S(2)}) copy-start(f32[3,512]{1,0:T(4,128)} %bias_ref.2) | copy-start | bytes 18436
  22.6 14.9 %copy-start = (bf16[6,512,288]{1,2,0:T(8,128)(2,1)S(1)}, bf16[6,512,288]{1,2,0:T(8,128)(2,1)}, u32[]{:S(2)}) copy-start(bf16[6,512,288]{1,2,0:T(8,128)(2,1)} %param.10) | copy-start | bytes 5308420
  37.5 24.7 %copy-start.4 = (bf16[3,256,288]{1,2,0:T(8,128)(2,1)S(1)}, bf16[3,256,288]{1,2,0:T(8,128)(2,1)}, u32[]{:S(2)}) copy-start(bf16[3,256,288]{1,2,0:T(8,128)(2,1)} %param.7) | copy-start | bytes 1327108
  37.5 24.7 %copy-start.6 = (f32[3,288]{1,0:T(4,128)S(1)}, f32[3,288]{1,0:T(4,128)}, u32[]{:S(2)}) copy-start(f32[3,288]{1,0:T(4,128)} %bias_ref.3) | copy-start | bytes 10372
  38.6 1.6 %collective-permute-start = (bf16[128,864]{1,0:T(8,128)(2,1)S(1)}, bf16[128,864]{1,0:T(8,128)(2,1)S(1)}, u32[]{:S(2)}, u32[]{:S(2)}) collective-permute-start(bf16[128,864]{1,0:T(8,128)(2,1)S(1)} %get-tuple-element.20), channel_id=1, source_target_pairs={{0,1},{1,0},{2,3},{3,2},{4,5},{5,4},{6,7},{7,6},{8,9},{9,8},{10,11... | collective-permute-start | bytes 663560 | tf_op jit(solution)/shard_map/ppermute | solution.py:333
  77.8 1.5 %collective-permute-start.1 = (bf16[128,864]{1,0:T(8,128)(2,1)S(1)}, bf16[128,864]{1,0:T(8,128)(2,1)S(1)}, u32[]{:S(2)}, u32[]{:S(2)}) collective-permute-start(bf16[128,864]{1,0:T(8,128)(2,1)S(1)} %bitcast.19), channel_id=1, source_target_pairs={{0,1},{1,0},{2,3},{3,2},{4,5},{5,4},{6,7},{7,6},{8,9},{9,8},{10,11... | collective-permute-start | bytes 663560 | tf_op jit(solution)/shard_map/ppermute | solution.py:337
  96.8 16.1 %copy-start.2 = (bf16[3,256,288]{1,2,0:T(8,128)(2,1)S(1)}, bf16[3,256,288]{1,2,0:T(8,128)(2,1)}, u32[]{:S(2)}) copy-start(bf16[3,256,288]{1,2,0:T(8,128)(2,1)} %param.6) | copy-start | bytes 1327108

commit v8 on v7

--- a/solution.py
+++ b/solution.py
@@ -75,7 +75,7 @@
         out_ref[k, layers * tiles * rows :, :] = extra.astype(BF16)
 
 
-def on_chip(kernel, name, args, out_shape, scratch_shapes=()):
+def on_chip(kernel, name, args, out_shape, flops=None):
     vmem = pl.BlockSpec(memory_space=pltpu.VMEM)
     smem = pl.BlockSpec(memory_space=pltpu.SMEM)
     return pl.pallas_call(
@@ -83,8 +83,8 @@
         in_specs=[smem if arg.dtype == jnp.int32 else vmem for arg in args],
         out_specs=jax.tree.map(lambda _: vmem, out_shape),
         out_shape=out_shape,
-        scratch_shapes=scratch_shapes,
         compiler_params=pltpu.CompilerParams(vmem_limit_bytes=VMEM),
+        cost_estimate=flops and pl.CostEstimate(flops=flops, bytes_accessed=flops // 128, transcendentals=0),
         name=name,
     )(*args)
 
@@ -135,34 +135,32 @@
     )
 
 
-def decode_kernel(layers, core_ref, features_ref, weight_ref, theirs_ref, mine_ref, held_ref):
+def decode_kernel(layers, ours, core_ref, features_ref, weight_ref, out_ref):
     width, feature_dev = weight_ref.shape[1:]
-    half = theirs_ref.shape[0]
-    core = core_ref[0]
+    half = out_ref.shape[0]
+    side = core_ref[0] if ours else 1 - core_ref[0]
+    rows = pl.ds(pl.multiple_of(side * half, half), half)
     for b in range(layers):
         total = None
         for a in range(b + 1):
             term = contract(
-                features_ref[:, a * feature_dev : (a + 1) * feature_dev],
+                features_ref[rows, a * feature_dev : (a + 1) * feature_dev],
                 weight_ref[pair_number(a, b, layers)],
                 1,
                 1,
             )
             total = term if total is None else total + term
-        held_ref[:, b * width : (b + 1) * width] = total
-    for ref, side in ((theirs_ref, 1 - core), (mine_ref, core)):
-        ref[...] = held_ref[pl.ds(pl.multiple_of(side * half, half), half), :].astype(ref.dtype)
-
-
-def decode(core, features, dec_t, layers):
-    tokens = features.shape[0]
-    columns = layers * dec_t.shape[1]
-    return on_chip(
-        functools.partial(decode_kernel, layers),
-        "decode",
+        out_ref[:, b * width : (b + 1) * width] = total.astype(out_ref.dtype)
+
+
+def decode(core, features, dec_t, layers, ours):
+    half = features.shape[0] // 2
+    return on_chip(
+        functools.partial(decode_kernel, layers, ours),
+        "decode_ours" if ours else "decode_theirs",
         (core, features, dec_t),
-        [jax.ShapeDtypeStruct((tokens // 2, columns), kind) for kind in (BF16, F32)],
-        [pltpu.VMEM((tokens, columns), F32)],
+        jax.ShapeDtypeStruct((half, layers * dec_t.shape[1]), F32 if ours else BF16),
+        2 * half * dec_t.size,
     )
 
 
@@ -190,13 +188,8 @@
     )
 
 
-def upstream_kernel(layers, core_ref, mine_ref, theirs_ref, weight_ref, out_ref, error_ref):
+def upstream_rows(layers, error_ref, weight_ref, store):
     width, feature_dev = weight_ref.shape[1:]
-    slots = out_ref.shape[0]
-    half = mine_ref.shape[0]
-    core = core_ref[0]
-    for ref, side in ((mine_ref, core), (theirs_ref, 1 - core)):
-        error_ref[pl.ds(pl.multiple_of(side * half, half), half), :] = ref[...]
     for a in range(layers):
         total = None
         for b in range(a, layers):
@@ -204,27 +197,58 @@
                 error_ref[:, b * width : (b + 1) * width], weight_ref[pair_number(a, b, layers)], 1, 0
             )
             total = term if total is None else total + term
-        store_tiles(out_ref, total.astype(BF16), a * feature_dev // LANES, slots)
+        store(total.astype(BF16), a * feature_dev // LANES)
+
+
+def upstream_ours_kernel(layers, ours_ref, weight_ref, out_ref):
+    blocks = out_ref.shape[0]
+    upstream_rows(layers, ours_ref, weight_ref, lambda x, first: store_tiles(out_ref, x, first, blocks))
+
+
+def upstream_ours(ours, dec_t, layers, blocks):
+    half = ours.shape[0]
+    rows = half // blocks * layers * dec_t.shape[2] // LANES
+    return on_chip(
+        functools.partial(upstream_ours_kernel, layers),
+        "upstream_ours",
+        (ours, dec_t),
+        jax.ShapeDtypeStruct((blocks, rows, LANES), BF16),
+        2 * half * dec_t.size,
+    )
+
+
+def upstream_kernel(layers, core_ref, ours_ref, theirs_ref, sent_ref, weight_ref, out_ref, error_ref):
+    blocks, rows, _ = sent_ref.shape
+    half = ours_ref.shape[0]
+    core = core_ref[0]
+    for ref, side in ((ours_ref, core), (theirs_ref, 1 - core)):
+        error_ref[pl.ds(pl.multiple_of(side * half, half), half), :] = ref[...]
+    for k in range(blocks):
+        out_ref[core * blocks + k, :rows, :] = sent_ref[k]
+    other = out_ref.at[pl.ds((1 - core) * blocks, blocks)]
+    upstream_rows(layers, theirs_ref, weight_ref, lambda x, first: store_tiles(other, x, first, blocks))
     wide = error_ref[...].astype(F32)
     squared = jnp.sum(wide * wide)
     coarse = squared.astype(BF16).astype(F32)
     fine = squared - coarse
     lane = lax.broadcasted_iota(jnp.int32, (EXTRA, LANES), 1)
     extra = jnp.where(lane == 0, coarse, jnp.where(lane == 1, fine, 0.0)).astype(BF16)
-    for k in range(slots):
-        out_ref[k, out_ref.shape[1] - EXTRA :, :] = extra
-
-
-def upstream(core, mine, theirs, dec_t, layers, slots):
-    half, columns = mine.shape
+    for k in range(2 * blocks):
+        out_ref[k, rows:, :] = extra
+
+
+def upstream(core, ours, theirs, sent_ours, dec_t, layers):
+    half, columns = ours.shape
+    blocks = sent_ours.shape[0]
     return on_chip(
         functools.partial(upstream_kernel, layers),
         "upstream",
-        (core, mine, theirs, dec_t),
+        (core, ours, theirs, sent_ours, dec_t),
         [
-            sent_shape(slots, 2 * half, layers * dec_t.shape[2]),
+            sent_shape(2 * blocks, 2 * half, layers * dec_t.shape[2]),
             jax.ShapeDtypeStruct((2 * half, columns), BF16),
         ],
+        2 * half * dec_t.size,
     )
 
 
@@ -329,14 +353,15 @@
     own_features = own_features_of(exchange(sent, SLOT), enc_bias, tokens // slots)
     features = sent_to_all(own_features, SLOT).reshape(tokens, -1)
 
-    theirs, mine = decode(core, features, dec_t, layers)
-    chip_sum = (mine + lax.ppermute(theirs, CORE, [(0, 1), (1, 0)]).astype(F32)).astype(BF16)
+    swap = [(0, 1), (1, 0)]
+    from_core = lax.ppermute(decode(core, features, dec_t, layers, False), CORE, swap)
+    chip_sum = (decode(core, features, dec_t, layers, True) + from_core.astype(F32)).astype(BF16)
     arrived = exchange(chip_sum.reshape(chips, portion, -1), CHIPS)
     own_error = own_error_of(offset, arrived, jnp.transpose(acts_out, (0, 2, 1)), dec_bias)
     half_error = sent_to_all(own_error, CHIPS).reshape(half, -1)
-    other_error = lax.ppermute(half_error, CORE, [(0, 1), (1, 0)])
-
-    sent, error = upstream(core, half_error, other_error, dec_t, layers, slots)
+    other_error = lax.ppermute(half_error, CORE, swap)
+    sent_ours = upstream_ours(half_error, dec_t, layers, slots // 2)
+    sent, error = upstream(core, half_error, other_error, sent_ours, dec_t, layers)
     own_delta, mse = own_delta_of(exchange(sent, SLOT), own_features, 1.0 / (layers * tokens * D))
     delta = sent_to_all(own_delta, SLOT).reshape(tokens, -1)
     enc_grad, bias_grad, dec_grad_t = gradients(acts_t, delta, features, error)

time: 117 us -> 116 us (level)
  waiting for transfers between devices: 2.96 us -> 1.43 us
    ppermute x2, waiting for transfers between devices: 2.96 us -> 1.43 us  [the longest x1 0.87 us: local(): other_error = lax.ppermute(half_error, CORE, swap)]
    pallas_call x5 -> x7, Pallas kernels: 4.32 us -> 5.21 us  [on_chip(): pl.pallas_call(kernel, in_specs=[smem if arg.dtype == jnp.int32 else vmem...]
  transfers between devices with their start and end apart: 2 -> 2, of which waited for: 2 -> 2; matrix products, arithmetic and copies ran while one was open for 0% -> 0% of each run, Pallas kernels for 0% -> 1%
where the time goes in v8:
time: 116 us
  blocking collectives  102 us (88%)
  Pallas kernels  9.5 us (8%)
  local copies, waits for them, and re-layouts  2.34 us (2%)
  waiting for transfers between devices  1.43 us (1%)
    all_to_all x6, blocking collectives, exchange(): return lax.all_to_all(tiles, axis, split_axis=0, concat_axis=0, tiled=True)  102 us
    pallas_call x7, Pallas kernels, on_chip(): pl.pallas_call(kernel, in_specs=[smem if arg.dtype == jnp.int32 else vmem...  5.21 us
    pallas_call x1, Pallas kernels, gradients(): pl.pallas_call(gradients_kernel, in_specs=[vmem] * 4, out_specs=[anywhere...  3.48 us
  transfers between devices with their start and end apart: 2, of which 2 were waited for; matrix products, arithmetic and copies ran while one was open for 0% of the time, Pallas kernels for 1%

profile of v8, /device:TPU:32, one launch (start us, length us, event | category | flops | bytes accessed | tf_op | source)
XLA Modules:
  0.0 115.8 jit_solution(4894103383335847483)
XLA Ops:
  0.6 0.0 copy-start.1
  0.7 1.0 copy-done.1
  1.7 0.0 copy-start.3
  1.7 1.2 %copy-done.3 = bf16[3,288,512]{2,1,0:T(8,128)(2,1)S(1)} copy-done((bf16[3,288,512]{2,1,0:T(8,128)(2,1)S(1)}, bf16[3,288,512]{2,1,0:T(8,128)(2,1)}, u32[]{:S(2)}) %copy-start.3) | copy-done | bytes 884760
  2.8 0.0 copy-start.5
  2.8 1.2 %encode.1 = bf16[8,400,128]{2,1,0:T(8,128)(2,1)S(1)} custom-call(bf16[3,288,256]{2,1,0:T(8,128)(2,1)S(1)} %bitcast.23, bf16[3,288,512]{2,1,0:T(8,128)(2,1)S(1)} %copy-done.3), custom_call_target="tpu_custom_call" | custom-call | tf_op jit(solution)/shard_map/encode/pallas_call | solution.py:81
  4.0 18.6 %all_to_all.30.arrived_ref = bf16[8,400,128]{2,1,0:T(8,128)(2,1)S(1)} all-to-all(bf16[8,400,128]{2,1,0:T(8,128)(2,1)S(1)} %encode.1), channel_id=1, replica_groups=mesh['slot_0'=2,'slot_1'=4,'feat_0'=2,'feat_1'=8,'feat_2'=2] {'slot_0','..., dimensions={0} | all-to-all | bytes 1638400 | tf_op jit(solution)/shard_map/all_to_all | solution.py:28
  22.6 0.0 copy-done.5
  22.6 0.0 copy-start
  22.6 0.7 own_features.1.features_ref
  23.3 0.1 broadcast_in_dim.6
  23.4 14.1 %all_to_all.31 = bf16[8,32,1536]{2,1,0:T(8,128)(2,1)S(1)} all-to-all(bf16[8,32,1536]{2,1,0:T(8,128)(2,1)S(1)} %broadcast_in_dim.6), channel_id=1, replica_groups=mesh['slot_0'=2,'slot_1'=4,'feat_0'=2,'feat_1'=8,'feat_2'=2] {'slot_0','..., dimensions={0} | all-to-all | bytes 1572864 | tf_op jit(solution)/shard_map/all_to_all | solution.py:28
  37.5 0.0 copy-done
  37.5 0.9 decode_theirs.1
  38.4 0.0 copy-start.4
  38.4 0.0 copy-start.6
  38.4 0.1 collective-permute-start
  38.5 0.9 decode_ours.1
  39.4 0.6 collective-permute-done
  40.0 22.0 %all_to_all.32.arrived_ref = bf16[16,8,864]{2,1,0:T(8,128)(2,1)S(1)} all-to-all(bf16[16,8,864]{2,1,0:T(8,128)(2,1)S(1)} %fusion), channel_id=1, replica_groups=mesh['slot_0'=2,'slot_1'=4,'feat_0'=2,'feat_1'=8,'feat_2'=2] {'feat_0','..., dimensions={0} | all-to-all | bytes 442368 | tf_op jit(solution)/shard_map/all_to_all | solution.py:28
  62.0 0.0 copy-done.4
  62.0 0.0 copy-done.6
  62.0 0.3 own_error.1
  62.3 15.3 %all_to_all.33 = bf16[16,8,864]{2,1,0:T(8,128)(2,1)S(1)} all-to-all(bf16[16,8,864]{2,1,0:T(8,128)(2,1)S(1)} %broadcast_in_dim.7), channel_id=1, replica_groups=mesh['slot_0'=2,'slot_1'=4,'feat_0'=2,'feat_1'=8,'feat_2'=2] {'feat_0','..., dimensions={0} | all-to-all | bytes 442368 | tf_op jit(solution)/shard_map/all_to_all | solution.py:28
  77.6 0.0 collective-permute-start.1
  77.6 0.6 upstream_ours.1.sent_ref
  78.3 0.9 collective-permute-done.1.theirs_ref
  79.1 0.6 upstream.1
  79.8 16.4 %all_to_all.34.arrived_ref = bf16[8,400,128]{2,1,0:T(8,128)(2,1)S(1)} all-to-all(bf16[8,400,128]{2,1,0:T(8,128)(2,1)S(1)} %get-tuple-element.17), channel_id=1, replica_groups=mesh['slot_0'=2,'slot_1'=4,'feat_0'=2,'feat_1'=8,'feat_2'=2] {'slot_0','..., dimensions={0} | all-to-all | bytes 1638400 | tf_op jit(solution)/shard_map/all_to_all | solution.py:28
  96.2 0.0 copy-start.2
  96.2 0.8 own_delta.1
  97.0 0.1 broadcast_in_dim.8
  97.1 15.2 %all_to_all.35 = bf16[8,32,1536]{2,1,0:T(8,128)(2,1)S(1)} all-to-all(bf16[8,32,1536]{2,1,0:T(8,128)(2,1)S(1)} %broadcast_in_dim.8), channel_id=1, replica_groups=mesh['slot_0'=2,'slot_1'=4,'feat_0'=2,'feat_1'=8,'feat_2'=2] {'slot_0','..., dimensions={0} | all-to-all | bytes 1572864 | tf_op jit(solution)/shard_map/all_to_all | solution.py:28
  112.3 0.0 copy-done.2
  112.3 3.5 %gradients.1 = (f32[3,288,512]{2,1,0:T(8,128)}, f32[3,512]{1,0:T(4,128)}, f32[6,288,512]{2,1,0:T(8,128)}) custom-call(bf16[3,288,256]{2,1,0:T(8,128)(2,1)S(1)} %bitcast.24, bf16[256,1536]{1,0:T(8,128)(2,1)S(1)} %bitcast.19, bf16[256,1536]{1,0:T(8,128)(2,1)S(1)} %bitcast.18, bf16[256,864]{1,0:T(8,128)(2,1)S(1)} %get-tuple-element.19.error_ref), custom_call_target="tpu_custom_call" | custom-call | tf_op jit(solution)/shard_map/gradients/pallas_call | solution.py:321
  (2 shorter events, 0.1 us)
Async XLA Ops:
  0.6 1.0 copy-start.1
  1.7 1.2 %copy-start.3 = (bf16[3,288,512]{2,1,0:T(8,128)(2,1)S(1)}, bf16[3,288,512]{2,1,0:T(8,128)(2,1)}, u32[]{:S(2)}) copy-start(bf16[3,288,512]{2,1,0:T(8,128)(2,1)} %weight_ref.1) | copy-start | bytes 2654212
  2.8 19.8 %copy-start.5 = (f32[3,512]{1,0:T(4,128)S(1)}, f32[3,512]{1,0:T(4,128)}, u32[]{:S(2)}) copy-start(f32[3,512]{1,0:T(4,128)} %bias_ref.2) | copy-start | bytes 18436
  22.6 14.9 %copy-start = (bf16[6,512,288]{1,2,0:T(8,128)(2,1)S(1)}, bf16[6,512,288]{1,2,0:T(8,128)(2,1)}, u32[]{:S(2)}) copy-start(bf16[6,512,288]{1,2,0:T(8,128)(2,1)} %param.10) | copy-start | bytes 5308420
  38.4 23.6 %copy-start.4 = (bf16[3,256,288]{1,2,0:T(8,128)(2,1)S(1)}, bf16[3,256,288]{1,2,0:T(8,128)(2,1)}, u32[]{:S(2)}) copy-start(bf16[3,256,288]{1,2,0:T(8,128)(2,1)} %param.7) | copy-start | bytes 1327108
  38.4 23.6 %copy-start.6 = (f32[3,288]{1,0:T(4,128)S(1)}, f32[3,288]{1,0:T(4,128)}, u32[]{:S(2)}) copy-start(f32[3,288]{1,0:T(4,128)} %bias_ref.3) | copy-start | bytes 10372
  38.4 1.6 %collective-permute-start = (bf16[128,864]{1,0:T(8,128)(2,1)S(1)}, bf16[128,864]{1,0:T(8,128)(2,1)S(1)}, u32[]{:S(2)}, u32[]{:S(2)}) collective-permute-start(bf16[128,864]{1,0:T(8,128)(2,1)S(1)} %decode_theirs.1), channel_id=1, source_target_pairs={{0,1},{1,0},{2,3},{3,2},{4,5},{5,4},{6,7},{7,6},{8,9},{9,8},{10,11... | collective-permute-start | bytes 663560 | tf_op jit(solution)/shard_map/ppermute | solution.py:357
  77.6 1.5 %collective-permute-start.1 = (bf16[128,864]{1,0:T(8,128)(2,1)S(1)}, bf16[128,864]{1,0:T(8,128)(2,1)S(1)}, u32[]{:S(2)}, u32[]{:S(2)}) collective-permute-start(bf16[128,864]{1,0:T(8,128)(2,1)S(1)} %bitcast.20), channel_id=1, source_target_pairs={{0,1},{1,0},{2,3},{3,2},{4,5},{5,4},{6,7},{7,6},{8,9},{9,8},{10,11... | collective-permute-start | bytes 663560 | tf_op jit(solution)/shard_map/ppermute | solution.py:362
  96.2 16.1 %copy-start.2 = (bf16[3,256,288]{1,2,0:T(8,128)(2,1)S(1)}, bf16[3,256,288]{1,2,0:T(8,128)(2,1)}, u32[]{:S(2)}) copy-start(bf16[3,256,288]{1,2,0:T(8,128)(2,1)} %param.6) | copy-start | bytes 1327108

commit v9 on v8

--- a/solution.py
+++ b/solution.py
@@ -16,6 +16,7 @@
 LANES = 128
 EXTRA = 16
 VMEM = 16 * 2**20
+ALONE = 56 * 2**20
 OCTAVES = 250.0
 ABOVE = 1.0078125
 TINY = 1e-30
@@ -49,14 +50,22 @@
             ]
 
 
-def encode_kernel(acts_ref, weight_ref, out_ref):
+def encode_kernel(acts_hbm, weight_hbm, out_ref, acts_ref, weight_ref, acts_sems, weight_sems):
     layers = acts_ref.shape[0]
+    arriving = []
+    for a in range(layers):
+        for source, held, sems in ((weight_hbm, weight_ref, weight_sems), (acts_hbm, acts_ref, acts_sems)):
+            copy = pltpu.make_async_copy(source.at[a], held.at[a], sems.at[a])
+            copy.start()
+            arriving.append(copy)
     feature_dev = weight_ref.shape[2]
     slots = out_ref.shape[0]
     rows = acts_ref.shape[2] // slots
     tiles = feature_dev // LANES
     scales = []
     for a in range(layers):
+        arriving[2 * a].wait()
+        arriving[2 * a + 1].wait()
         preact = contract(acts_ref[a], weight_ref[a], 0, 0)
         size = jnp.abs(preact)
         largest = jnp.maximum(jnp.max(size, axis=1, keepdims=True), TINY)
@@ -96,7 +105,21 @@
 def encode(acts_t, enc_weight, slots):
     layers, _, tokens = acts_t.shape
     shape = sent_shape(slots, tokens, layers * enc_weight.shape[2])
-    return on_chip(encode_kernel, "encode", (acts_t, enc_weight), shape)
+    anywhere = pl.BlockSpec(memory_space=pl.ANY)
+    return pl.pallas_call(
+        encode_kernel,
+        in_specs=[anywhere, anywhere],
+        out_specs=pl.BlockSpec(memory_space=pltpu.VMEM),
+        out_shape=pltpu.VMEM(shape.shape, shape.dtype),
+        scratch_shapes=[
+            pltpu.VMEM(acts_t.shape, BF16),
+            pltpu.VMEM(enc_weight.shape, BF16),
+            pltpu.SemaphoreType.DMA((layers,)),
+            pltpu.SemaphoreType.DMA((layers,)),
+        ],
+        compiler_params=pltpu.CompilerParams(vmem_limit_bytes=ALONE),
+        name="encode",
+    )(acts_t, enc_weight)
 
 
 def features_kernel(arrived_ref, bias_ref, own_ref):
@@ -252,7 +275,7 @@
     )
 
 
-def delta_kernel(share, arrived_ref, features_ref, own_ref, mse_ref):
+def delta_kernel(arrived_ref, features_ref, own_ref, extra_ref):
     slots = arrived_ref.shape[0]
     rows, columns = features_ref.shape
     total = arrived_ref[0].astype(F32)
@@ -263,77 +286,77 @@
         delta = jnp.where(features_ref[:, at] > 0, total[j * rows : (j + 1) * rows, :], 0.0)
         own_ref[:, at] = delta.astype(BF16)
     last = columns // LANES * rows
-    mse_ref[0, 0] = jnp.sum(total[last : last + 1, :]) * share
-
-
-def own_delta_of(arrived, own_features, share):
-    vmem = pl.BlockSpec(memory_space=pltpu.VMEM)
-    return pl.pallas_call(
-        functools.partial(delta_kernel, share),
-        in_specs=[vmem, vmem],
-        out_specs=[vmem, pl.BlockSpec(memory_space=pltpu.SMEM)],
-        out_shape=[
-            jax.ShapeDtypeStruct(own_features.shape, BF16),
-            jax.ShapeDtypeStruct((1, 1), F32),
-        ],
-        compiler_params=pltpu.CompilerParams(vmem_limit_bytes=VMEM),
-        name="own_delta",
-    )(arrived, own_features)
+    extra_ref[...] = total[last : last + EXTRA, :]
+
+
+def own_delta_of(arrived, own_features):
+    return on_chip(
+        delta_kernel,
+        "own_delta",
+        (arrived, own_features),
+        [pltpu.VMEM(own_features.shape, BF16), pltpu.VMEM((EXTRA, LANES), F32)],
+    )
 
 
 def gradients_kernel(
-    acts_ref, delta_ref, features_ref, error_ref,
-    enc_hbm, bias_ref, dec_hbm, enc_held, dec_held, enc_sems, dec_sems,
+    share, acts_ref, delta_ref, features_ref, error_ref, extra_ref,
+    enc_hbm, bias_hbm, dec_hbm, mse_hbm,
+    enc_held, bias_held, dec_held, mse_held, enc_sems, dec_sems, small_sems,
 ):
     layers, width, tokens = acts_ref.shape
     feature_dev = enc_held.shape[2]
     leaving = []
 
-    def send(held, out, sems, k):
-        copy = pltpu.make_async_copy(held.at[k], out.at[k], sems.at[k])
+    def send(held, out, sem):
+        copy = pltpu.make_async_copy(held, out, sem)
         copy.start()
         leaving.append(copy)
 
-    for a in range(layers):
-        columns = slice(a * feature_dev, (a + 1) * feature_dev)
+    def layer(a):
+        return slice(a * feature_dev, (a + 1) * feature_dev)
+
+    for a in range(layers):
         for b in range(a, layers):
             pair = pair_number(a, b, layers)
-            dec_held[pair] = contract(error_ref[:, b * width : (b + 1) * width], features_ref[:, columns], 0, 0)
-            send(dec_held, dec_hbm, dec_sems, pair)
+            dec_held[pair] = contract(
+                error_ref[:, b * width : (b + 1) * width], features_ref[:, layer(a)], 0, 0
+            )
+            send(dec_held.at[pair], dec_hbm.at[pair], dec_sems.at[pair])
+    mse_held[...] = jnp.sum(extra_ref[:1, :], axis=1, keepdims=True) * share
+    send(mse_held, mse_hbm, small_sems.at[0])
     ones = jnp.ones((8, tokens), BF16)
     for a in range(layers):
-        delta = delta_ref[:, a * feature_dev : (a + 1) * feature_dev]
-        enc_held[a] = contract(acts_ref[a], delta, 1, 0)
-        send(enc_held, enc_hbm, enc_sems, a)
-        bias_ref[a : a + 1, :] = contract(ones, delta, 1, 0)[:1]
+        bias_held[a : a + 1, :] = contract(ones, delta_ref[:, layer(a)], 1, 0)[:1]
+    send(bias_held, bias_hbm, small_sems.at[1])
+    for a in range(layers):
+        enc_held[a] = contract(acts_ref[a], delta_ref[:, layer(a)], 1, 0)
+        send(enc_held.at[a], enc_hbm.at[a], enc_sems.at[a])
     for copy in leaving:
         copy.wait()
 
 
-def gradients(acts_t, delta, features, error):
-    layers, width, tokens = acts_t.shape
+def gradients(acts_t, delta, features, error, extra, share):
+    layers, width, _ = acts_t.shape
     feature_dev = delta.shape[1] // layers
     pairs = layers * (layers + 1) // 2
     vmem = pl.BlockSpec(memory_space=pltpu.VMEM)
     anywhere = pl.BlockSpec(memory_space=pl.ANY)
-    enc_shape = (layers, width, feature_dev)
-    dec_shape = (pairs, width, feature_dev)
+    shapes = (
+        (layers, width, feature_dev),
+        (layers, feature_dev),
+        (pairs, width, feature_dev),
+        (1, 1),
+    )
     return pl.pallas_call(
-        gradients_kernel,
-        in_specs=[vmem] * 4,
-        out_specs=[anywhere, vmem, anywhere],
-        out_shape=[
-            jax.ShapeDtypeStruct(shape, F32) for shape in (enc_shape, (layers, feature_dev), dec_shape)
-        ],
-        scratch_shapes=[
-            pltpu.VMEM(enc_shape, F32),
-            pltpu.VMEM(dec_shape, F32),
-            pltpu.SemaphoreType.DMA((layers,)),
-            pltpu.SemaphoreType.DMA((pairs,)),
-        ],
+        functools.partial(gradients_kernel, share),
+        in_specs=[vmem] * 5,
+        out_specs=[anywhere] * 4,
+        out_shape=[jax.ShapeDtypeStruct(shape, F32) for shape in shapes],
+        scratch_shapes=[pltpu.VMEM(shape, F32) for shape in shapes]
+        + [pltpu.SemaphoreType.DMA((count,)) for count in (layers, pairs, 2)],
         compiler_params=pltpu.CompilerParams(vmem_limit_bytes=VMEM),
         name="gradients",
-    )(acts_t, delta, features, error)
+    )(acts_t, delta, features, error, extra)
 
 
 def local(acts_in, acts_out, enc_weight, enc_bias, dec_weight, dec_bias):
@@ -362,9 +385,10 @@
     other_error = lax.ppermute(half_error, CORE, swap)
     sent_ours = upstream_ours(half_error, dec_t, layers, slots // 2)
     sent, error = upstream(core, half_error, other_error, sent_ours, dec_t, layers)
-    own_delta, mse = own_delta_of(exchange(sent, SLOT), own_features, 1.0 / (layers * tokens * D))
+    own_delta, extra = own_delta_of(exchange(sent, SLOT), own_features)
     delta = sent_to_all(own_delta, SLOT).reshape(tokens, -1)
-    enc_grad, bias_grad, dec_grad_t = gradients(acts_t, delta, features, error)
+    share = 1.0 / (layers * tokens * D)
+    enc_grad, bias_grad, dec_grad_t, mse = gradients(acts_t, delta, features, error, extra, share)
     return (enc_grad, bias_grad, jnp.transpose(dec_grad_t, (0, 2, 1)), mse.reshape(()))
 
 

time: 116 us -> 114 us (0.983)
  local copies, waits for them, and re-layouts: 2.34 us -> 0.16 us
    unnamed x14 -> x10, local copies, waits for them, and re-layouts: 2.2 us -> 0.02 us
    pallas_call x2, Pallas kernels: 4.28 us -> 5.71 us  [the longest x1 2.91 us: gradients(): pl.pallas_call(functools.partial(gradients_kernel, share), in_specs=[vmem...]
where the time goes in v9:
time: 114 us
  blocking collectives  102 us (89%)
  Pallas kernels  9.89 us (9%)
  waiting for transfers between devices  1.43 us (1%)
    all_to_all x6, blocking collectives, exchange(): return lax.all_to_all(tiles, axis, split_axis=0, concat_axis=0, tiled=True)  102 us
    pallas_call x7, Pallas kernels, on_chip(): pl.pallas_call(kernel, in_specs=[smem if arg.dtype == jnp.int32 else vmem...  4.18 us
    pallas_call x1, Pallas kernels, gradients(): pl.pallas_call(functools.partial(gradients_kernel, share), in_specs=[vmem...  2.91 us
    pallas_call x1, Pallas kernels, encode(): pl.pallas_call(encode_kernel, in_specs=[anywhere, anywhere], out_specs=pl...  2.8 us
  transfers between devices with their start and end apart: 2, of which 2 were waited for; matrix products, arithmetic and copies ran while one was open for 0% of the time, Pallas kernels for 1%

profile of v9, /device:TPU:32, one launch (start us, length us, event | category | flops | bytes accessed | tf_op | source)
XLA Modules:
  0.0 114.0 jit_solution(4944392033533493072)
XLA Ops:
  0.6 0.0 copy-start.3
  0.7 2.8 %encode.1 = bf16[8,400,128]{2,1,0:T(8,128)(2,1)S(1)} custom-call(bf16[3,288,256]{2,1,0:T(8,128)(2,1)} %bitcast.23, bf16[3,288,512]{2,1,0:T(8,128)(2,1)} %weight_hbm.1), custom_call_target="tpu_custom_call" | custom-call | tf_op jit(solution)/shard_map/encode/pallas_call | solution.py:109
  3.5 18.6 %all_to_all.30.arrived_ref = bf16[8,400,128]{2,1,0:T(8,128)(2,1)S(1)} all-to-all(bf16[8,400,128]{2,1,0:T(8,128)(2,1)S(1)} %encode.1), channel_id=1, replica_groups=mesh['slot_0'=2,'slot_1'=4,'feat_0'=2,'feat_1'=8,'feat_2'=2] {'slot_0','..., dimensions={0} | all-to-all | bytes 1638400 | tf_op jit(solution)/shard_map/all_to_all | solution.py:29
  22.1 0.0 copy-done.3
  22.1 0.0 copy-start
  22.1 0.7 own_features.1.features_ref
  22.7 0.1 broadcast_in_dim.6
  22.8 14.1 %all_to_all.31 = bf16[8,32,1536]{2,1,0:T(8,128)(2,1)S(1)} all-to-all(bf16[8,32,1536]{2,1,0:T(8,128)(2,1)S(1)} %broadcast_in_dim.6), channel_id=1, replica_groups=mesh['slot_0'=2,'slot_1'=4,'feat_0'=2,'feat_1'=8,'feat_2'=2] {'slot_0','..., dimensions={0} | all-to-all | bytes 1572864 | tf_op jit(solution)/shard_map/all_to_all | solution.py:29
  36.9 0.0 copy-done
  36.9 0.9 decode_theirs.1
  37.8 0.0 copy-start.2
  37.8 0.0 copy-start.4
  37.8 0.1 collective-permute-start
  37.9 0.9 decode_ours.1
  38.9 0.6 collective-permute-done
  39.5 22.0 %all_to_all.32.arrived_ref = bf16[16,8,864]{2,1,0:T(8,128)(2,1)S(1)} all-to-all(bf16[16,8,864]{2,1,0:T(8,128)(2,1)S(1)} %fusion), channel_id=1, replica_groups=mesh['slot_0'=2,'slot_1'=4,'feat_0'=2,'feat_1'=8,'feat_2'=2] {'feat_0','..., dimensions={0} | all-to-all | bytes 442368 | tf_op jit(solution)/shard_map/all_to_all | solution.py:29
  61.4 0.0 copy-done.2
  61.4 0.0 copy-done.4
  61.4 0.3 own_error.1
  61.8 15.3 %all_to_all.33 = bf16[16,8,864]{2,1,0:T(8,128)(2,1)S(1)} all-to-all(bf16[16,8,864]{2,1,0:T(8,128)(2,1)S(1)} %broadcast_in_dim.7), channel_id=1, replica_groups=mesh['slot_0'=2,'slot_1'=4,'feat_0'=2,'feat_1'=8,'feat_2'=2] {'feat_0','..., dimensions={0} | all-to-all | bytes 442368 | tf_op jit(solution)/shard_map/all_to_all | solution.py:29
  77.1 0.0 collective-permute-start.1
  77.1 0.6 upstream_ours.1.sent_ref
  77.7 0.9 collective-permute-done.1.theirs_ref
  78.6 0.6 upstream.1
  79.2 16.4 %all_to_all.34.arrived_ref = bf16[8,400,128]{2,1,0:T(8,128)(2,1)S(1)} all-to-all(bf16[8,400,128]{2,1,0:T(8,128)(2,1)S(1)} %get-tuple-element.18), channel_id=1, replica_groups=mesh['slot_0'=2,'slot_1'=4,'feat_0'=2,'feat_1'=8,'feat_2'=2] {'slot_0','..., dimensions={0} | all-to-all | bytes 1638400 | tf_op jit(solution)/shard_map/all_to_all | solution.py:29
  95.6 0.0 copy-start.1
  95.7 0.1 own_delta.1
  95.8 0.1 broadcast_in_dim.8
  95.9 15.2 %all_to_all.35 = bf16[8,32,1536]{2,1,0:T(8,128)(2,1)S(1)} all-to-all(bf16[8,32,1536]{2,1,0:T(8,128)(2,1)S(1)} %broadcast_in_dim.8), channel_id=1, replica_groups=mesh['slot_0'=2,'slot_1'=4,'feat_0'=2,'feat_1'=8,'feat_2'=2] {'slot_0','..., dimensions={0} | all-to-all | bytes 1572864 | tf_op jit(solution)/shard_map/all_to_all | solution.py:29
  111.1 0.0 copy-done.1
  111.1 2.9 %gradients.1 = (f32[3,288,512]{2,1,0:T(8,128)}, f32[3,512]{1,0:T(4,128)}, f32[6,288,512]{2,1,0:T(8,128)}, f32[1,1]{1,0:T(1,128)}) custom-call(bf16[3,288,256]{2,1,0:T(8,128)(2,1)S(1)} %bitcast.24, bf16[256,1536]{1,0:T(8,128)(2,1)S(1)} %bitcast.19, bf16[256,1536]{1,0:T(8,128)(2,1)S(1)} %bitcast.18, bf16[256,864]{1,0:T(8,128)(2,1)S(1)} %get-tuple-element.20.error_ref, ...), custom_call_target="tpu_custom_call" | custom-call | tf_op jit(solution)/shard_map/gradients/pallas_call | solution.py:350
  (2 shorter events, 0.1 us)
Async XLA Ops:
  0.6 21.4 %copy-start.3 = (f32[3,512]{1,0:T(4,128)S(1)}, f32[3,512]{1,0:T(4,128)}, u32[]{:S(2)}) copy-start(f32[3,512]{1,0:T(4,128)} %bias_ref.2) | copy-start | bytes 18436
  22.1 14.9 %copy-start = (bf16[6,512,288]{1,2,0:T(8,128)(2,1)S(1)}, bf16[6,512,288]{1,2,0:T(8,128)(2,1)}, u32[]{:S(2)}) copy-start(bf16[6,512,288]{1,2,0:T(8,128)(2,1)} %param.10) | copy-start | bytes 5308420
  37.8 23.6 %copy-start.2 = (bf16[3,256,288]{1,2,0:T(8,128)(2,1)S(1)}, bf16[3,256,288]{1,2,0:T(8,128)(2,1)}, u32[]{:S(2)}) copy-start(bf16[3,256,288]{1,2,0:T(8,128)(2,1)} %param.7) | copy-start | bytes 1327108
  37.8 23.6 %copy-start.4 = (f32[3,288]{1,0:T(4,128)S(1)}, f32[3,288]{1,0:T(4,128)}, u32[]{:S(2)}) copy-start(f32[3,288]{1,0:T(4,128)} %bias_ref.3) | copy-start | bytes 10372
  37.8 1.6 %collective-permute-start = (bf16[128,864]{1,0:T(8,128)(2,1)S(1)}, bf16[128,864]{1,0:T(8,128)(2,1)S(1)}, u32[]{:S(2)}, u32[]{:S(2)}) collective-permute-start(bf16[128,864]{1,0:T(8,128)(2,1)S(1)} %decode_theirs.1), channel_id=1, source_target_pairs={{0,1},{1,0},{2,3},{3,2},{4,5},{5,4},{6,7},{7,6},{8,9},{9,8},{10,11... | collective-permute-start | bytes 663560 | tf_op jit(solution)/shard_map/ppermute | solution.py:380
  77.1 1.5 %collective-permute-start.1 = (bf16[128,864]{1,0:T(8,128)(2,1)S(1)}, bf16[128,864]{1,0:T(8,128)(2,1)S(1)}, u32[]{:S(2)}, u32[]{:S(2)}) collective-permute-start(bf16[128,864]{1,0:T(8,128)(2,1)S(1)} %bitcast.20), channel_id=1, source_target_pairs={{0,1},{1,0},{2,3},{3,2},{4,5},{5,4},{6,7},{7,6},{8,9},{9,8},{10,11... | collective-permute-start | bytes 663560 | tf_op jit(solution)/shard_map/ppermute | solution.py:385
  95.6 15.4 %copy-start.1 = (bf16[3,256,288]{1,2,0:T(8,128)(2,1)S(1)}, bf16[3,256,288]{1,2,0:T(8,128)(2,1)}, u32[]{:S(2)}) copy-start(bf16[3,256,288]{1,2,0:T(8,128)(2,1)} %param.6) | copy-start | bytes 1327108

commit v10 on v9

--- a/solution.py
+++ b/solution.py
@@ -15,6 +15,7 @@
 CORE = "feat_2"
 LANES = 128
 EXTRA = 16
+EARLY = 1
 VMEM = 16 * 2**20
 ALONE = 56 * 2**20
 OCTAVES = 250.0
@@ -240,7 +241,28 @@
     )
 
 
-def upstream_kernel(layers, core_ref, ours_ref, theirs_ref, sent_ref, weight_ref, out_ref, error_ref):
+def decoder_grads(layers, error_ref, features_ref, held_ref, out_hbm, sems):
+    width, feature_dev = held_ref.shape[1:]
+    copies = []
+    for a in range(layers):
+        for b in range(a, layers):
+            pair = pair_number(a, b, layers)
+            held_ref[pair] = contract(
+                error_ref[:, b * width : (b + 1) * width],
+                features_ref[:, a * feature_dev : (a + 1) * feature_dev],
+                0,
+                0,
+            )
+            copy = pltpu.make_async_copy(held_ref.at[pair], out_hbm.at[pair], sems.at[pair])
+            copy.start()
+            copies.append(copy)
+    return copies
+
+
+def upstream_kernel(
+    layers, core_ref, ours_ref, theirs_ref, sent_ref, weight_ref, features_ref,
+    out_ref, error_ref, grad_hbm, held_ref, sems,
+):
     blocks, rows, _ = sent_ref.shape
     half = ours_ref.shape[0]
     core = core_ref[0]
@@ -259,20 +281,30 @@
     for k in range(2 * blocks):
         out_ref[k, rows:, :] = extra
 
-
-def upstream(core, ours, theirs, sent_ours, dec_t, layers):
+    @pl.when(core == EARLY)
+    def _():
+        for copy in decoder_grads(layers, error_ref, features_ref, held_ref, grad_hbm, sems):
+            copy.wait()
+
+
+def upstream(core, ours, theirs, sent_ours, dec_t, features, layers):
     half, columns = ours.shape
     blocks = sent_ours.shape[0]
-    return on_chip(
+    vmem = pl.BlockSpec(memory_space=pltpu.VMEM)
+    sent = sent_shape(2 * blocks, 2 * half, layers * dec_t.shape[2])
+    return pl.pallas_call(
         functools.partial(upstream_kernel, layers),
-        "upstream",
-        (core, ours, theirs, sent_ours, dec_t),
-        [
-            sent_shape(2 * blocks, 2 * half, layers * dec_t.shape[2]),
-            jax.ShapeDtypeStruct((2 * half, columns), BF16),
+        in_specs=[pl.BlockSpec(memory_space=pltpu.SMEM)] + [vmem] * 5,
+        out_specs=[vmem, vmem, pl.BlockSpec(memory_space=pl.ANY)],
+        out_shape=[
+            pltpu.VMEM(sent.shape, BF16),
+            pltpu.VMEM((2 * half, columns), BF16),
+            jax.ShapeDtypeStruct(dec_t.shape, F32),
         ],
-        2 * half * dec_t.size,
-    )
+        scratch_shapes=[pltpu.VMEM(dec_t.shape, F32), pltpu.SemaphoreType.DMA((dec_t.shape[0],))],
+        compiler_params=pltpu.CompilerParams(vmem_limit_bytes=VMEM),
+        name="upstream",
+    )(core, ours, theirs, sent_ours, dec_t, features)
 
 
 def delta_kernel(arrived_ref, features_ref, own_ref, extra_ref):
@@ -299,12 +331,14 @@
 
 
 def gradients_kernel(
-    share, acts_ref, delta_ref, features_ref, error_ref, extra_ref,
+    share, core_ref, acts_ref, delta_ref, features_ref, error_ref, extra_ref, early_hbm,
     enc_hbm, bias_hbm, dec_hbm, mse_hbm,
     enc_held, bias_held, dec_held, mse_held, enc_sems, dec_sems, small_sems,
 ):
-    layers, width, tokens = acts_ref.shape
+    del early_hbm
+    layers, _, tokens = acts_ref.shape
     feature_dev = enc_held.shape[2]
+    late = core_ref[0] != EARLY
     leaving = []
 
     def send(held, out, sem):
@@ -315,13 +349,10 @@
     def layer(a):
         return slice(a * feature_dev, (a + 1) * feature_dev)
 
-    for a in range(layers):
-        for b in range(a, layers):
-            pair = pair_number(a, b, layers)
-            dec_held[pair] = contract(
-                error_ref[:, b * width : (b + 1) * width], features_ref[:, layer(a)], 0, 0
-            )
-            send(dec_held.at[pair], dec_hbm.at[pair], dec_sems.at[pair])
+    @pl.when(late)
+    def _():
+        decoder_grads(layers, error_ref, features_ref, dec_held, dec_hbm, dec_sems)
+
     mse_held[...] = jnp.sum(extra_ref[:1, :], axis=1, keepdims=True) * share
     send(mse_held, mse_hbm, small_sems.at[0])
     ones = jnp.ones((8, tokens), BF16)
@@ -334,8 +365,13 @@
     for copy in leaving:
         copy.wait()
 
-
-def gradients(acts_t, delta, features, error, extra, share):
+    @pl.when(late)
+    def _():
+        for pair in range(dec_held.shape[0]):
+            pltpu.make_async_copy(dec_held.at[pair], dec_hbm.at[pair], dec_sems.at[pair]).wait()
+
+
+def gradients(core, acts_t, delta, features, error, extra, dec_grad_t, share):
     layers, width, _ = acts_t.shape
     feature_dev = delta.shape[1] // layers
     pairs = layers * (layers + 1) // 2
@@ -349,14 +385,15 @@
     )
     return pl.pallas_call(
         functools.partial(gradients_kernel, share),
-        in_specs=[vmem] * 5,
+        in_specs=[pl.BlockSpec(memory_space=pltpu.SMEM)] + [vmem] * 5 + [anywhere],
         out_specs=[anywhere] * 4,
         out_shape=[jax.ShapeDtypeStruct(shape, F32) for shape in shapes],
         scratch_shapes=[pltpu.VMEM(shape, F32) for shape in shapes]
         + [pltpu.SemaphoreType.DMA((count,)) for count in (layers, pairs, 2)],
+        input_output_aliases={6: 2},
         compiler_params=pltpu.CompilerParams(vmem_limit_bytes=VMEM),
         name="gradients",
-    )(acts_t, delta, features, error, extra)
+    )(core, acts_t, delta, features, error, extra, dec_grad_t)
 
 
 def local(acts_in, acts_out, enc_weight, enc_bias, dec_weight, dec_bias):
@@ -384,11 +421,13 @@
     half_error = sent_to_all(own_error, CHIPS).reshape(half, -1)
     other_error = lax.ppermute(half_error, CORE, swap)
     sent_ours = upstream_ours(half_error, dec_t, layers, slots // 2)
-    sent, error = upstream(core, half_error, other_error, sent_ours, dec_t, layers)
+    sent, error, early = upstream(core, half_error, other_error, sent_ours, dec_t, features, layers)
     own_delta, extra = own_delta_of(exchange(sent, SLOT), own_features)
     delta = sent_to_all(own_delta, SLOT).reshape(tokens, -1)
     share = 1.0 / (layers * tokens * D)
-    enc_grad, bias_grad, dec_grad_t, mse = gradients(acts_t, delta, features, error, extra, share)
+    enc_grad, bias_grad, dec_grad_t, mse = gradients(
+        core, acts_t, delta, features, error, extra, early, share
+    )
     return (enc_grad, bias_grad, jnp.transpose(dec_grad_t, (0, 2, 1)), mse.reshape(()))
 
 

time: 114 us -> 115 us (level)
    pallas_call x1 -> x2, Pallas kernels: 2.91 us -> 3.57 us  [the longest x1 2.86 us: gradients(): pl.pallas_call(functools.partial(gradients_kernel, share), in_specs=[pl.B...]
    pallas_call x7 -> x6, Pallas kernels: 4.18 us -> 3.55 us  [on_chip(): pl.pallas_call(kernel, in_specs=[smem if arg.dtype == jnp.int32 else vmem...]
where the time goes in v10:
time: 115 us
  blocking collectives  102 us (89%)
  Pallas kernels  10 us (9%)
  waiting for transfers between devices  1.42 us (1%)
    all_to_all x6, blocking collectives, exchange(): return lax.all_to_all(tiles, axis, split_axis=0, concat_axis=0, tiled=True)  102 us
    pallas_call x6, Pallas kernels, on_chip(): pl.pallas_call(kernel, in_specs=[smem if arg.dtype == jnp.int32 else vmem...  3.55 us
    pallas_call x1, Pallas kernels, encode(): pl.pallas_call(encode_kernel, in_specs=[anywhere, anywhere], out_specs=pl...  2.92 us
    pallas_call x1, Pallas kernels, gradients(): pl.pallas_call(functools.partial(gradients_kernel, share), in_specs=[pl.B...  2.86 us
  transfers between devices with their start and end apart: 2, of which 2 were waited for; matrix products, arithmetic and copies ran while one was open for 0% of the time, Pallas kernels for 1%

profile of v10, /device:TPU:32, one launch (start us, length us, event | category | flops | bytes accessed | tf_op | source)
XLA Modules:
  0.0 114.9 jit_solution(11920056699518420536)
XLA Ops:
  0.6 0.0 copy-start.3
  0.7 0.0 copy-start
  0.7 2.9 %encode.1 = bf16[8,400,128]{2,1,0:T(8,128)(2,1)S(1)} custom-call(bf16[3,288,256]{2,1,0:T(8,128)(2,1)} %bitcast.24, bf16[3,288,512]{2,1,0:T(8,128)(2,1)} %weight_hbm.1), custom_call_target="tpu_custom_call" | custom-call | tf_op jit(solution)/shard_map/encode/pallas_call | solution.py:110
  3.6 18.6 %all_to_all.30.arrived_ref = bf16[8,400,128]{2,1,0:T(8,128)(2,1)S(1)} all-to-all(bf16[8,400,128]{2,1,0:T(8,128)(2,1)S(1)} %encode.1), channel_id=1, replica_groups=mesh['slot_0'=2,'slot_1'=4,'feat_0'=2,'feat_1'=8,'feat_2'=2] {'slot_0','..., dimensions={0} | all-to-all | bytes 1638400 | tf_op jit(solution)/shard_map/all_to_all | solution.py:30
  22.2 0.0 copy-done.3
  22.2 0.7 own_features.1.features_ref
  22.9 0.1 broadcast_in_dim.6
  22.9 14.1 %all_to_all.31 = bf16[8,32,1536]{2,1,0:T(8,128)(2,1)S(1)} all-to-all(bf16[8,32,1536]{2,1,0:T(8,128)(2,1)S(1)} %broadcast_in_dim.6), channel_id=1, replica_groups=mesh['slot_0'=2,'slot_1'=4,'feat_0'=2,'feat_1'=8,'feat_2'=2] {'slot_0','..., dimensions={0} | all-to-all | bytes 1572864 | tf_op jit(solution)/shard_map/all_to_all | solution.py:30
  37.1 0.0 copy-done
  37.1 0.0 copy-start.2
  37.1 0.0 copy-start.4
  37.1 0.9 decode_theirs.1
  38.0 0.1 collective-permute-start
  38.1 0.9 decode_ours.1
  39.0 0.6 collective-permute-done
  39.5 0.1 fusion
  39.6 22.0 %all_to_all.32.arrived_ref = bf16[16,8,864]{2,1,0:T(8,128)(2,1)S(1)} all-to-all(bf16[16,8,864]{2,1,0:T(8,128)(2,1)S(1)} %fusion), channel_id=1, replica_groups=mesh['slot_0'=2,'slot_1'=4,'feat_0'=2,'feat_1'=8,'feat_2'=2] {'feat_0','..., dimensions={0} | all-to-all | bytes 442368 | tf_op jit(solution)/shard_map/all_to_all | solution.py:30
  61.6 0.0 copy-done.2
  61.6 0.0 copy-done.4
  61.6 0.3 own_error.1
  61.9 15.3 %all_to_all.33 = bf16[16,8,864]{2,1,0:T(8,128)(2,1)S(1)} all-to-all(bf16[16,8,864]{2,1,0:T(8,128)(2,1)S(1)} %broadcast_in_dim.7), channel_id=1, replica_groups=mesh['slot_0'=2,'slot_1'=4,'feat_0'=2,'feat_1'=8,'feat_2'=2] {'feat_0','..., dimensions={0} | all-to-all | bytes 442368 | tf_op jit(solution)/shard_map/all_to_all | solution.py:30
  77.2 0.0 collective-permute-start.1
  77.2 0.6 upstream_ours.1.sent_ref
  77.8 0.0 copy-start.1
  77.9 0.8 collective-permute-done.1.theirs_ref
  78.7 0.7 upstream.1
  79.4 15.9 %all_to_all.34.arrived_ref = bf16[8,400,128]{2,1,0:T(8,128)(2,1)S(1)} all-to-all(bf16[8,400,128]{2,1,0:T(8,128)(2,1)S(1)} %get-tuple-element.19), channel_id=1, replica_groups=mesh['slot_0'=2,'slot_1'=4,'feat_0'=2,'feat_1'=8,'feat_2'=2] {'slot_0','..., dimensions={0} | all-to-all | bytes 1638400 | tf_op jit(solution)/shard_map/all_to_all | solution.py:30
  95.3 0.1 own_delta.1
  95.5 0.1 broadcast_in_dim.8
  95.6 16.5 %all_to_all.35 = bf16[8,32,1536]{2,1,0:T(8,128)(2,1)S(1)} all-to-all(bf16[8,32,1536]{2,1,0:T(8,128)(2,1)S(1)} %broadcast_in_dim.8), channel_id=1, replica_groups=mesh['slot_0'=2,'slot_1'=4,'feat_0'=2,'feat_1'=8,'feat_2'=2] {'slot_0','..., dimensions={0} | all-to-all | bytes 1572864 | tf_op jit(solution)/shard_map/all_to_all | solution.py:30
  112.1 0.0 copy-done.1
  112.1 2.9 %gradients.1 = (f32[3,288,512]{2,1,0:T(8,128)}, f32[3,512]{1,0:T(4,128)}, f32[6,288,512]{2,1,0:T(8,128)}, f32[1,1]{1,0:T(1,128)}) custom-call(s32[1]{0:T(128)} %bitcast.1.core_ref, bf16[3,288,256]{2,1,0:T(8,128)(2,1)S(1)} %bitcast.25, bf16[256,1536]{1,0:T(8,128)(2,1)S(1)} %bitcast.20, ...), custom_call_target="tpu_custom_call", output_to_operand_aliasing={{2}: (6, {})} | custom-call | tf_op jit(solution)/shard_map/gradients/pallas_call | solution.py:386
  (1 shorter events, 0.0 us)
Async XLA Ops:
  0.6 21.6 %copy-start.3 = (f32[3,512]{1,0:T(4,128)S(1)}, f32[3,512]{1,0:T(4,128)}, u32[]{:S(2)}) copy-start(f32[3,512]{1,0:T(4,128)} %bias_ref.2) | copy-start | bytes 18436
  0.7 36.4 %copy-start = (bf16[6,512,288]{1,2,0:T(8,128)(2,1)S(1)}, bf16[6,512,288]{1,2,0:T(8,128)(2,1)}, u32[]{:S(2)}) copy-start(bf16[6,512,288]{1,2,0:T(8,128)(2,1)} %param.10) | copy-start | bytes 5308420
  37.1 24.5 %copy-start.2 = (bf16[3,256,288]{1,2,0:T(8,128)(2,1)S(1)}, bf16[3,256,288]{1,2,0:T(8,128)(2,1)}, u32[]{:S(2)}) copy-start(bf16[3,256,288]{1,2,0:T(8,128)(2,1)} %param.7) | copy-start | bytes 1327108
  37.1 24.5 %copy-start.4 = (f32[3,288]{1,0:T(4,128)S(1)}, f32[3,288]{1,0:T(4,128)}, u32[]{:S(2)}) copy-start(f32[3,288]{1,0:T(4,128)} %bias_ref.3) | copy-start | bytes 10372
  38.0 1.6 %collective-permute-start = (bf16[128,864]{1,0:T(8,128)(2,1)S(1)}, bf16[128,864]{1,0:T(8,128)(2,1)S(1)}, u32[]{:S(2)}, u32[]{:S(2)}) collective-permute-start(bf16[128,864]{1,0:T(8,128)(2,1)S(1)} %decode_theirs.1), channel_id=1, source_target_pairs={{0,1},{1,0},{2,3},{3,2},{4,5},{5,4},{6,7},{7,6},{8,9},{9,8},{10,11... | collective-permute-start | bytes 663560 | tf_op jit(solution)/shard_map/ppermute | solution.py:417
  77.2 1.5 %collective-permute-start.1 = (bf16[128,864]{1,0:T(8,128)(2,1)S(1)}, bf16[128,864]{1,0:T(8,128)(2,1)S(1)}, u32[]{:S(2)}, u32[]{:S(2)}) collective-permute-start(bf16[128,864]{1,0:T(8,128)(2,1)S(1)} %bitcast.21), channel_id=1, source_target_pairs={{0,1},{1,0},{2,3},{3,2},{4,5},{5,4},{6,7},{7,6},{8,9},{9,8},{10,11... | collective-permute-start | bytes 663560 | tf_op jit(solution)/shard_map/ppermute | solution.py:422
  77.8 34.2 %copy-start.1 = (bf16[3,256,288]{1,2,0:T(8,128)(2,1)S(1)}, bf16[3,256,288]{1,2,0:T(8,128)(2,1)}, u32[]{:S(2)}) copy-start(bf16[3,256,288]{1,2,0:T(8,128)(2,1)} %param.6) | copy-start | bytes 1327108

commit v11 on v9

--- a/solution.py
+++ b/solution.py
@@ -84,7 +84,7 @@
         out_ref[k, layers * tiles * rows :, :] = extra.astype(BF16)
 
 
-def on_chip(kernel, name, args, out_shape, flops=None):
+def on_chip(kernel, name, args, out_shape, scratch_shapes=()):
     vmem = pl.BlockSpec(memory_space=pltpu.VMEM)
     smem = pl.BlockSpec(memory_space=pltpu.SMEM)
     return pl.pallas_call(
@@ -93,7 +93,7 @@
         out_specs=jax.tree.map(lambda _: vmem, out_shape),
         out_shape=out_shape,
         compiler_params=pltpu.CompilerParams(vmem_limit_bytes=VMEM),
-        cost_estimate=flops and pl.CostEstimate(flops=flops, bytes_accessed=flops // 128, transcendentals=0),
+        scratch_shapes=scratch_shapes,
         name=name,
     )(*args)
 
@@ -158,32 +158,34 @@
     )
 
 
-def decode_kernel(layers, ours, core_ref, features_ref, weight_ref, out_ref):
+def decode_kernel(layers, core_ref, features_ref, weight_ref, theirs_ref, ours_ref, held_ref):
     width, feature_dev = weight_ref.shape[1:]
-    half = out_ref.shape[0]
-    side = core_ref[0] if ours else 1 - core_ref[0]
-    rows = pl.ds(pl.multiple_of(side * half, half), half)
+    chips, cores, rows, _ = held_ref.shape
+    core = core_ref[0]
     for b in range(layers):
         total = None
         for a in range(b + 1):
             term = contract(
-                features_ref[rows, a * feature_dev : (a + 1) * feature_dev],
+                features_ref[:, a * feature_dev : (a + 1) * feature_dev],
                 weight_ref[pair_number(a, b, layers)],
                 1,
                 1,
             )
             total = term if total is None else total + term
-        out_ref[:, b * width : (b + 1) * width] = total.astype(out_ref.dtype)
-
-
-def decode(core, features, dec_t, layers, ours):
-    half = features.shape[0] // 2
-    return on_chip(
-        functools.partial(decode_kernel, layers, ours),
-        "decode_ours" if ours else "decode_theirs",
+        held_ref[:, :, :, b * width : (b + 1) * width] = total.reshape(chips, cores, rows, width)
+    for ref, side in ((theirs_ref, 1 - core), (ours_ref, core)):
+        ref[...] = held_ref[:, side].reshape(ref.shape).astype(ref.dtype)
+
+
+def decode(core, features, dec_t, layers, chips):
+    tokens = features.shape[0]
+    columns = layers * dec_t.shape[1]
+    return on_chip(
+        functools.partial(decode_kernel, layers),
+        "decode",
         (core, features, dec_t),
-        jax.ShapeDtypeStruct((half, layers * dec_t.shape[1]), F32 if ours else BF16),
-        2 * half * dec_t.size,
+        [jax.ShapeDtypeStruct((tokens // 2, columns), kind) for kind in (BF16, F32)],
+        [pltpu.VMEM((chips, 2, tokens // chips // 2, columns), F32)],
     )
 
 
@@ -211,8 +213,9 @@
     )
 
 
-def upstream_rows(layers, error_ref, weight_ref, store):
+def upstream_kernel(layers, error_ref, weight_ref, out_ref):
     width, feature_dev = weight_ref.shape[1:]
+    slots = out_ref.shape[0]
     for a in range(layers):
         total = None
         for b in range(a, layers):
@@ -220,58 +223,23 @@
                 error_ref[:, b * width : (b + 1) * width], weight_ref[pair_number(a, b, layers)], 1, 0
             )
             total = term if total is None else total + term
-        store(total.astype(BF16), a * feature_dev // LANES)
-
-
-def upstream_ours_kernel(layers, ours_ref, weight_ref, out_ref):
-    blocks = out_ref.shape[0]
-    upstream_rows(layers, ours_ref, weight_ref, lambda x, first: store_tiles(out_ref, x, first, blocks))
-
-
-def upstream_ours(ours, dec_t, layers, blocks):
-    half = ours.shape[0]
-    rows = half // blocks * layers * dec_t.shape[2] // LANES
-    return on_chip(
-        functools.partial(upstream_ours_kernel, layers),
-        "upstream_ours",
-        (ours, dec_t),
-        jax.ShapeDtypeStruct((blocks, rows, LANES), BF16),
-        2 * half * dec_t.size,
-    )
-
-
-def upstream_kernel(layers, core_ref, ours_ref, theirs_ref, sent_ref, weight_ref, out_ref, error_ref):
-    blocks, rows, _ = sent_ref.shape
-    half = ours_ref.shape[0]
-    core = core_ref[0]
-    for ref, side in ((ours_ref, core), (theirs_ref, 1 - core)):
-        error_ref[pl.ds(pl.multiple_of(side * half, half), half), :] = ref[...]
-    for k in range(blocks):
-        out_ref[core * blocks + k, :rows, :] = sent_ref[k]
-    other = out_ref.at[pl.ds((1 - core) * blocks, blocks)]
-    upstream_rows(layers, theirs_ref, weight_ref, lambda x, first: store_tiles(other, x, first, blocks))
+        store_tiles(out_ref, total.astype(BF16), a * feature_dev // LANES, slots)
     wide = error_ref[...].astype(F32)
     squared = jnp.sum(wide * wide)
     coarse = squared.astype(BF16).astype(F32)
     fine = squared - coarse
     lane = lax.broadcasted_iota(jnp.int32, (EXTRA, LANES), 1)
     extra = jnp.where(lane == 0, coarse, jnp.where(lane == 1, fine, 0.0)).astype(BF16)
-    for k in range(2 * blocks):
-        out_ref[k, rows:, :] = extra
-
-
-def upstream(core, ours, theirs, sent_ours, dec_t, layers):
-    half, columns = ours.shape
-    blocks = sent_ours.shape[0]
+    for k in range(slots):
+        out_ref[k, out_ref.shape[1] - EXTRA :, :] = extra
+
+
+def upstream(error, dec_t, layers, slots):
     return on_chip(
         functools.partial(upstream_kernel, layers),
         "upstream",
-        (core, ours, theirs, sent_ours, dec_t),
-        [
-            sent_shape(2 * blocks, 2 * half, layers * dec_t.shape[2]),
-            jax.ShapeDtypeStruct((2 * half, columns), BF16),
-        ],
-        2 * half * dec_t.size,
+        (error, dec_t),
+        sent_shape(slots, error.shape[0], layers * dec_t.shape[2]),
     )
 
 
@@ -367,24 +335,27 @@
     acts_t = jnp.transpose(acts_in, (0, 2, 1))
     dec_t = jnp.transpose(dec_weight, (0, 2, 1))
 
-    half = tokens // 2
-    portion = half // chips
+    portion = tokens // chips // 2
     core = core.reshape(1)
-    offset = core * half + lax.axis_index(CHIPS) * portion
+    offset = (lax.axis_index(CHIPS) * 2 + core) * portion
     sent = encode(acts_t, enc_weight, slots)
     sent, core, offset = lax.optimization_barrier((sent, core, offset))
     own_features = own_features_of(exchange(sent, SLOT), enc_bias, tokens // slots)
     features = sent_to_all(own_features, SLOT).reshape(tokens, -1)
 
     swap = [(0, 1), (1, 0)]
-    from_core = lax.ppermute(decode(core, features, dec_t, layers, False), CORE, swap)
-    chip_sum = (decode(core, features, dec_t, layers, True) + from_core.astype(F32)).astype(BF16)
+    theirs, ours = decode(core, features, dec_t, layers, chips)
+    chip_sum = (ours + lax.ppermute(theirs, CORE, swap).astype(F32)).astype(BF16)
     arrived = exchange(chip_sum.reshape(chips, portion, -1), CHIPS)
     own_error = own_error_of(offset, arrived, jnp.transpose(acts_out, (0, 2, 1)), dec_bias)
-    half_error = sent_to_all(own_error, CHIPS).reshape(half, -1)
-    other_error = lax.ppermute(half_error, CORE, swap)
-    sent_ours = upstream_ours(half_error, dec_t, layers, slots // 2)
-    sent, error = upstream(core, half_error, other_error, sent_ours, dec_t, layers)
+    other_error = lax.ppermute(own_error, CORE, swap)
+    first = core[0] == 0
+    chip_error = jnp.concatenate(
+        [jnp.where(first, own_error, other_error), jnp.where(first, other_error, own_error)], axis=0
+    )
+    error = sent_to_all(chip_error, CHIPS).reshape(tokens, -1)
+
+    sent = upstream(error, dec_t, layers, slots)
     own_delta, extra = own_delta_of(exchange(sent, SLOT), own_features)
     delta = sent_to_all(own_delta, SLOT).reshape(tokens, -1)
     share = 1.0 / (layers * tokens * D)

time: 114 us -> 114 us (level)
  waiting for transfers between devices: 1.43 us -> 2.64 us
    ppermute x2, waiting for transfers between devices: 1.43 us -> 2.64 us  [the longest x1 1.48 us: local(): lax.ppermute(theirs, CORE, swap).astype(F32)]
    pallas_call x7 -> x5, Pallas kernels: 4.18 us -> 3.24 us  [on_chip(): pl.pallas_call(kernel, in_specs=[smem if arg.dtype == jnp.int32 else vmem...]
  transfers between devices with their start and end apart: 2 -> 2, of which waited for: 2 -> 2; matrix products, arithmetic and copies ran while one was open for 0% -> 0% of each run, Pallas kernels for 1% -> 0%
where the time goes in v11:
time: 114 us
  blocking collectives  101 us (89%)
  Pallas kernels  8.94 us (8%)
  waiting for transfers between devices  2.64 us (2%)
    all_to_all x6, blocking collectives, exchange(): return lax.all_to_all(tiles, axis, split_axis=0, concat_axis=0, tiled=True)  101 us
    pallas_call x5, Pallas kernels, on_chip(): pl.pallas_call(kernel, in_specs=[smem if arg.dtype == jnp.int32 else vmem...  3.24 us
    pallas_call x1, Pallas kernels, gradients(): pl.pallas_call(functools.partial(gradients_kernel, share), in_specs=[vmem...  2.9 us
    pallas_call x1, Pallas kernels, encode(): pl.pallas_call(encode_kernel, in_specs=[anywhere, anywhere], out_specs=pl...  2.8 us
  transfers between devices with their start and end apart: 2, of which 2 were waited for; matrix products, arithmetic and copies ran while one was open for 0% of the time, Pallas kernels for 0%

profile of v11, /device:TPU:32, one launch (start us, length us, event | category | flops | bytes accessed | tf_op | source)
XLA Modules:
  0.0 113.8 jit_solution(3754798883568963054)
XLA Ops:
  0.6 0.0 copy-start.3
  0.7 2.8 %encode.1 = bf16[8,400,128]{2,1,0:T(8,128)(2,1)S(1)} custom-call(bf16[3,288,256]{2,1,0:T(8,128)(2,1)} %bitcast.20, bf16[3,288,512]{2,1,0:T(8,128)(2,1)} %weight_hbm.1), custom_call_target="tpu_custom_call" | custom-call | tf_op jit(solution)/shard_map/encode/pallas_call | solution.py:109
  3.5 18.6 %all_to_all.30.arrived_ref = bf16[8,400,128]{2,1,0:T(8,128)(2,1)S(1)} all-to-all(bf16[8,400,128]{2,1,0:T(8,128)(2,1)S(1)} %encode.1), channel_id=1, replica_groups=mesh['slot_0'=2,'slot_1'=4,'feat_0'=2,'feat_1'=8,'feat_2'=2] {'slot_0','..., dimensions={0} | all-to-all | bytes 1638400 | tf_op jit(solution)/shard_map/all_to_all | solution.py:29
  22.1 0.0 copy-done.3
  22.1 0.0 copy-start
  22.1 0.7 own_features.1.features_ref
  22.7 0.1 broadcast_in_dim.6
  22.8 14.1 %all_to_all.31 = bf16[8,32,1536]{2,1,0:T(8,128)(2,1)S(1)} all-to-all(bf16[8,32,1536]{2,1,0:T(8,128)(2,1)S(1)} %broadcast_in_dim.6), channel_id=1, replica_groups=mesh['slot_0'=2,'slot_1'=4,'feat_0'=2,'feat_1'=8,'feat_2'=2] {'slot_0','..., dimensions={0} | all-to-all | bytes 1572864 | tf_op jit(solution)/shard_map/all_to_all | solution.py:29
  36.9 0.0 copy-done
  36.9 0.0 copy-start.2
  36.9 0.0 copy-start.4
  36.9 1.1 decode.1
  38.0 0.1 collective-permute-start
  38.1 1.5 %collective-permute-done = bf16[128,864]{1,0:T(8,128)(2,1)S(1)} collective-permute-done((bf16[128,864]{1,0:T(8,128)(2,1)S(1)}, bf16[128,864]{1,0:T(8,128)(2,1)S(1)}, u32[]{:S(2)}, u32[]{:S(2)}) %collective-permute-start) | collective-permute-done | bytes 221216 | tf_op jit(solution)/shard_map/ppermute | solution.py:348
  39.7 22.0 %all_to_all.32.arrived_ref = bf16[16,8,864]{2,1,0:T(8,128)(2,1)S(1)} all-to-all(bf16[16,8,864]{2,1,0:T(8,128)(2,1)S(1)} %fusion), channel_id=1, replica_groups=mesh['slot_0'=2,'slot_1'=4,'feat_0'=2,'feat_1'=8,'feat_2'=2] {'feat_0','..., dimensions={0} | all-to-all | bytes 442368 | tf_op jit(solution)/shard_map/all_to_all | solution.py:29
  61.6 0.0 copy-done.2
  61.6 0.0 copy-done.4
  61.6 0.3 own_error.1
  62.0 0.1 collective-permute-start.1
  62.0 1.2 %collective-permute-done.1 = bf16[8,864]{1,0:T(8,128)(2,1)S(1)} collective-permute-done((bf16[8,864]{1,0:T(8,128)(2,1)S(1)}, bf16[8,864]{1,0:T(8,128)(2,1)S(1)}, u32[]{:S(2)}, u32[]{:S(2)}) %collective-permute-start.1) | collective-permute-done | bytes 13856 | tf_op jit(solution)/shard_map/ppermute | solution.py:351
  63.2 19.7 %all_to_all.33 = bf16[16,16,864]{2,1,0:T(8,128)(2,1)S(1)} all-to-all(bf16[16,16,864]{2,1,0:T(8,128)(2,1)S(1)} %broadcast_in_dim.7), channel_id=1, replica_groups=mesh['slot_0'=2,'slot_1'=4,'feat_0'=2,'feat_1'=8,'feat_2'=2] {'feat_0','..., dimensions={0} | all-to-all | bytes 884736 | tf_op jit(solution)/shard_map/all_to_all | solution.py:29
  82.9 1.0 upstream.1
  83.9 14.2 %all_to_all.34.arrived_ref = bf16[8,400,128]{2,1,0:T(8,128)(2,1)S(1)} all-to-all(bf16[8,400,128]{2,1,0:T(8,128)(2,1)S(1)} %upstream.1), channel_id=1, replica_groups=mesh['slot_0'=2,'slot_1'=4,'feat_0'=2,'feat_1'=8,'feat_2'=2] {'slot_0','..., dimensions={0} | all-to-all | bytes 1638400 | tf_op jit(solution)/shard_map/all_to_all | solution.py:29
  98.1 0.0 copy-start.1
  98.1 0.1 own_delta.1
  98.3 0.1 broadcast_in_dim.8
  98.3 12.5 %all_to_all.35 = bf16[8,32,1536]{2,1,0:T(8,128)(2,1)S(1)} all-to-all(bf16[8,32,1536]{2,1,0:T(8,128)(2,1)S(1)} %broadcast_in_dim.8), channel_id=1, replica_groups=mesh['slot_0'=2,'slot_1'=4,'feat_0'=2,'feat_1'=8,'feat_2'=2] {'slot_0','..., dimensions={0} | all-to-all | bytes 1572864 | tf_op jit(solution)/shard_map/all_to_all | solution.py:29
  110.9 0.0 copy-done.1
  110.9 2.9 %gradients.1 = (f32[3,288,512]{2,1,0:T(8,128)}, f32[3,512]{1,0:T(4,128)}, f32[6,288,512]{2,1,0:T(8,128)}, f32[1,1]{1,0:T(1,128)}) custom-call(bf16[3,288,256]{2,1,0:T(8,128)(2,1)S(1)} %bitcast.21, bf16[256,1536]{1,0:T(8,128)(2,1)S(1)} %bitcast.19, bf16[256,1536]{1,0:T(8,128)(2,1)S(1)} %bitcast.16, bf16[256,864]{1,0:T(8,128)(2,1)S(1)} %bitcast.18, ...), custom_call_target="tpu_custom_call" | custom-call | tf_op jit(solution)/shard_map/gradients/pallas_call | solution.py:318
  (4 shorter events, 0.1 us)
Async XLA Ops:
  0.6 21.4 %copy-start.3 = (f32[3,512]{1,0:T(4,128)S(1)}, f32[3,512]{1,0:T(4,128)}, u32[]{:S(2)}) copy-start(f32[3,512]{1,0:T(4,128)} %bias_ref.2) | copy-start | bytes 18436
  22.1 14.9 %copy-start = (bf16[6,512,288]{1,2,0:T(8,128)(2,1)S(1)}, bf16[6,512,288]{1,2,0:T(8,128)(2,1)}, u32[]{:S(2)}) copy-start(bf16[6,512,288]{1,2,0:T(8,128)(2,1)} %param.10) | copy-start | bytes 5308420
  36.9 24.7 %copy-start.2 = (bf16[3,256,288]{1,2,0:T(8,128)(2,1)S(1)}, bf16[3,256,288]{1,2,0:T(8,128)(2,1)}, u32[]{:S(2)}) copy-start(bf16[3,256,288]{1,2,0:T(8,128)(2,1)} %param.7) | copy-start | bytes 1327108
  36.9 24.7 %copy-start.4 = (f32[3,288]{1,0:T(4,128)S(1)}, f32[3,288]{1,0:T(4,128)}, u32[]{:S(2)}) copy-start(f32[3,288]{1,0:T(4,128)} %bias_ref.3) | copy-start | bytes 10372
  38.0 1.6 %collective-permute-start = (bf16[128,864]{1,0:T(8,128)(2,1)S(1)}, bf16[128,864]{1,0:T(8,128)(2,1)S(1)}, u32[]{:S(2)}, u32[]{:S(2)}) collective-permute-start(bf16[128,864]{1,0:T(8,128)(2,1)S(1)} %get-tuple-element.19), channel_id=1, source_target_pairs={{0,1},{1,0},{2,3},{3,2},{4,5},{5,4},{6,7},{7,6},{8,9},{9,8},{10,11... | collective-permute-start | bytes 663560 | tf_op jit(solution)/shard_map/ppermute | solution.py:348
  62.0 1.2 %collective-permute-start.1 = (bf16[8,864]{1,0:T(8,128)(2,1)S(1)}, bf16[8,864]{1,0:T(8,128)(2,1)S(1)}, u32[]{:S(2)}, u32[]{:S(2)}) collective-permute-start(bf16[8,864]{1,0:T(8,128)(2,1)S(1)} %own_error.1), channel_id=1, source_target_pairs={{0,1},{1,0},{2,3},{3,2},{4,5},{5,4},{6,7},{7,6},{8,9},{9,8},{10,11... | collective-permute-start | bytes 41480 | tf_op jit(solution)/shard_map/ppermute | solution.py:351
  98.1 12.7 %copy-start.1 = (bf16[3,256,288]{1,2,0:T(8,128)(2,1)S(1)}, bf16[3,256,288]{1,2,0:T(8,128)(2,1)}, u32[]{:S(2)}) copy-start(bf16[3,256,288]{1,2,0:T(8,128)(2,1)} %param.6) | copy-start | bytes 1327108

commit v12 on v9

--- a/solution.py
+++ b/solution.py
@@ -211,100 +211,119 @@
     )
 
 
-def upstream_rows(layers, error_ref, weight_ref, store):
-    width, feature_dev = weight_ref.shape[1:]
-    for a in range(layers):
-        total = None
-        for b in range(a, layers):
-            term = contract(
-                error_ref[:, b * width : (b + 1) * width], weight_ref[pair_number(a, b, layers)], 1, 0
-            )
-            total = term if total is None else total + term
-        store(total.astype(BF16), a * feature_dev // LANES)
-
-
-def upstream_ours_kernel(layers, ours_ref, weight_ref, out_ref):
-    blocks = out_ref.shape[0]
-    upstream_rows(layers, ours_ref, weight_ref, lambda x, first: store_tiles(out_ref, x, first, blocks))
-
-
-def upstream_ours(ours, dec_t, layers, blocks):
-    half = ours.shape[0]
-    rows = half // blocks * layers * dec_t.shape[2] // LANES
-    return on_chip(
-        functools.partial(upstream_ours_kernel, layers),
-        "upstream_ours",
-        (ours, dec_t),
-        jax.ShapeDtypeStruct((blocks, rows, LANES), BF16),
-        2 * half * dec_t.size,
-    )
-
-
-def upstream_kernel(layers, core_ref, ours_ref, theirs_ref, sent_ref, weight_ref, out_ref, error_ref):
-    blocks, rows, _ = sent_ref.shape
-    half = ours_ref.shape[0]
-    core = core_ref[0]
-    for ref, side in ((ours_ref, core), (theirs_ref, 1 - core)):
-        error_ref[pl.ds(pl.multiple_of(side * half, half), half), :] = ref[...]
-    for k in range(blocks):
-        out_ref[core * blocks + k, :rows, :] = sent_ref[k]
-    other = out_ref.at[pl.ds((1 - core) * blocks, blocks)]
-    upstream_rows(layers, theirs_ref, weight_ref, lambda x, first: store_tiles(other, x, first, blocks))
+def upstream_kernel(layers, error_ref, ours_ref, theirs_ref, out_ref):
+    width, feature_dev = ours_ref.shape[1:]
+    slots = out_ref.shape[0]
+    tiles = feature_dev // LANES
+    for side, weight_ref in enumerate((ours_ref, theirs_ref)):
+        for a in range(layers):
+            total = None
+            for b in range(a, layers):
+                term = contract(
+                    error_ref[:, b * width : (b + 1) * width], weight_ref[pair_number(a, b, layers)], 1, 0
+                )
+                total = term if total is None else total + term
+            store_tiles(out_ref, total.astype(BF16), (side * layers + a) * tiles, slots)
     wide = error_ref[...].astype(F32)
     squared = jnp.sum(wide * wide)
     coarse = squared.astype(BF16).astype(F32)
     fine = squared - coarse
     lane = lax.broadcasted_iota(jnp.int32, (EXTRA, LANES), 1)
     extra = jnp.where(lane == 0, coarse, jnp.where(lane == 1, fine, 0.0)).astype(BF16)
-    for k in range(2 * blocks):
-        out_ref[k, rows:, :] = extra
-
-
-def upstream(core, ours, theirs, sent_ours, dec_t, layers):
-    half, columns = ours.shape
-    blocks = sent_ours.shape[0]
+    for k in range(slots):
+        out_ref[k, out_ref.shape[1] - EXTRA :, :] = extra
+
+
+def upstream(error, dec_t, other_dec_t, layers, slots):
     return on_chip(
         functools.partial(upstream_kernel, layers),
         "upstream",
-        (core, ours, theirs, sent_ours, dec_t),
-        [
-            sent_shape(2 * blocks, 2 * half, layers * dec_t.shape[2]),
-            jax.ShapeDtypeStruct((2 * half, columns), BF16),
-        ],
-        2 * half * dec_t.size,
-    )
-
-
-def delta_kernel(arrived_ref, features_ref, own_ref, extra_ref):
+        (error, dec_t, other_dec_t),
+        sent_shape(slots, error.shape[0], 2 * layers * dec_t.shape[2]),
+    )
+
+
+def delta_kernel(arrived_ref, ours_ref, theirs_ref, own_ref, extra_ref):
     slots = arrived_ref.shape[0]
-    rows, columns = features_ref.shape
+    rows, columns = ours_ref.shape
     total = arrived_ref[0].astype(F32)
     for k in range(1, slots):
         total = total + arrived_ref[k].astype(F32)
-    for j in range(columns // LANES):
-        at = slice(j * LANES, (j + 1) * LANES)
-        delta = jnp.where(features_ref[:, at] > 0, total[j * rows : (j + 1) * rows, :], 0.0)
-        own_ref[:, at] = delta.astype(BF16)
-    last = columns // LANES * rows
-    extra_ref[...] = total[last : last + EXTRA, :]
-
-
-def own_delta_of(arrived, own_features):
+    tiles = columns // LANES
+    for side, features_ref in enumerate((ours_ref, theirs_ref)):
+        for j in range(tiles):
+            at = (side * tiles + j) * rows
+            delta = jnp.where(
+                features_ref[:, j * LANES : (j + 1) * LANES] > 0, total[at : at + rows, :], 0.0
+            )
+            own_ref[side, :, j * LANES : (j + 1) * LANES] = delta.astype(BF16)
+    extra_ref[...] = total[2 * tiles * rows :, :]
+
+
+def own_delta_of(arrived, ours, theirs):
     return on_chip(
         delta_kernel,
         "own_delta",
-        (arrived, own_features),
-        [pltpu.VMEM(own_features.shape, BF16), pltpu.VMEM((EXTRA, LANES), F32)],
-    )
-
-
-def gradients_kernel(
-    share, acts_ref, delta_ref, features_ref, error_ref, extra_ref,
-    enc_hbm, bias_hbm, dec_hbm, mse_hbm,
-    enc_held, bias_held, dec_held, mse_held, enc_sems, dec_sems, small_sems,
+        (arrived, ours, theirs),
+        [pltpu.VMEM((2, *ours.shape), BF16), pltpu.VMEM((EXTRA, LANES), F32)],
+    )
+
+
+def join(held_ref, core, ours_ref, theirs_ref):
+    half = held_ref.shape[0] // 2
+    for ref, side in ((ours_ref, core), (theirs_ref, 1 - core)):
+        held_ref[pl.ds(pl.multiple_of(side * half, half), half), :] = ref[...].reshape(half, -1)
+
+
+def decoder_grad_kernel(layers, core_ref, ours_ref, theirs_ref, features_ref, out_hbm, error_ref, held_ref, sems):
+    width, feature_dev = held_ref.shape[1:]
+    join(error_ref, core_ref[0], ours_ref, theirs_ref)
+    leaving = []
+    for a in range(layers):
+        for b in range(a, layers):
+            pair = pair_number(a, b, layers)
+            held_ref[pair] = contract(
+                error_ref[:, b * width : (b + 1) * width],
+                features_ref[:, a * feature_dev : (a + 1) * feature_dev],
+                0,
+                0,
+            )
+            copy = pltpu.make_async_copy(held_ref.at[pair], out_hbm.at[pair], sems.at[pair])
+            copy.start()
+            leaving.append(copy)
+    for copy in leaving:
+        copy.wait()
+
+
+def decoder_grad(core, ours, theirs, features, layers):
+    tokens = features.shape[0]
+    pairs = layers * (layers + 1) // 2
+    shape = (pairs, ours.shape[1] // layers, features.shape[1] // layers)
+    vmem = pl.BlockSpec(memory_space=pltpu.VMEM)
+    return pl.pallas_call(
+        functools.partial(decoder_grad_kernel, layers),
+        in_specs=[pl.BlockSpec(memory_space=pltpu.SMEM)] + [vmem] * 3,
+        out_specs=pl.BlockSpec(memory_space=pl.ANY),
+        out_shape=jax.ShapeDtypeStruct(shape, F32),
+        scratch_shapes=[
+            pltpu.VMEM((tokens, ours.shape[1]), BF16),
+            pltpu.VMEM(shape, F32),
+            pltpu.SemaphoreType.DMA((pairs,)),
+        ],
+        compiler_params=pltpu.CompilerParams(vmem_limit_bytes=VMEM),
+        cost_estimate=pl.CostEstimate(flops=2**29, bytes_accessed=2**22, transcendentals=0),
+        name="decoder_grad",
+    )(core, ours, theirs, features)
+
+
+def encoder_grad_kernel(
+    share, core_ref, acts_ref, ours_ref, theirs_ref, extra_ref, other_extra_ref,
+    enc_hbm, bias_hbm, mse_hbm,
+    enc_held, bias_held, mse_held, delta_ref, enc_sems, small_sems,
 ):
-    layers, width, tokens = acts_ref.shape
+    layers, _, tokens = acts_ref.shape
     feature_dev = enc_held.shape[2]
+    join(delta_ref, core_ref[0], ours_ref, theirs_ref)
     leaving = []
 
     def send(held, out, sem):
@@ -316,47 +335,35 @@
         return slice(a * feature_dev, (a + 1) * feature_dev)
 
     for a in range(layers):
-        for b in range(a, layers):
-            pair = pair_number(a, b, layers)
-            dec_held[pair] = contract(
-                error_ref[:, b * width : (b + 1) * width], features_ref[:, layer(a)], 0, 0
-            )
-            send(dec_held.at[pair], dec_hbm.at[pair], dec_sems.at[pair])
-    mse_held[...] = jnp.sum(extra_ref[:1, :], axis=1, keepdims=True) * share
+        enc_held[a] = contract(acts_ref[a], delta_ref[:, layer(a)], 1, 0)
+        send(enc_held.at[a], enc_hbm.at[a], enc_sems.at[a])
+    both = extra_ref[:1, :] + other_extra_ref[:1, :]
+    mse_held[...] = jnp.sum(both, axis=1, keepdims=True) * share
     send(mse_held, mse_hbm, small_sems.at[0])
     ones = jnp.ones((8, tokens), BF16)
     for a in range(layers):
         bias_held[a : a + 1, :] = contract(ones, delta_ref[:, layer(a)], 1, 0)[:1]
     send(bias_held, bias_hbm, small_sems.at[1])
-    for a in range(layers):
-        enc_held[a] = contract(acts_ref[a], delta_ref[:, layer(a)], 1, 0)
-        send(enc_held.at[a], enc_hbm.at[a], enc_sems.at[a])
     for copy in leaving:
         copy.wait()
 
 
-def gradients(acts_t, delta, features, error, extra, share):
-    layers, width, _ = acts_t.shape
-    feature_dev = delta.shape[1] // layers
-    pairs = layers * (layers + 1) // 2
+def encoder_grad(core, acts_t, ours, theirs, extra, other_extra, share):
+    layers, width, tokens = acts_t.shape
+    columns = theirs.shape[1]
     vmem = pl.BlockSpec(memory_space=pltpu.VMEM)
-    anywhere = pl.BlockSpec(memory_space=pl.ANY)
-    shapes = (
-        (layers, width, feature_dev),
-        (layers, feature_dev),
-        (pairs, width, feature_dev),
-        (1, 1),
-    )
+    shapes = ((layers, width, columns // layers), (layers, columns // layers), (1, 1))
     return pl.pallas_call(
-        functools.partial(gradients_kernel, share),
-        in_specs=[vmem] * 5,
-        out_specs=[anywhere] * 4,
+        functools.partial(encoder_grad_kernel, share),
+        in_specs=[pl.BlockSpec(memory_space=pltpu.SMEM)] + [vmem] * 5,
+        out_specs=[pl.BlockSpec(memory_space=pl.ANY)] * 3,
         out_shape=[jax.ShapeDtypeStruct(shape, F32) for shape in shapes],
         scratch_shapes=[pltpu.VMEM(shape, F32) for shape in shapes]
-        + [pltpu.SemaphoreType.DMA((count,)) for count in (layers, pairs, 2)],
+        + [pltpu.VMEM((tokens, columns), BF16)]
+        + [pltpu.SemaphoreType.DMA((count,)) for count in (layers, 2)],
         compiler_params=pltpu.CompilerParams(vmem_limit_bytes=VMEM),
-        name="gradients",
-    )(acts_t, delta, features, error, extra)
+        name="encoder_grad",
+    )(core, acts_t, ours, theirs, extra, other_extra)
 
 
 def local(acts_in, acts_out, enc_weight, enc_bias, dec_weight, dec_bias):
@@ -371,24 +378,38 @@
     portion = half // chips
     core = core.reshape(1)
     offset = core * half + lax.axis_index(CHIPS) * portion
+    swap = [(0, 1), (1, 0)]
+    other_dec_t = lax.ppermute(dec_t, CORE, swap)
     sent = encode(acts_t, enc_weight, slots)
     sent, core, offset = lax.optimization_barrier((sent, core, offset))
-    own_features = own_features_of(exchange(sent, SLOT), enc_bias, tokens // slots)
+    arrived, other_dec_t = lax.optimization_barrier((exchange(sent, SLOT), other_dec_t))
+    own_features = own_features_of(arrived, enc_bias, tokens // slots)
     features = sent_to_all(own_features, SLOT).reshape(tokens, -1)
 
-    swap = [(0, 1), (1, 0)]
     from_core = lax.ppermute(decode(core, features, dec_t, layers, False), CORE, swap)
     chip_sum = (decode(core, features, dec_t, layers, True) + from_core.astype(F32)).astype(BF16)
+    rows = half // slots
+    at = lax.axis_index(SLOT) * rows
+
+    def block(side):
+        return lax.dynamic_slice_in_dim(features, side * half + at, rows, 0)
+
+    own_block = block(core[0])
+    other_block = lax.ppermute(block(1 - core[0]), CORE, swap)
+    chip_sum, own_block, other_block = lax.optimization_barrier((chip_sum, own_block, other_block))
     arrived = exchange(chip_sum.reshape(chips, portion, -1), CHIPS)
     own_error = own_error_of(offset, arrived, jnp.transpose(acts_out, (0, 2, 1)), dec_bias)
     half_error = sent_to_all(own_error, CHIPS).reshape(half, -1)
     other_error = lax.ppermute(half_error, CORE, swap)
-    sent_ours = upstream_ours(half_error, dec_t, layers, slots // 2)
-    sent, error = upstream(core, half_error, other_error, sent_ours, dec_t, layers)
-    own_delta, extra = own_delta_of(exchange(sent, SLOT), own_features)
-    delta = sent_to_all(own_delta, SLOT).reshape(tokens, -1)
+    sent = upstream(half_error, dec_t, other_dec_t, layers, slots)
+    own_delta, extra = own_delta_of(exchange(sent, SLOT), own_block, other_block)
+    other_extra = lax.ppermute(extra, CORE, swap)
+    gathered = sent_to_all(own_delta, SLOT)
+    ours = gathered[:, 0].reshape(half, -1)
+    theirs = lax.ppermute(gathered[:, 1].reshape(half, -1), CORE, swap)
+    dec_grad_t = decoder_grad(core, half_error, other_error, features, layers)
     share = 1.0 / (layers * tokens * D)
-    enc_grad, bias_grad, dec_grad_t, mse = gradients(acts_t, delta, features, error, extra, share)
+    enc_grad, bias_grad, mse = encoder_grad(core, acts_t, ours, theirs, extra, other_extra, share)
     return (enc_grad, bias_grad, jnp.transpose(dec_grad_t, (0, 2, 1)), mse.reshape(()))
 
 

time: 114 us -> 116 us (1.018); the launches traced: 114 us -> 115 us
  blocking collectives: 102 us -> 83 us
  waiting for transfers between devices: 1.43 us -> 14.2 us
  starting transfers between devices: 0.1 us -> 4.99 us
    all_to_all x6 -> x5, blocking collectives: 102 us -> 83 us  [exchange(): return lax.all_to_all(tiles, axis, split_axis=0, concat_axis=0, tiled=True)]
    all_to_all x0 -> x1, waiting for transfers between devices: none -> 12.7 us  [exchange(): return lax.all_to_all(tiles, axis, split_axis=0, concat_axis=0, tiled=True)]
    all_to_all x0 -> x1, starting transfers between devices: none -> 3.55 us  [exchange(): return lax.all_to_all(tiles, axis, split_axis=0, concat_axis=0, tiled=True)]
    pallas_call x1 -> x2, Pallas kernels: 2.91 us -> 3.81 us  [the longest x1 2.26 us: decoder_grad(): pl.pallas_call(functools.partial(decoder_grad_kernel, layers), in_specs=[...]
    pallas_call x7 -> x6, Pallas kernels: 4.18 us -> 3.94 us  [on_chip(): pl.pallas_call(kernel, in_specs=[smem if arg.dtype == jnp.int32 else vmem...]
  transfers between devices with their start and end apart: 2 -> 7, of which waited for: 2 -> 2; matrix products, arithmetic and copies ran while one was open for 0% -> 0% of each run, Pallas kernels for 1% -> 5%
where the time goes in v12:
time: 116 us; the launch traced here: 115 us
  blocking collectives  83 us (72%)
  waiting for transfers between devices  14.2 us (12%)
  Pallas kernels  10.5 us (9%)
  starting transfers between devices  4.99 us (4%)
    all_to_all x5, blocking collectives, exchange(): return lax.all_to_all(tiles, axis, split_axis=0, concat_axis=0, tiled=True)  83 us
    all_to_all x1, waiting for transfers between devices, exchange(): return lax.all_to_all(tiles, axis, split_axis=0, concat_axis=0, tiled=True)  12.7 us
    pallas_call x6, Pallas kernels, on_chip(): pl.pallas_call(kernel, in_specs=[smem if arg.dtype == jnp.int32 else vmem...  3.94 us
    all_to_all x1, starting transfers between devices, exchange(): return lax.all_to_all(tiles, axis, split_axis=0, concat_axis=0, tiled=True)  3.55 us
    pallas_call x1, Pallas kernels, encode(): pl.pallas_call(encode_kernel, in_specs=[anywhere, anywhere], out_specs=pl...  2.8 us
  transfers between devices with their start and end apart: 7, of which 2 were waited for; matrix products, arithmetic and copies ran while one was open for 0% of the time, Pallas kernels for 5%

profile of v12, /device:TPU:32, one launch (start us, length us, event | category | flops | bytes accessed | tf_op | source)
XLA Modules:
  0.0 114.8 jit_solution(17531324581845847165)
XLA Ops:
  0.6 0.1 collective-permute-start
  0.7 0.0 copy-start.5
  0.8 2.8 %encode.1 = bf16[8,400,128]{2,1,0:T(8,128)(2,1)S(1)} custom-call(bf16[3,288,256]{2,1,0:T(8,128)(2,1)} %bitcast.25, bf16[3,288,512]{2,1,0:T(8,128)(2,1)} %weight_hbm.1), custom_call_target="tpu_custom_call" | custom-call | tf_op jit(solution)/shard_map/encode/pallas_call | solution.py:109
  3.6 19.2 %all_to_all.30.arrived_ref = bf16[8,400,128]{2,1,0:T(8,128)(2,1)S(1)} all-to-all(bf16[8,400,128]{2,1,0:T(8,128)(2,1)S(1)} %encode.1), channel_id=1, replica_groups=mesh['slot_0'=2,'slot_1'=4,'feat_0'=2,'feat_1'=8,'feat_2'=2] {'slot_0','..., dimensions={0} | all-to-all | bytes 1638400 | tf_op jit(solution)/shard_map/all_to_all | solution.py:29
  22.8 0.0 copy-start
  22.8 0.0 collective-permute-done.theirs_ref
  22.8 0.0 copy-done.5
  22.8 0.0 copy-start.1
  22.8 0.7 own_features.1
  23.5 0.9 broadcast_in_dim.6
  24.4 0.0 copy-done.1
  24.4 3.5 %all-to-all-start.1 = ((bf16[8,32,1536]{2,1,0:T(8,128)(2,1)}), bf16[8,32,1536]{2,1,0:T(8,128)(2,1)S(1)}, u32[]{:S(2)}, u32[]{:S(2)}) async-start(bf16[8,32,1536]{2,1,0:T(8,128)(2,1)} %broadcast_in_dim.6), calls=%async_computation.1 | async-start | bytes 1572864 | tf_op jit(solution)/shard_map/all_to_all | solution.py:29
  28.0 12.7 %all-to-all-done.1 = bf16[8,32,1536]{2,1,0:T(8,128)(2,1)S(1)} async-done(((bf16[8,32,1536]{2,1,0:T(8,128)(2,1)}), bf16[8,32,1536]{2,1,0:T(8,128)(2,1)S(1)}, u32[]{:S(2)}, u32[]{:S(2)}) %all-to-all-start.1) | async-done | bytes 786464 | tf_op jit(solution)/shard_map/all_to_all | solution.py:29
  40.7 0.0 copy-done
  40.7 0.9 decode_theirs.1
  41.6 0.1 collective-permute-start.1
  41.7 0.0 copy-start.4
  41.7 0.0 copy-start.6
  41.8 0.6 collective-permute-start.2
  42.3 0.9 decode_ours.1
  43.2 0.0 copy-start.2
  43.2 0.0 collective-permute-done.1
  43.3 0.0 collective-permute-done.2.theirs_ref
  43.3 22.2 %all_to_all.31.arrived_ref = bf16[16,8,864]{2,1,0:T(8,128)(2,1)S(1)} all-to-all(bf16[16,8,864]{2,1,0:T(8,128)(2,1)S(1)} %bitcast.30), channel_id=1, replica_groups=mesh['slot_0'=2,'slot_1'=4,'feat_0'=2,'feat_1'=8,'feat_2'=2] {'feat_0','..., dimensions={0} | all-to-all | bytes 442368 | tf_op jit(solution)/shard_map/all_to_all | solution.py:29
  65.5 0.0 copy-done.4
  65.5 0.0 copy-done.6
  65.5 0.3 own_error.1
  65.9 15.3 %all_to_all.32 = bf16[16,8,864]{2,1,0:T(8,128)(2,1)S(1)} all-to-all(bf16[16,8,864]{2,1,0:T(8,128)(2,1)S(1)} %broadcast_in_dim.7), channel_id=1, replica_groups=mesh['slot_0'=2,'slot_1'=4,'feat_0'=2,'feat_1'=8,'feat_2'=2] {'feat_0','..., dimensions={0} | all-to-all | bytes 442368 | tf_op jit(solution)/shard_map/all_to_all | solution.py:29
  81.2 0.0 copy-done.2
  81.2 1.0 upstream.1
  82.2 13.8 %all_to_all.33.arrived_ref = bf16[8,400,128]{2,1,0:T(8,128)(2,1)S(1)} all-to-all(bf16[8,400,128]{2,1,0:T(8,128)(2,1)S(1)} %upstream.1), channel_id=1, replica_groups=mesh['slot_0'=2,'slot_1'=4,'feat_0'=2,'feat_1'=8,'feat_2'=2] {'slot_0','..., dimensions={0} | all-to-all | bytes 1638400 | tf_op jit(solution)/shard_map/all_to_all | solution.py:29
  96.0 0.1 own_delta.1
  96.1 0.1 broadcast_in_dim.8
  96.2 12.5 %all_to_all.34 = bf16[8,2,16,1536]{3,2,1,0:T(8,128)(2,1)S(1)} all-to-all(bf16[8,2,16,1536]{3,2,1,0:T(8,128)(2,1)S(1)} %broadcast_in_dim.8), channel_id=1, replica_groups=mesh['slot_0'=2,'slot_1'=4,'feat_0'=2,'feat_1'=8,'feat_2'=2] {'slot_0','..., dimensions={0} | all-to-all | bytes 1572864 | tf_op jit(solution)/shard_map/all_to_all | solution.py:29
  108.7 0.1 fusion
  108.8 0.1 collective-permute-start.3
  108.9 0.5 collective-permute-start.5
  109.4 0.0 copy-start.3
  109.4 0.1 collective-permute-start.4
  109.5 1.4 %collective-permute-done.5.theirs_ref = bf16[128,864]{1,0:T(8,128)(2,1)S(1)} collective-permute-done((bf16[128,864]{1,0:T(8,128)(2,1)S(1)}, bf16[128,864]{1,0:T(8,128)(2,1)S(1)}, u32[]{:S(2)}, u32[]{:S(2)}) %collective-permute-start.5) | collective-permute-done | bytes 221216 | tf_op jit(solution)/shard_map/ppermute | solution.py:403
  110.9 2.3 %decoder_grad.1 = f32[6,288,512]{2,1,0:T(8,128)} custom-call(s32[1]{0:T(128)} %bitcast.1.core_ref, bf16[128,864]{1,0:T(8,128)(2,1)S(1)} %bitcast.24, bf16[128,864]{1,0:T(8,128)(2,1)S(1)} %collective-permute-done.5.theirs_ref, bf16[256,1536]{1,0:T(8,128)(2,1)S(1)} %bitcast.21), custom_call_target="tpu_custom_call" | custom-call | flops 536870912 | bytes 4194304 | tf_op jit(solution)/shard_map/decoder_grad/pallas_call | solution.py:303
  113.2 0.0 collective-permute-done.4.other_extra_ref
  113.2 0.0 collective-permute-done.3.theirs_ref
  113.2 0.0 copy-done.3
  113.2 1.6 %encoder_grad.1 = (f32[3,288,512]{2,1,0:T(8,128)}, f32[3,512]{1,0:T(4,128)}, f32[1,1]{1,0:T(1,128)}) custom-call(s32[1]{0:T(128)} %bitcast.1.core_ref, bf16[3,288,256]{2,1,0:T(8,128)(2,1)S(1)} %bitcast.26, bf16[128,1536]{1,0:T(8,128)(2,1)S(1)} %bitcast.27, bf16[128,1536]{1,0:T(8,128)(2,1)S(1)} %collective-permute-done.3.theirs_ref, ...), custom_call_target="tpu_custom_call" | custom-call | tf_op jit(solution)/shard_map/encoder_grad/pallas_call | solution.py:356
  (3 shorter events, 0.1 us)
Async XLA Ops:
  0.6 22.1 %collective-permute-start = (bf16[6,288,512]{2,1,0:T(8,128)(2,1)}, bf16[6,288,512]{2,1,0:T(8,128)(2,1)S(1)}, u32[]{:S(2)}, u32[]{:S(2)}) collective-permute-start(bf16[6,288,512]{2,1,0:T(8,128)(2,1)} %bitcast.14), channel_id=1, source_target_pairs={{0,1},{1,0},{2,3},{3,2},{4,5},{5,4},{6,7},{7,6},{8,9},{9,8},{10,11... | collective-permute-start | bytes 5308424 | tf_op jit(solution)/shard_map/ppermute | solution.py:382
  0.7 22.0 %copy-start.5 = (f32[3,512]{1,0:T(4,128)S(1)}, f32[3,512]{1,0:T(4,128)}, u32[]{:S(2)}) copy-start(f32[3,512]{1,0:T(4,128)} %bias_ref.2) | copy-start | bytes 18436
  22.8 17.9 %copy-start = (bf16[6,512,288]{1,2,0:T(8,128)(2,1)S(1)}, bf16[6,512,288]{1,2,0:T(8,128)(2,1)}, u32[]{:S(2)}) copy-start(bf16[6,512,288]{1,2,0:T(8,128)(2,1)} %param.10) | copy-start | bytes 5308420
  22.8 1.6 %copy-start.1 = (bf16[6,288,512]{2,1,0:T(8,128)(2,1)}, bf16[6,288,512]{2,1,0:T(8,128)(2,1)S(1)}, u32[]{:S(2)}) copy-start(bf16[6,288,512]{2,1,0:T(8,128)(2,1)S(1)} %collective-permute-done.theirs_ref) | copy-start | bytes 5308420
  24.4 16.3 %all-to-all-start.1 = ((bf16[8,32,1536]{2,1,0:T(8,128)(2,1)}), bf16[8,32,1536]{2,1,0:T(8,128)(2,1)S(1)}, u32[]{:S(2)}, u32[]{:S(2)}) async-start(bf16[8,32,1536]{2,1,0:T(8,128)(2,1)} %broadcast_in_dim.6), calls=%async_computation.1 | async-start | bytes 1572864 | tf_op jit(solution)/shard_map/all_to_all | solution.py:29
  41.6 1.6 %collective-permute-start.1 = (bf16[128,864]{1,0:T(8,128)(2,1)S(1)}, bf16[128,864]{1,0:T(8,128)(2,1)S(1)}, u32[]{:S(2)}, u32[]{:S(2)}) collective-permute-start(bf16[128,864]{1,0:T(8,128)(2,1)S(1)} %decode_theirs.1), channel_id=1, source_target_pairs={{0,1},{1,0},{2,3},{3,2},{4,5},{5,4},{6,7},{7,6},{8,9},{9,8},{10,11... | collective-permute-start | bytes 663560 | tf_op jit(solution)/shard_map/ppermute | solution.py:389
  41.7 23.8 %copy-start.4 = (bf16[3,256,288]{1,2,0:T(8,128)(2,1)S(1)}, bf16[3,256,288]{1,2,0:T(8,128)(2,1)}, u32[]{:S(2)}) copy-start(bf16[3,256,288]{1,2,0:T(8,128)(2,1)} %param.7) | copy-start | bytes 1327108
  41.7 23.8 %copy-start.6 = (f32[3,288]{1,0:T(4,128)S(1)}, f32[3,288]{1,0:T(4,128)}, u32[]{:S(2)}) copy-start(f32[3,288]{1,0:T(4,128)} %bias_ref.3) | copy-start | bytes 10372
  41.8 1.5 %collective-permute-start.2 = (bf16[16,1536]{1,0:T(8,128)(2,1)S(1)}, bf16[16,1536]{1,0:T(8,128)(2,1)S(1)}, u32[]{:S(2)}, u32[]{:S(2)}) collective-permute-start(bf16[16,1536]{1,0:T(8,128)(2,1)S(1)} %get-tuple-element.32), channel_id=1, source_target_pairs={{0,1},{1,0},{2,3},{3,2},{4,5},{5,4},{6,7},{7,6},{8,9},{9,8},{10,11... | collective-permute-start | bytes 147464 | tf_op jit(solution)/shard_map/ppermute | solution.py:398
  43.2 38.0 %copy-start.2 = (bf16[6,288,512]{2,1,0:T(8,128)(2,1)S(1)}, bf16[6,288,512]{2,1,0:T(8,128)(2,1)}, u32[]{:S(2)}) copy-start(bf16[6,288,512]{2,1,0:T(8,128)(2,1)} %copy-done.1) | copy-start | bytes 5308420
  108.8 4.4 %collective-permute-start.3 = (bf16[128,1536]{1,0:T(8,128)(2,1)S(1)}, bf16[128,1536]{1,0:T(8,128)(2,1)S(1)}, u32[]{:S(2)}, u32[]{:S(2)}) collective-permute-start(bf16[128,1536]{1,0:T(8,128)(2,1)S(1)} %bitcast.31), channel_id=1, source_target_pairs={{0,1},{1,0},{2,3},{3,2},{4,5},{5,4},{6,7},{7,6},{8,9},{9,8},{10,11... | collective-permute-start | bytes 1179656 | tf_op jit(solution)/shard_map/ppermute | solution.py:409
  108.9 2.0 %collective-permute-start.5 = (bf16[128,864]{1,0:T(8,128)(2,1)S(1)}, bf16[128,864]{1,0:T(8,128)(2,1)S(1)}, u32[]{:S(2)}, u32[]{:S(2)}) collective-permute-start(bf16[128,864]{1,0:T(8,128)(2,1)S(1)} %bitcast.23), channel_id=1, source_target_pairs={{0,1},{1,0},{2,3},{3,2},{4,5},{5,4},{6,7},{7,6},{8,9},{9,8},{10,11... | collective-permute-start | bytes 663560 | tf_op jit(solution)/shard_map/ppermute | solution.py:403
  109.4 3.8 %copy-start.3 = (bf16[3,256,288]{1,2,0:T(8,128)(2,1)S(1)}, bf16[3,256,288]{1,2,0:T(8,128)(2,1)}, u32[]{:S(2)}) copy-start(bf16[3,256,288]{1,2,0:T(8,128)(2,1)} %param.6) | copy-start | bytes 1327108
  109.4 3.8 %collective-permute-start.4 = (f32[16,128]{1,0:T(8,128)S(1)}, f32[16,128]{1,0:T(8,128)S(1)}, u32[]{:S(2)}, u32[]{:S(2)}) collective-permute-start(f32[16,128]{1,0:T(8,128)S(1)} %get-tuple-element.26.extra_ref), channel_id=1, source_target_pairs={{0,1},{1,0},{2,3},{3,2},{4,5},{5,4},{6,7},{7,6},{8,9},{9,8},{10,11... | collective-permute-start | bytes 24584 | tf_op jit(solution)/shard_map/ppermute | solution.py:406
